TPU v7x, 32 devices: a whole 2x2x4 slice. The times are simulated.
32 devices in a mesh: win: 8 (over z, y), seq: 4 (over x, core).
Axes of the slice: x: 2, y: 2, z: 4, core: 2. Of those that a mesh axis runs over, the one named last changes fastest.
Arguments:
- inputs: bfloat16 [8, 1024, 1536], P('win', 'seq'), may hold values from -6 to 6
- skips: bfloat16 [8, 2048, 1280], P('win', 'seq'), may hold values from -6 to 6
- counts: int32 [8, 2048, 2608], P('win', 'seq'), may hold values from 0 to 4, as said below
- ln1_gain: bfloat16 [1536], P(('win', 'seq')), may hold values from 0.5 to 1.5
- ln1_bias: bfloat16 [1536], P(('win', 'seq')), may hold values from -1 to 1
- w_query: bfloat16 [1536, 512], P(('win', 'seq')), may hold values from -0.15625 to 0.15625
- w_key: bfloat16 [1536, 512], P(('win', 'seq')), may hold values from -0.15625 to 0.15625
- w_value: bfloat16 [1536, 1536], P(('win', 'seq')), may hold values from -0.15625 to 0.15625
- w_rel: bfloat16 [32, 512], P(None, ('win', 'seq')), may hold values from -1 to 1
- content_bias: bfloat16 [512], P(('win', 'seq')), may hold values from -3 to 3
- position_bias: bfloat16 [512], P(('win', 'seq')), may hold values from -3 to 3
- w_out: bfloat16 [1536, 1536], P(('win', 'seq')), may hold values from -1.25 to 1.25
- ln2_gain: bfloat16 [1536], P(('win', 'seq')), may hold values from 0.5 to 1.5
- ln2_bias: bfloat16 [1536], P(('win', 'seq')), may hold values from -1 to 1
- w_in: bfloat16 [1536, 3072], P(('win', 'seq')), may hold values from -0.15625 to 0.15625
- b_in: bfloat16 [3072], P(('win', 'seq')), may hold values from -3 to 3
- w_hid: bfloat16 [3072, 1536], P(('win', 'seq')), may hold values from -0.109375 to 0.109375
- b_hid: bfloat16 [1536], P(('win', 'seq')), may hold values from -3 to 3
- w_up: bfloat16 [1536, 1536], P(('win', 'seq')), may hold values from -0.15625 to 0.15625
- w_skip: bfloat16 [1280, 1536], P(('win', 'seq')), may hold values from -0.15625 to 0.15625
- m_bias: bfloat16 [1536], P(('win', 'seq')), may hold values from -3 to 3
- w_depth: bfloat16 [3, 1536], P(None, ('win', 'seq')), may hold values from -2 to 2
- w_point: bfloat16 [1536, 1536], P(('win', 'seq')), may hold values from -0.15625 to 0.15625
- p_bias: bfloat16 [1536], P(('win', 'seq')), may hold values from -3 to 3
- w_head: bfloat16 [1536, 2608], P(('win', 'seq')), may hold values from -0.009765625 to 0.009765625
- head_bias: bfloat16 [2608], replicated, may hold values from 0.5 to 1.5
Outputs:
- loss: float32 [], replicated
- activations: bfloat16 [8, 2048, 1536], P('win', 'seq')
- grad_inputs: float32 [8, 1024, 1536], P('win', 'seq')
- grad_skips: float32 [8, 2048, 1280], P('win', 'seq')
- grad_ln1_gain: float32 [1536], P(('win', 'seq'))
- grad_ln1_bias: float32 [1536], P(('win', 'seq'))
- grad_w_query: float32 [1536, 512], P(('win', 'seq'))
- grad_w_key: float32 [1536, 512], P(('win', 'seq'))
- grad_w_value: float32 [1536, 1536], P(('win', 'seq'))
- grad_w_rel: float32 [32, 512], P(None, ('win', 'seq'))
- grad_content_bias: float32 [512], P(('win', 'seq'))
- grad_position_bias: float32 [512], P(('win', 'seq'))
- grad_w_out: float32 [1536, 1536], P(('win', 'seq'))
- grad_ln2_gain: float32 [1536], P(('win', 'seq'))
- grad_ln2_bias: float32 [1536], P(('win', 'seq'))
- grad_w_in: float32 [1536, 3072], P(('win', 'seq'))
- grad_b_in: float32 [3072], P(('win', 'seq'))
- grad_w_hid: float32 [3072, 1536], P(('win', 'seq'))
- grad_b_hid: float32 [1536], P(('win', 'seq'))
- grad_w_up: float32 [1536, 1536], P(('win', 'seq'))
- grad_w_skip: float32 [1280, 1536], P(('win', 'seq'))
- grad_m_bias: float32 [1536], P(('win', 'seq'))
- grad_w_depth: float32 [3, 1536], P(None, ('win', 'seq'))
- grad_w_point: float32 [1536, 1536], P(('win', 'seq'))
- grad_p_bias: float32 [1536], P(('win', 'seq'))
- grad_w_head: float32 [1536, 2608], P(('win', 'seq'))
- grad_head_bias: float32 [2608], replicated
Inputs may be any that keep to these rules, and one draw needn't show every extreme that they name: counts are whole numbers from 0 to 4 (at bin p of a window at most 1 + 4p // 2048).
All inputs are finite; a program needn't handle non-finite values.
Results may differ from a plain program's by a relative error of at most 0.025.
Values may be sent and summed in bfloat16 or wider, within the bound.
No kernel may reach another device: no remote copies, remote signals or barrier semaphores. Data moves between devices by JAX's collectives and lax.ppermute only.
A program may use at most 384 MiB of HBM per device.

v0:
```python
import math

import jax
import jax.numpy as jnp
from jax import lax
from jax.sharding import PartitionSpec as P

D = 1536
HEADS = 8
KEY = 64
VAL = 192
BASIS = 32
CS = 1280
TRACKS = 2608
TOK_SEQ = 256
SEQS_DEV = 1
HK = 512
HV = 1536


EPS = 1e-05
HIGH = lax.Precision.HIGHEST


def with_halo(cells, sides, width):
    for axis, dim in sides:
        count = lax.axis_size(axis)
        ends = count - 1
        head = lax.slice_in_dim(cells, 0, width, axis=dim)
        tail = lax.slice_in_dim(cells, cells.shape[dim] - width, cells.shape[dim], axis=dim)
        cells = jnp.concatenate(
            [
                lax.ppermute(tail, axis, [(i, (i + 1) % count) for i in range(ends)]),
                cells,
                lax.ppermute(head, axis, [((i + 1) % count, i) for i in range(ends)]),
            ],
            axis=dim,
        )
    return cells


def basis_table(offsets, seq_len, basis_count):
    halves = basis_count // 2
    ramped = jnp.arange(halves, dtype=jnp.int32).astype(jnp.float32) / (halves - 1)
    half_life = 3.0 * jnp.exp(ramped * math.log(seq_len / 3.0))
    distance = jnp.abs(offsets)[..., None]
    decays = jnp.exp(-math.log(2.0) * distance / half_life)
    return jnp.concatenate([decays, jnp.sign(offsets)[..., None] * decays], axis=-1)


def layer_norm(values, gain_row, bias_row):
    centred = values - jnp.mean(values, axis=-1, keepdims=True)
    spread = jnp.mean(centred * centred, axis=-1, keepdims=True)
    return centred * lax.rsqrt(spread + EPS) * gain_row + bias_row


def smooth_act(values):
    return jax.nn.gelu(values, approximate=True)


def product(first_arg, second_arg):
    return jnp.dot(first_arg, second_arg, preferred_element_type=jnp.float32)


def weight_product(first_arg, second_arg):
    return lax.dot_general(
        first_arg, second_arg, (((0,), (0,)), ((), ())), preferred_element_type=jnp.float32
    )


def input_product(first_arg, second_arg):
    return lax.dot_general(
        first_arg, second_arg, (((1,), (1,)), ((), ())), preferred_element_type=jnp.float32
    )


def score_block(query_blk, pos_blk, key_blk, query_first, key_first, seq_len):
    row_pos = query_first + jnp.arange(query_blk.shape[1], dtype=jnp.int32)
    col_pos = key_first + jnp.arange(key_blk.shape[1], dtype=jnp.int32)
    offsets = (row_pos[:, None] - col_pos[None, :]).astype(jnp.float32)
    basis_grid = basis_table(offsets, seq_len, BASIS).astype(jnp.bfloat16)
    key_heads = key_blk.reshape(key_blk.shape[0], key_blk.shape[1], HEADS, KEY)
    content = jnp.einsum(
        "snhk,schk->shnc", query_blk, key_heads, preferred_element_type=jnp.float32
    )
    position = jnp.einsum("snhb,ncb->shnc", pos_blk, basis_grid, preferred_element_type=jnp.float32)
    return (content + position, basis_grid)


def body(
    inputs,
    skips,
    counts,
    ln1_gain,
    ln1_bias,
    w_query,
    w_key,
    w_value,
    w_rel,
    content_bias,
    position_bias,
    w_out,
    ln2_gain,
    ln2_bias,
    w_in,
    b_in,
    w_hid,
    b_hid,
    w_up,
    w_skip,
    m_bias,
    w_depth,
    w_point,
    p_bias,
    w_head,
    head_bias,
):
    seq_count = lax.axis_size("seq")
    seq_len = TOK_SEQ * seq_count
    first_pos = lax.axis_index("seq") * TOK_SEQ
    row_count = SEQS_DEV * TOK_SEQ
    blk_len = 512
    blk_count = seq_len // blk_len
    blk_steps = jnp.arange(blk_count, dtype=jnp.int32)
    mixer_full = (
        lax.all_gather(ln1_gain, ("win", "seq"), axis=0, tiled=True),
        lax.all_gather(ln1_bias, ("win", "seq"), axis=0, tiled=True),
        lax.all_gather(w_query, ("win", "seq"), axis=0, tiled=True),
        lax.all_gather(w_key, ("win", "seq"), axis=0, tiled=True),
        lax.all_gather(w_value, ("win", "seq"), axis=0, tiled=True),
        lax.all_gather(w_rel, ("win", "seq"), axis=1, tiled=True),
        lax.all_gather(content_bias, ("win", "seq"), axis=0, tiled=True),
        lax.all_gather(position_bias, ("win", "seq"), axis=0, tiled=True),
        lax.all_gather(w_out, ("win", "seq"), axis=0, tiled=True),
    )
    tail_full = (
        lax.all_gather(ln2_gain, ("win", "seq"), axis=0, tiled=True),
        lax.all_gather(ln2_bias, ("win", "seq"), axis=0, tiled=True),
        lax.all_gather(w_in, ("win", "seq"), axis=0, tiled=True),
        lax.all_gather(b_in, ("win", "seq"), axis=0, tiled=True),
        lax.all_gather(w_hid, ("win", "seq"), axis=0, tiled=True),
        lax.all_gather(b_hid, ("win", "seq"), axis=0, tiled=True),
        lax.all_gather(w_up, ("win", "seq"), axis=0, tiled=True),
        lax.all_gather(w_skip, ("win", "seq"), axis=0, tiled=True),
        lax.all_gather(m_bias, ("win", "seq"), axis=0, tiled=True),
        lax.all_gather(w_depth, ("win", "seq"), axis=1, tiled=True),
        lax.all_gather(w_point, ("win", "seq"), axis=0, tiled=True),
        lax.all_gather(p_bias, ("win", "seq"), axis=0, tiled=True),
        lax.all_gather(w_head, ("win", "seq"), axis=0, tiled=True),
    )
    gain_one = mixer_full[0].astype(jnp.float32)
    bias_one = mixer_full[1].astype(jnp.float32)
    query_full = mixer_full[2]
    key_full = mixer_full[3]
    value_full = mixer_full[4]
    rel_full = mixer_full[5].astype(jnp.float32).reshape(BASIS, HEADS, KEY)
    content_full = mixer_full[6].astype(jnp.float32)
    position_full = mixer_full[7].astype(jnp.float32)
    out_full = mixer_full[8]
    gain_two = tail_full[0].astype(jnp.float32)
    bias_two = tail_full[1].astype(jnp.float32)
    in_full = tail_full[2]
    in_bias = tail_full[3].astype(jnp.float32)
    hid_full = tail_full[4]
    hid_bias = tail_full[5].astype(jnp.float32)
    up_full = tail_full[6]
    skip_full = tail_full[7]
    merge_bias = tail_full[8].astype(jnp.float32)
    depth_full = tail_full[9].astype(jnp.float32)
    point_full = tail_full[10]
    point_bias = tail_full[11].astype(jnp.float32)
    head_full = tail_full[12]
    inputs_f = inputs.astype(jnp.float32).reshape(row_count, D)
    normed = layer_norm(inputs_f, gain_one, bias_one).astype(jnp.bfloat16)
    query_raw = product(normed, query_full) * 0.125
    queries = (query_raw + content_full).astype(jnp.bfloat16).reshape(SEQS_DEV, TOK_SEQ, HEADS, KEY)
    pos_in = (query_raw + position_full).reshape(row_count, HEADS, KEY)
    pos_query = (
        jnp.einsum("lhk,bhk->lhb", pos_in, rel_full, precision=HIGH)
        .astype(jnp.bfloat16)
        .reshape(SEQS_DEV, TOK_SEQ, HEADS, BASIS)
    )
    key_rows = product(normed, key_full).astype(jnp.bfloat16).reshape(SEQS_DEV, TOK_SEQ, HK)
    values = product(normed, value_full).astype(jnp.bfloat16).reshape(SEQS_DEV, TOK_SEQ, HV)
    keys_all, values_all = (
        lax.all_gather(key_rows, "seq", axis=1, tiled=True),
        lax.all_gather(values, "seq", axis=1, tiled=True),
    )

    def key_block(whole_rows, blk_index):
        return lax.dynamic_slice_in_dim(whole_rows, blk_index * blk_len, blk_len, 1)

    def value_block(blk_index):
        return key_block(values_all, blk_index).reshape(SEQS_DEV, blk_len, HEADS, VAL)

    def scores_at(blk_index):
        return score_block(
            queries,
            pos_query,
            key_block(keys_all, blk_index),
            first_pos,
            blk_index * blk_len,
            seq_len,
        )

    def max_step(state_pair, blk_index):
        row_max, row_sum = state_pair
        scores, basis_grid = scores_at(blk_index)
        new_max = jnp.maximum(row_max, jnp.max(scores, axis=-1))
        row_sum = row_sum * jnp.exp(row_max - new_max) + jnp.sum(
            jnp.exp(scores - new_max[..., None]), axis=-1
        )
        return ((new_max, row_sum), None)

    start_max = jnp.full((SEQS_DEV, HEADS, TOK_SEQ), -jnp.inf, jnp.float32)
    (row_max, row_sum), _ = lax.scan(max_step, (start_max, jnp.zeros_like(start_max)), blk_steps)
    log_norm = row_max + jnp.log(row_sum)

    def mix_step(mixed_sum, blk_index):
        scores, basis_grid = scores_at(blk_index)
        weights = jnp.exp(scores - log_norm[..., None]).astype(jnp.bfloat16)
        mixed_sum = mixed_sum + jnp.einsum(
            "shnc,schv->snhv", weights, value_block(blk_index), preferred_element_type=jnp.float32
        )
        return (mixed_sum, None)

    mixed_sum, _ = lax.scan(
        mix_step, jnp.zeros((SEQS_DEV, TOK_SEQ, HEADS, VAL), jnp.float32), blk_steps
    )
    attended = mixed_sum.reshape(row_count, HV).astype(jnp.bfloat16)
    resid_one = inputs_f + product(attended, out_full)
    normed_two = layer_norm(resid_one, gain_two, bias_two).astype(jnp.bfloat16)
    pre_act = product(normed_two, in_full) + in_bias
    hidden = smooth_act(pre_act).astype(jnp.bfloat16)
    lift_in = (resid_one + product(hidden, hid_full) + hid_bias).astype(jnp.bfloat16)
    lifted = product(lift_in, up_full).reshape(SEQS_DEV, TOK_SEQ, D)
    skip_rows = skips.reshape(2 * row_count, CS)
    merged = (
        jnp.repeat(lifted, 2, axis=1)
        + product(skip_rows, skip_full).reshape(SEQS_DEV, 2 * TOK_SEQ, D)
        + merge_bias
    )
    padded = with_halo(merged.astype(jnp.bfloat16), (("seq", 1),), 1).astype(merged.dtype)
    depth_out = (
        depth_full[0] * padded[:, :-2]
        + depth_full[1] * padded[:, 1:-1]
        + depth_full[2] * padded[:, 2:]
    ).astype(jnp.bfloat16)
    output = (
        merged
        + product(depth_out.reshape(2 * row_count, D), point_full).reshape(SEQS_DEV, 2 * TOK_SEQ, D)
        + point_bias
    )
    head_in = output.astype(jnp.bfloat16)
    head_rows = head_in.reshape(2 * row_count, D)
    logits = (product(head_rows, head_full) + head_bias.astype(jnp.float32)).reshape(
        SEQS_DEV, 2 * TOK_SEQ, TRACKS
    )
    rate_rows = jax.nn.softplus(logits)
    count_rows = counts.astype(jnp.float32)
    part_rate = jnp.sum(rate_rows, axis=1)
    part_count = jnp.sum(count_rows, axis=1)
    total_rate, total_count = lax.psum((part_rate, part_count), "seq")
    log_total = jnp.log(total_rate)
    window_terms = jnp.sum(total_count * log_total) + 0.2 * jnp.sum(
        total_rate - total_count * log_total
    )
    local_loss = -jnp.sum(count_rows * jnp.log(rate_rows)) + jnp.where(
        lax.axis_index("seq") == 0, window_terms, 0.0
    )
    count_ratio = total_count / total_rate
    grad_rate = -count_rows / rate_rows + (0.2 + 0.8 * count_ratio)[:, None, :]
    grad_logit = (grad_rate * jax.nn.sigmoid(logits)).astype(jnp.bfloat16)
    bias_part = jnp.sum(grad_logit, axis=(0, 1), dtype=jnp.float32)
    loss_total, head_bias_grad = lax.psum((local_loss, bias_part), ("win", "seq"))
    loss_mean = loss_total / (SEQS_DEV * lax.axis_size("win") * 2 * seq_len * TRACKS)
    grad_rows = grad_logit.reshape(2 * row_count, TRACKS)
    head_grad = weight_product(head_rows, grad_rows)
    grad_out = input_product(grad_rows, head_full).astype(jnp.bfloat16)
    point_grad = weight_product(depth_out.reshape(2 * row_count, D), grad_out)
    pbias_grad = jnp.sum(grad_out, axis=0, dtype=jnp.float32)
    grad_depth = (
        input_product(grad_out, point_full).astype(jnp.bfloat16).reshape(SEQS_DEV, 2 * TOK_SEQ, D)
    )
    depth_grad = jnp.stack(
        [
            jnp.sum(grad_depth * padded[:, :-2], axis=(0, 1)),
            jnp.sum(grad_depth * padded[:, 1:-1], axis=(0, 1)),
            jnp.sum(grad_depth * padded[:, 2:], axis=(0, 1)),
        ]
    )
    depth_pad = with_halo(grad_depth, (("seq", 1),), 1)
    grad_merged = (
        grad_out.reshape(SEQS_DEV, 2 * TOK_SEQ, D).astype(jnp.float32)
        + depth_full[0] * depth_pad[:, 2:]
        + depth_full[1] * depth_pad[:, 1:-1]
        + depth_full[2] * depth_pad[:, :-2]
    )
    merged_low = grad_merged.astype(jnp.bfloat16)
    merged_rows = merged_low.reshape(2 * row_count, D)
    skip_weight_grad = weight_product(skip_rows, merged_rows)
    skip_grad = input_product(merged_rows, skip_full).reshape(SEQS_DEV, 2 * TOK_SEQ, CS)
    mbias_grad = jnp.sum(merged_rows, axis=0, dtype=jnp.float32)
    lift_grad = (
        jnp.sum(merged_low.reshape(SEQS_DEV, TOK_SEQ, 2, D), axis=2, dtype=jnp.float32)
        .reshape(row_count, D)
        .astype(jnp.bfloat16)
    )
    up_grad = weight_product(lift_in, lift_grad)
    grad_two = input_product(lift_grad, up_full).astype(jnp.bfloat16)
    hid_grad = weight_product(hidden, grad_two)
    hbias_grad = jnp.sum(grad_two, axis=0, dtype=jnp.float32)
    grad_hidden = input_product(grad_two, hid_full).astype(jnp.bfloat16)
    _, pull_act = jax.vjp(smooth_act, pre_act)
    grad_pre = pull_act(grad_hidden.astype(jnp.float32))[0].astype(jnp.bfloat16)
    in_grad = weight_product(normed_two, grad_pre)
    ibias_grad = jnp.sum(grad_pre, axis=0, dtype=jnp.float32)
    _, pull_two = jax.vjp(layer_norm, resid_one, gain_two, bias_two)
    grad_resid, gain_two_grad, bias_two_grad = pull_two(input_product(grad_pre, in_full))
    grad_one = (grad_two.astype(jnp.float32) + grad_resid).astype(jnp.bfloat16)
    out_grad = weight_product(attended, grad_one)
    grad_att = (
        input_product(grad_one, out_full)
        .astype(jnp.bfloat16)
        .reshape(SEQS_DEV, TOK_SEQ, HEADS, VAL)
    )

    def grad_parts(blk_index):
        key_blk = key_block(keys_all, blk_index)
        scores, basis_grid = score_block(
            queries, pos_query, key_blk, first_pos, blk_index * blk_len, seq_len
        )
        soft_probs = jnp.exp(scores - log_norm[..., None])
        prob_grad = jnp.einsum(
            "snhv,schv->shnc", grad_att, value_block(blk_index), preferred_element_type=jnp.float32
        )
        return (key_blk, basis_grid, soft_probs, prob_grad)

    def delta_step(delta_sum, blk_index):
        key_blk, basis_grid, soft_probs, prob_grad = grad_parts(blk_index)
        return (delta_sum + jnp.sum(soft_probs * prob_grad, axis=-1), None)

    row_delta, _ = lax.scan(
        delta_step, jnp.zeros((SEQS_DEV, HEADS, TOK_SEQ), jnp.float32), blk_steps
    )

    def query_terms(state_pair, blk_index):
        key_blk, basis_grid, soft_probs, prob_grad = grad_parts(blk_index)
        score_grad = (soft_probs * (prob_grad - row_delta[..., None])).astype(jnp.bfloat16)
        key_heads = key_blk.reshape(SEQS_DEV, blk_len, HEADS, KEY)
        query_acc = state_pair[0] + jnp.einsum(
            "shnc,schk->snhk", score_grad, key_heads, preferred_element_type=jnp.float32
        )
        pos_acc = state_pair[1] + jnp.einsum(
            "shnc,ncb->snhb", score_grad, basis_grid, preferred_element_type=jnp.float32
        )
        return ((query_acc, pos_acc), score_grad, soft_probs)

    query_zero = jnp.zeros((SEQS_DEV, TOK_SEQ, HEADS, KEY), jnp.float32)
    pos_zero = jnp.zeros((SEQS_DEV, TOK_SEQ, HEADS, BASIS), jnp.float32)

    def sum_step(state_four, blk_index):
        pair_next, score_grad, soft_probs = query_terms((state_four[0], state_four[1]), blk_index)
        key_part = jnp.einsum(
            "shnc,snhk->schk", score_grad, queries, preferred_element_type=jnp.float32
        ).reshape(SEQS_DEV, blk_len, HK)
        value_part = jnp.einsum(
            "shnc,snhv->schv",
            soft_probs.astype(jnp.bfloat16),
            grad_att,
            preferred_element_type=jnp.float32,
        ).reshape(SEQS_DEV, blk_len, HV)
        key_acc = lax.dynamic_update_slice_in_dim(state_four[2], key_part, blk_index * blk_len, 1)
        value_acc = lax.dynamic_update_slice_in_dim(
            state_four[3], value_part, blk_index * blk_len, 1
        )
        return ((pair_next[0], pair_next[1], key_acc, value_acc), None)

    start_four = (
        query_zero,
        pos_zero,
        jnp.zeros((SEQS_DEV, seq_len, HK), jnp.float32),
        jnp.zeros((SEQS_DEV, seq_len, HV), jnp.float32),
    )
    (query_acc, pos_acc, key_terms_all, value_terms_all), _ = lax.scan(
        sum_step, start_four, blk_steps
    )
    key_sum, value_sum = (
        lax.psum_scatter(
            key_terms_all.astype(jnp.bfloat16), "seq", scatter_dimension=1, tiled=True
        ).astype(jnp.float32),
        lax.psum_scatter(
            value_terms_all.astype(jnp.bfloat16), "seq", scatter_dimension=1, tiled=True
        ).astype(jnp.float32),
    )
    key_grad = key_sum.reshape(row_count, HK).astype(jnp.bfloat16)
    value_grad = value_sum.reshape(row_count, HV).astype(jnp.bfloat16)
    query_low = query_acc.astype(jnp.bfloat16).reshape(row_count, HK)
    content_grad = jnp.sum(query_low, axis=0, dtype=jnp.float32)
    pos_low = pos_acc.astype(jnp.bfloat16).reshape(row_count, HEADS, BASIS).astype(jnp.float32)
    pos_in_grad = jnp.einsum("lhb,bhk->lhk", pos_low, rel_full, precision=HIGH)
    rel_grad = jnp.einsum("lhb,lhk->bhk", pos_low, pos_in, precision=HIGH).reshape(BASIS, HK)
    position_grad = jnp.sum(pos_in_grad, axis=0).reshape(HK)
    query_grad = (
        0.125 * (query_low.astype(jnp.float32) + pos_in_grad.reshape(row_count, HK))
    ).astype(jnp.bfloat16)
    wq_grad = weight_product(normed, query_grad)
    wk_grad = weight_product(normed, key_grad)
    wv_grad = weight_product(normed, value_grad)
    grad_normed = (
        input_product(query_grad, query_full)
        + input_product(key_grad, key_full)
        + input_product(value_grad, value_full)
    )
    _, pull_one = jax.vjp(layer_norm, inputs_f, gain_one, bias_one)
    grad_norm_in, gain_one_grad, bias_one_grad = pull_one(grad_normed)
    grad_inputs = (grad_one.astype(jnp.float32) + grad_norm_in).reshape(SEQS_DEV, TOK_SEQ, D)
    mixer_grads = (
        lax.psum_scatter(gain_one_grad, ("win", "seq"), scatter_dimension=0, tiled=True),
        lax.psum_scatter(bias_one_grad, ("win", "seq"), scatter_dimension=0, tiled=True),
        lax.psum_scatter(wq_grad, ("win", "seq"), scatter_dimension=0, tiled=True),
        lax.psum_scatter(wk_grad, ("win", "seq"), scatter_dimension=0, tiled=True),
        lax.psum_scatter(wv_grad, ("win", "seq"), scatter_dimension=0, tiled=True),
        lax.psum_scatter(rel_grad, ("win", "seq"), scatter_dimension=1, tiled=True),
        lax.psum_scatter(content_grad, ("win", "seq"), scatter_dimension=0, tiled=True),
        lax.psum_scatter(position_grad, ("win", "seq"), scatter_dimension=0, tiled=True),
        lax.psum_scatter(out_grad, ("win", "seq"), scatter_dimension=0, tiled=True),
    )
    tail_grads = (
        lax.psum_scatter(gain_two_grad, ("win", "seq"), scatter_dimension=0, tiled=True),
        lax.psum_scatter(bias_two_grad, ("win", "seq"), scatter_dimension=0, tiled=True),
        lax.psum_scatter(in_grad, ("win", "seq"), scatter_dimension=0, tiled=True),
        lax.psum_scatter(ibias_grad, ("win", "seq"), scatter_dimension=0, tiled=True),
        lax.psum_scatter(hid_grad, ("win", "seq"), scatter_dimension=0, tiled=True),
        lax.psum_scatter(hbias_grad, ("win", "seq"), scatter_dimension=0, tiled=True),
        lax.psum_scatter(up_grad, ("win", "seq"), scatter_dimension=0, tiled=True),
        lax.psum_scatter(skip_weight_grad, ("win", "seq"), scatter_dimension=0, tiled=True),
        lax.psum_scatter(mbias_grad, ("win", "seq"), scatter_dimension=0, tiled=True),
        lax.psum_scatter(depth_grad, ("win", "seq"), scatter_dimension=1, tiled=True),
        lax.psum_scatter(point_grad, ("win", "seq"), scatter_dimension=0, tiled=True),
        lax.psum_scatter(pbias_grad, ("win", "seq"), scatter_dimension=0, tiled=True),
        lax.psum_scatter(head_grad, ("win", "seq"), scatter_dimension=0, tiled=True),
    )
    return (
        (loss_mean, head_in, grad_inputs, skip_grad)
        + tuple(mixer_grads)
        + tuple(tail_grads)
        + (head_bias_grad,)
    )


def solution(mesh):
    return jax.shard_map(
        body,
        mesh=mesh,
        in_specs=(
            P("win", "seq", None),
            P("win", "seq", None),
            P("win", "seq", None),
            P(("win", "seq")),
            P(("win", "seq")),
            P(("win", "seq"), None),
            P(("win", "seq"), None),
            P(("win", "seq"), None),
            P(None, ("win", "seq")),
            P(("win", "seq")),
            P(("win", "seq")),
            P(("win", "seq"), None),
            P(("win", "seq")),
            P(("win", "seq")),
            P(("win", "seq"), None),
            P(("win", "seq")),
            P(("win", "seq"), None),
            P(("win", "seq")),
            P(("win", "seq"), None),
            P(("win", "seq"), None),
            P(("win", "seq")),
            P(None, ("win", "seq")),
            P(("win", "seq"), None),
            P(("win", "seq")),
            P(("win", "seq"), None),
            P(),
        ),
        out_specs=(
            P(),
            P("win", "seq", None),
            P("win", "seq", None),
            P("win", "seq", None),
            P(("win", "seq")),
            P(("win", "seq")),
            P(("win", "seq"), None),
            P(("win", "seq"), None),
            P(("win", "seq"), None),
            P(None, ("win", "seq")),
            P(("win", "seq")),
            P(("win", "seq")),
            P(("win", "seq"), None),
            P(("win", "seq")),
            P(("win", "seq")),
            P(("win", "seq"), None),
            P(("win", "seq")),
            P(("win", "seq"), None),
            P(("win", "seq")),
            P(("win", "seq"), None),
            P(("win", "seq"), None),
            P(("win", "seq")),
            P(None, ("win", "seq")),
            P(("win", "seq"), None),
            P(("win", "seq")),
            P(("win", "seq"), None),
            P(),
        ),
        check_vma=False,
    )
```

profile of v0, /device:TPU:0, one launch (start us, length us, event | category | flops | bytes accessed | tf_op | source)
XLA Modules:
  0.0 2819.7 jit_solution(10923740324737899767)
XLA Ops:
  18.0 43.4 %all-reduce.22 = (bf16[1536]{0:T(1024)(128)(2,1)S(1)}, bf16[1536]{0:T(1024)(128)(2,1)S(1)}, bf16[512]{0:T(512)(128)(2,1)S(1)}, bf16[512]{0:T(512)(128)(2,1)S(1)}...) all-reduce(bf16[1536]{0:T(1024)(128)(2,1)S(1)} %dynamic-update-slic, ...), channel_id=1, replica_groups=mesh['win'=8,'seq'=4] {'win','seq'}, use_global_device_ids=true, to_apply=%add.1 | all-reduce | flops 14848 | bytes 59392
  72.0 62.4 %all-gather.16.cloned.1.call-done = bf16[1536,1536]{1,0:T(8,128)(2,1)} async-done(((bf16[48,1536]{1,0:T(8,128)(2,1)}), bf16[1536,1536]{1,0:T(8,128)(2,1)}) %all-gather.16.cloned.1.call-update) | async-done | bytes 4718608 | tf_op jit(solution)/shard_map/all_gather | solution.py:130
  143.9 39.8 %all_gather.81 = bf16[32,512]{0,1:T(8,128)(2,1)S(1)} all-gather(bf16[32,16]{0,1:T(8,128)(2,1)S(1)} %copy-done.75), channel_id=1, replica_groups=mesh['win'=8,'seq'=4] {'win','seq'}, dimensions={1}, use_global_device_ids=true | all-gather | bytes 33792 | tf_op jit(solution)/shard_map/all_gather | solution.py:131
  185.0 36.8 %all-gather.2 = bf16[32,48,3]{1,2,0:T(4,128)(2,1)S(1)} all-gather(bf16[1,48,3]{1,2,0:T(4,128)(2,1)S(1)} %bitcast.554), channel_id=1, replica_groups=mesh['win'=8,'seq'=4] {'win','seq'}, dimensions={0}, use_global_device_ids=true | all-gather | bytes 9504 | tf_op jit(solution)/shard_map/all_gather | solution.py:146
  229.4 49.0 %while.60 = (s32[]{:T(128)}, f32[1,8,256]{2,1,0:T(8,128)S(1)}, f32[1,8,256]{2,1,0:T(8,128)S(1)}, s32[2]{0:T(128)S(1)}, bf16[1,1024,512]{1,2,0:T(8,128)(2,1)}, /*...) while((s32[]{:T(128)}, f32[1,8,256]{2,1,0:T(8,128)S(1)}, ...), condition=%wide.region_5.6_spmd.clone, body=%wide.region_2.5_spmd.clone.sunk | while | flops 231353136 | bytes 46119232 | solution.py:216
  283.1 46.7 %while.61 = (s32[]{:T(128)}, f32[1,256,8,192]{1,3,2,0:T(8,128)}, s32[2]{0:T(128)S(1)}, bf16[1,1024,1536]{1,2,0:T(8,128)(2,1)}, bf16[1,1024,512]{1,2,0:T(8,128)(2...) while((s32[]{:T(128)}, f32[1,256,8,192]{1,3,2,0:T(8,128)}, ...), condition=%wide.region_7.8_spmd.clone, body=%wide.region_6.7_spmd.clone.sunk | while | flops 633733952 | bytes 45496652 | solution.py:227
  337.2 52.4 %all-gather.24.cloned.1.call-done = bf16[1536,3072]{1,0:T(8,128)(2,1)} async-done(((bf16[48,3072]{1,0:T(8,128)(2,1)}), bf16[1536,3072]{1,0:T(8,128)(2,1)}) %all-gather.24.cloned.1.call-update) | async-done | bytes 9437200 | tf_op jit(solution)/shard_map/all_gather | solution.py:139
  397.5 75.5 %all-gather.26.cloned.1.call-done = bf16[3072,1536]{1,0:T(8,128)(2,1)} async-done(((bf16[96,1536]{1,0:T(8,128)(2,1)}), bf16[3072,1536]{1,0:T(8,128)(2,1)}) %all-gather.26.cloned.1.call-update) | async-done | bytes 9437200 | tf_op jit(solution)/shard_map/all_gather | solution.py:141
  481.4 56.9 %all-gather.28.cloned.1.call-done = bf16[1536,1536]{1,0:T(8,128)(2,1)} async-done(((bf16[48,1536]{1,0:T(8,128)(2,1)}), bf16[1536,1536]{1,0:T(8,128)(2,1)}) %all-gather.28.cloned.1.call-update) | async-done | bytes 4718608 | tf_op jit(solution)/shard_map/all_gather | solution.py:143
  550.2 50.9 %all-gather.30.cloned.1.call-done = bf16[1280,1536]{1,0:T(8,128)(2,1)} async-done(((bf16[40,1536]{1,0:T(8,128)(2,1)}), bf16[1280,1536]{1,0:T(8,128)(2,1)}) %all-gather.30.cloned.1.call-update) | async-done | bytes 3932176 | tf_op jit(solution)/shard_map/all_gather | solution.py:144
  616.9 49.4 %all-gather.32.cloned.1.call-done = bf16[1536,1536]{1,0:T(8,128)(2,1)} async-done(((bf16[48,1536]{1,0:T(8,128)(2,1)}), bf16[1536,1536]{1,0:T(8,128)(2,1)}) %all-gather.32.cloned.1.call-update) | async-done | bytes 4718608 | tf_op jit(solution)/shard_map/all_gather | solution.py:147
  673.8 70.8 %all-gather.34.cloned.1.call-done = bf16[1536,2608]{1,0:T(8,128)(2,1)} async-done(((bf16[48,2608]{1,0:T(8,128)(2,1)}), bf16[1536,2608]{1,0:T(8,128)(2,1)}) %all-gather.34.cloned.1.call-update) | async-done | bytes 8011792 | tf_op jit(solution)/shard_map/all_gather | solution.py:149
  744.6 14.3 convert_reduce_fusion.1
  764.8 11.4 all-reduce.21
  845.4 43.9 %while.62 = (s32[]{:T(128)}, f32[1,8,256]{2,1,0:T(8,128)S(1)}, s32[2]{0:T(128)S(1)}, bf16[1,1024,512]{1,2,0:T(8,128)(2,1)}, bf16[1,256,8,64]{1,3,2,0:T(8,128)(2,...) while((s32[]{:T(128)}, f32[1,8,256]{2,1,0:T(8,128)S(1)}, ...), condition=%wide.region_23.24_spmd.clone, body=%wide.region_21.23_spmd.clone.sunk | while | flops 633998144 | bytes 80918928 | solution.py:343
  892.5 86.9 %while.63 = (s32[]{:T(128)}, f32[1,256,8,64]{1,3,2,0:T(8,128)}, f32[1,256,8,32]{3,2,1,0:T(8,128)}, bf16[1,1024,512]{1,2,0:T(8,128)(2,1)}, bf16[1,1024,1536]{1,2,...) while((s32[]{:T(128)}, f32[1,256,8,64]{1,3,2,0:T(8,128)}, ...), condition=%wide.region_25.26_spmd.clone, body=%wide.region_24.25_spmd.clone.sunk | while | flops 1391461120 | bytes 157440672 | solution.py:385
  990.9 14.2 reduce-scatter.21.cloned.1.call-done
  1055.1 12.7 fusion.87
  1068.5 11.2 fusion.132
  1104.5 41.6 %reduce-scatter.47.cloned.1.call-done = f32[48,3]{1,0:T(8,128)} async-done(((f32[1536,3]{1,0:T(8,128)}), f32[48,3]{1,0:T(8,128)}) %reduce-scatter.47.cloned.1.call-update) | async-done | bytes 592
  1154.5 41.8 %all-reduce.24 = (f32[]{:T(128)}, f32[1536]{0:T(1024)S(1)}, f32[1536]{0:T(1024)S(1)}, f32[512]{0:T(512)S(1)}, f32[512]{0:T(512)S(1)}, /*index=5*/f32[1536]{0:T(1...) all-reduce(f32[]{:T(128)S(6)} %add.491, ...), channel_id=1, replica_groups=mesh['win'=8,'seq'=4] {'win','seq'}, use_global_device_ids=true, to_apply=%region_17.18 | all-reduce | flops 17457 | bytes 139656 | tf_op jit(solution)/shard_map/psum | solution.py:275
  1205.9 75.4 %reduce-scatter.43.cloned.1.call-done = f32[16,32]{1,0:T(8,128)} async-done(((f32[512,32]{1,0:T(8,128)}), f32[16,32]{1,0:T(8,128)}) %reduce-scatter.43.cloned.1.call-update) | async-done | bytes 2064
  1281.3 104.2 %reduce-scatter.25.cloned.1.call-done = f32[48,512]{1,0:T(8,128)} async-done(((f32[1536,512]{1,0:T(8,128)}), f32[48,512]{1,0:T(8,128)}) %reduce-scatter.25.cloned.1.call-update) | async-done | bytes 98320 | tf_op jit(solution)/shard_map/reduce_scatter | solution.py:421
  1385.5 107.2 %reduce-scatter.27.cloned.1.call-done = f32[48,512]{1,0:T(8,128)} async-done(((f32[1536,512]{1,0:T(8,128)}), f32[48,512]{1,0:T(8,128)}) %reduce-scatter.27.cloned.1.call-update) | async-done | bytes 98320 | tf_op jit(solution)/shard_map/reduce_scatter | solution.py:422
  1492.8 128.6 %reduce-scatter.45.cloned.1.call-done = f32[40,1536]{1,0:T(8,128)} async-done(((f32[1280,1536]{1,0:T(8,128)}), f32[40,1536]{1,0:T(8,128)}) %reduce-scatter.45.cloned.1.call-update) | async-done | bytes 245776
  1621.4 141.2 %reduce-scatter.39.cloned.1.call-done = f32[48,1536]{1,0:T(8,128)} async-done(((f32[1536,1536]{1,0:T(8,128)}), f32[48,1536]{1,0:T(8,128)}) %reduce-scatter.39.cloned.1.call-update) | async-done | bytes 294928 | tf_op jit(solution)/shard_map/reduce_scatter | solution.py:440
  1762.6 141.9 %reduce-scatter.31.cloned.1.call-done = f32[48,1536]{1,0:T(8,128)} async-done(((f32[1536,1536]{1,0:T(8,128)}), f32[48,1536]{1,0:T(8,128)}) %reduce-scatter.31.cloned.1.call-update) | async-done | bytes 294928 | tf_op jit(solution)/shard_map/reduce_scatter | solution.py:427
  1904.6 141.2 %reduce-scatter.37.cloned.1.call-done = f32[48,1536]{1,0:T(8,128)} async-done(((f32[1536,1536]{1,0:T(8,128)}), f32[48,1536]{1,0:T(8,128)}) %reduce-scatter.37.cloned.1.call-update) | async-done | bytes 294928 | tf_op jit(solution)/shard_map/reduce_scatter | solution.py:436
  2045.8 142.2 %reduce-scatter.29.cloned.1.call-done = f32[48,1536]{1,0:T(8,128)} async-done(((f32[1536,1536]{1,0:T(8,128)}), f32[48,1536]{1,0:T(8,128)}) %reduce-scatter.29.cloned.1.call-update) | async-done | bytes 294928 | tf_op jit(solution)/shard_map/reduce_scatter | solution.py:423
  2188.0 196.4 %reduce-scatter.41.cloned.1.call-done = f32[48,2608]{1,0:T(8,128)} async-done(((f32[1536,2608]{1,0:T(8,128)}), f32[48,2608]{1,0:T(8,128)}) %reduce-scatter.41.cloned.1.call-update) | async-done | bytes 500752 | tf_op jit(solution)/shard_map/reduce_scatter | solution.py:442
  2384.4 213.8 %reduce-scatter.33.cloned.1.call-done = f32[48,3072]{1,0:T(8,128)} async-done(((f32[1536,3072]{1,0:T(8,128)}), f32[48,3072]{1,0:T(8,128)}) %reduce-scatter.33.cloned.1.call-update) | async-done | bytes 589840 | tf_op jit(solution)/shard_map/reduce_scatter | solution.py:432
  2598.3 213.6 %reduce-scatter.35.cloned.1.call-done = f32[96,1536]{1,0:T(8,128)} async-done(((f32[3072,1536]{1,0:T(8,128)}), f32[96,1536]{1,0:T(8,128)}) %reduce-scatter.35.cloned.1.call-update) | async-done | bytes 589840 | tf_op jit(solution)/shard_map/reduce_scatter | solution.py:434
  (507 shorter events, 502.9 us)
Async XLA Ops:
  7.2 593.8 %copy-start = (bf16[1,512,1280]{2,1,0:T(8,128)(2,1)S(1)}, bf16[1,512,1280]{2,1,0:T(8,128)(2,1)}, u32[]{:S(2)}) copy-start(bf16[1,512,1280]{2,1,0:T(8,128)(2,1)} %param.35) | copy-start | bytes 3932164
  7.2 61.7 %all-gather.18.cloned.1.call-start = ((), (), s32[]{:S(2)}) async-start(), calls=%async_computation.15 | async-start | bytes 1622016 | tf_op jit(solution)/shard_map/all_gather | solution.py:129
  8.0 126.4 %all-gather.16.cloned.1.call-start = ((), (), s32[]{:S(2)}) async-start(), calls=%async_computation.14 | async-start | bytes 4866048 | tf_op jit(solution)/shard_map/all_gather | solution.py:130
  8.7 213.8 %all-gather.20.cloned.1.call-start = ((), (), s32[]{:S(2)}) async-start(), calls=%async_computation.16 | async-start | bytes 1622016 | tf_op jit(solution)/shard_map/all_gather | solution.py:128
  9.4 217.6 %all-gather.38.cloned.1.call-start = ((), (), s32[]{:S(2)}) async-start(), calls=%async_computation.36 | async-start | bytes 1310720 | tf_op jit(solution)/shard_map/all_gather | solution.py:186
  72.0 206.5 %all-gather.36.cloned.1.call-start = ((), (), s32[]{:S(2)}) async-start(), calls=%async_computation.35 | async-start | bytes 3932160 | tf_op jit(solution)/shard_map/all_gather | solution.py:187
  139.1 193.2 %all-gather.22.cloned.1.call-start = ((), (), s32[]{:S(2)}) async-start(), calls=%async_computation.17 | async-start | bytes 4866048 | tf_op jit(solution)/shard_map/all_gather | solution.py:134
  139.7 249.9 %all-gather.24.cloned.1.call-start = ((), (), s32[]{:S(2)}) async-start(), calls=%async_computation.18 | async-start | bytes 9732096 | tf_op jit(solution)/shard_map/all_gather | solution.py:139
  140.4 332.7 %all-gather.26.cloned.1.call-start = ((), (), s32[]{:S(2)}) async-start(), calls=%async_computation.19 | async-start | bytes 9732096 | tf_op jit(solution)/shard_map/all_gather | solution.py:141
  141.2 397.1 %all-gather.28.cloned.1.call-start = ((), (), s32[]{:S(2)}) async-start(), calls=%async_computation.20 | async-start | bytes 4866048 | tf_op jit(solution)/shard_map/all_gather | solution.py:143
  141.9 459.1 %all-gather.30.cloned.1.call-start = ((), (), s32[]{:S(2)}) async-start(), calls=%async_computation.21 | async-start | bytes 4055040 | tf_op jit(solution)/shard_map/all_gather | solution.py:144
  142.5 523.8 %all-gather.32.cloned.1.call-start = ((), (), s32[]{:S(2)}) async-start(), calls=%async_computation.22 | async-start | bytes 4866048 | tf_op jit(solution)/shard_map/all_gather | solution.py:147
  143.2 601.4 %all-gather.34.cloned.1.call-start = ((), (), s32[]{:S(2)}) async-start(), calls=%async_computation.23 | async-start | bytes 8515584 | tf_op jit(solution)/shard_map/all_gather | solution.py:149
  143.8 861.3 %reduce-scatter.21.cloned.1.call-start = ((), (), s32[]{:S(2)}) async-start(), calls=%async_computation.24 | async-start | bytes 1310720 | tf_op jit(solution)/shard_map/reduce_scatter | solution.py:389
  183.7 656.6 %copy-start.45 = (f32[1536]{0:T(1024)}, f32[1536]{0:T(1024)S(1)}, u32[]{:S(2)}) copy-start(f32[1536]{0:T(1024)S(1)} %convert_element_type.382) | copy-start | bytes 18436
  606.6 4.0 collective-permute-start
  608.8 3.8 collective-permute-start.1
  799.7 4.6 collective-permute-start.2
  801.0 3.8 collective-permute-start.3
  979.4 68.9 %reduce-scatter.23.cloned.1.call-start = ((), (), s32[]{:S(2)}) async-start(), calls=%async_computation.25 | async-start | bytes 3932160 | tf_op jit(solution)/shard_map/reduce_scatter | solution.py:392
  980.0 166.1 %reduce-scatter.47.cloned.1.call-start = ((), (), s32[]{:S(2)}) async-start(), calls=%async_computation.39 | async-start | bytes 811008
  981.4 299.9 %reduce-scatter.43.cloned.1.call-start = ((), (), s32[]{:S(2)}) async-start(), calls=%async_computation.37 | async-start | bytes 270336
  987.3 398.3 %reduce-scatter.25.cloned.1.call-start = ((), (), s32[]{:S(2)}) async-start(), calls=%async_computation.26 | async-start | bytes 3244032 | tf_op jit(solution)/shard_map/reduce_scatter | solution.py:421
  990.9 501.9 %reduce-scatter.27.cloned.1.call-start = ((), (), s32[]{:S(2)}) async-start(), calls=%async_computation.27 | async-start | bytes 3244032 | tf_op jit(solution)/shard_map/reduce_scatter | solution.py:422
  1008.4 613.0 %reduce-scatter.45.cloned.1.call-start = ((), (), s32[]{:S(2)}) async-start(), calls=%async_computation.38 | async-start | bytes 8110080
  1025.2 737.5 %reduce-scatter.39.cloned.1.call-start = ((), (), s32[]{:S(2)}) async-start(), calls=%async_computation.33 | async-start | bytes 9732096 | tf_op jit(solution)/shard_map/reduce_scatter | solution.py:440
  1033.6 871.0 %reduce-scatter.31.cloned.1.call-start = ((), (), s32[]{:S(2)}) async-start(), calls=%async_computation.29 | async-start | bytes 9732096 | tf_op jit(solution)/shard_map/reduce_scatter | solution.py:427
  1040.9 1004.9 %reduce-scatter.37.cloned.1.call-start = ((), (), s32[]{:S(2)}) async-start(), calls=%async_computation.32 | async-start | bytes 9732096 | tf_op jit(solution)/shard_map/reduce_scatter | solution.py:436
  1048.2 1139.7 %reduce-scatter.29.cloned.1.call-start = ((), (), s32[]{:S(2)}) async-start(), calls=%async_computation.28 | async-start | bytes 9732096 | tf_op jit(solution)/shard_map/reduce_scatter | solution.py:423
  1054.6 1329.8 %reduce-scatter.41.cloned.1.call-start = ((), (), s32[]{:S(2)}) async-start(), calls=%async_computation.34 | async-start | bytes 17031168 | tf_op jit(solution)/shard_map/reduce_scatter | solution.py:442
  1067.8 1530.5 %reduce-scatter.33.cloned.1.call-start = ((), (), s32[]{:S(2)}) async-start(), calls=%async_computation.30 | async-start | bytes 19464192 | tf_op jit(solution)/shard_map/reduce_scatter | solution.py:432
  1079.7 1732.1 %reduce-scatter.35.cloned.1.call-start = ((), (), s32[]{:S(2)}) async-start(), calls=%async_computation.31 | async-start | bytes 19464192 | tf_op jit(solution)/shard_map/reduce_scatter | solution.py:434
  (92 other events, 3382.1 us)
Sparse Core Ops, SparseCore 0:
  10.9 57.9 all-gather.17
  71.8 62.5 all-gather.15
  137.3 53.7 all-gather.19
  193.1 15.6 all-gather.37
  210.7 28.5 all-gather.35
  242.1 63.6 all-gather.21
  308.6 80.8 all-gather.23
  392.4 80.6 all-gather.25
  476.0 62.2 all-gather.27
  541.0 59.9 all-gather.29
  603.9 62.3 all-gather.31
  669.1 75.4 all-gather.33
  979.5 25.4 reduce-scatter.20
  1007.6 37.9 reduce-scatter.22
  1050.6 95.4 reduce-scatter.46
  1148.8 132.5 reduce-scatter.42
  1288.1 97.4 reduce-scatter.24
  1392.3 100.4 reduce-scatter.26
  1500.0 121.3 reduce-scatter.44
  1627.7 134.8 reduce-scatter.38
  1770.1 134.4 reduce-scatter.30
  1911.1 134.7 reduce-scatter.36
  2053.3 134.6 reduce-scatter.28
  2194.8 189.6 reduce-scatter.40
  2392.6 205.6 reduce-scatter.32
  2606.2 205.5 reduce-scatter.34
where the time goes:
time: 2830 us; the launch traced here: 2820 us
  waiting for transfers between devices  2090 us (74%)
  matrix products  295 us (10%)
  blocking collectives  173 us (6%)
  local copies, waits for them, and re-layouts  146 us (5%)
  other arithmetic  75 us (3%)
    unnamed x29, waiting for transfers between devices  253 us
    reduce_scatter x1, waiting for transfers between devices, body(): lax.psum_scatter(in_grad, ('win', 'seq'), scatter_dimension=0, tiled=True)  214 us
    reduce_scatter x1, waiting for transfers between devices, body(): lax.psum_scatter(hid_grad, ('win', 'seq'), scatter_dimension=0, tiled=True)  214 us
    reduce_scatter x1, waiting for transfers between devices, body(): lax.psum_scatter(head_grad, ('win', 'seq'), scatter_dimension=0, tiled=True)  196 us
    reduce_scatter x1, waiting for transfers between devices, body(): lax.psum_scatter(wv_grad, ('win', 'seq'), scatter_dimension=0, tiled=True)  142 us
    reduce_scatter x1, waiting for transfers between devices, body(): lax.psum_scatter(out_grad, ('win', 'seq'), scatter_dimension=0, tiled=True)  142 us
    reduce_scatter x1, waiting for transfers between devices, body(): lax.psum_scatter(point_grad, ('win', 'seq'), scatter_dimension=0, tiled=T...  141 us
    reduce_scatter x1, waiting for transfers between devices, body(): lax.psum_scatter(up_grad, ('win', 'seq'), scatter_dimension=0, tiled=True)  141 us
  transfers between devices with their start and end apart: 30, of which 23 were waited for; matrix products, arithmetic and copies ran while one was open for 10% of the time, Pallas kernels for 0%

commit v1 on v0

--- a/solution.py
+++ b/solution.py
@@ -1,8 +1,11 @@
+import functools
 import math
 
 import jax
 import jax.numpy as jnp
 from jax import lax
+from jax.experimental import pallas as pl
+from jax.experimental.pallas import tpu as pltpu
 from jax.sharding import PartitionSpec as P
 
 D = 1536
@@ -18,6 +21,8 @@
 HV = 1536
 
 
+WIN, SEQ = "win", "seq"
+BOTH = (WIN, SEQ)
 EPS = 1e-05
 HIGH = lax.Precision.HIGHEST
 
@@ -87,7 +92,522 @@
     return (content + position, basis_grid)
 
 
-def body(
+F32 = jnp.float32
+LOW = jnp.bfloat16
+ROWS = 256
+FF = 3072
+RANKS = 4
+WINDOWS = 8
+
+
+def wide_table(seq_len):
+    offsets = (seq_len - 1 - jnp.arange(2 * seq_len, dtype=jnp.int32)).astype(F32)
+    return basis_table(offsets, seq_len, BASIS).astype(LOW).T
+
+
+def offset_window(table_ref, keys):
+    start = keys - ROWS - pl.program_id(0) * ROWS
+    return table_ref[:, pl.ds(pl.multiple_of(start, 128), keys + ROWS)]
+
+
+def row_scores(query, key, pos_query, window):
+    keys = key.shape[0]
+    wide = product(pos_query, window)
+    lined = pltpu.roll(wide, keys + 1, 1, stride=1, stride_axis=0)
+    return input_product(query, key) + lined[:, :keys]
+
+
+def head_columns(head):
+    return (
+        slice(head * KEY, (head + 1) * KEY),
+        slice(head * VAL, (head + 1) * VAL),
+        slice(head * BASIS, (head + 1) * BASIS),
+    )
+
+
+def mix_kernel(heads, q_ref, k_ref, v_ref, pos_ref, table_ref, out_ref, norm_ref):
+    window = offset_window(table_ref, k_ref.shape[0])
+    for head in range(heads):
+        ks, vs, bs = head_columns(head)
+        scores = row_scores(q_ref[:, ks], k_ref[:, ks], pos_ref[:, bs], window)
+        top = jnp.max(scores, axis=1, keepdims=True)
+        powers = jnp.exp(scores - top)
+        total = jnp.sum(powers, axis=1, keepdims=True)
+        weights = (powers * (1.0 / total)).astype(LOW)
+        out_ref[:, vs] = product(weights, v_ref[:, vs]).astype(LOW)
+        norm_ref[:, head : head + 1] = top + jnp.log(total)
+
+
+def mix_grad_kernel(
+    heads,
+    q_ref,
+    k_ref,
+    v_ref,
+    pos_ref,
+    table_ref,
+    norm_ref,
+    ga_ref,
+    dq_ref,
+    dpos_ref,
+    dk_ref,
+    dv_ref,
+    dk_sum,
+    dv_sum,
+):
+    step = pl.program_id(0)
+    keys = k_ref.shape[0]
+    window = offset_window(table_ref, keys)
+    down = lax.broadcasted_iota(jnp.int32, (ROWS, ROWS), 0)
+    across = lax.broadcasted_iota(jnp.int32, (ROWS, ROWS), 1)
+    flip = (down + across == ROWS - 1).astype(LOW)
+
+    @pl.when(step == 0)
+    def _():
+        dk_sum[...] = jnp.zeros_like(dk_sum)
+        dv_sum[...] = jnp.zeros_like(dv_sum)
+
+    for head in range(heads):
+        ks, vs, bs = head_columns(head)
+        query, key, value, grad = q_ref[:, ks], k_ref[:, ks], v_ref[:, vs], ga_ref[:, vs]
+        scores = row_scores(query, key, pos_ref[:, bs], window)
+        probs = jnp.exp(scores - norm_ref[:, head : head + 1])
+        dprob = input_product(grad, value)
+        delta = jnp.sum(probs * dprob, axis=1, keepdims=True)
+        dscore = (probs * (dprob - delta)).astype(LOW)
+        dq_ref[:, ks] = product(dscore, key).astype(LOW)
+        dk_sum[:, ks] += weight_product(dscore, query)
+        dv_sum[:, vs] += weight_product(probs.astype(LOW), grad)
+        wide = jnp.concatenate([product(flip, dscore), jnp.zeros((ROWS, ROWS), F32)], axis=1)
+        lined = pltpu.roll(wide, 0, 1, stride=1, stride_axis=0).astype(LOW)
+        turned = input_product(lined, window).astype(LOW)
+        dpos_ref[:, bs] = product(flip, turned).astype(LOW)
+
+    @pl.when(step == pl.num_programs(0) - 1)
+    def _():
+        dk_ref[...] = dk_sum[...].astype(LOW)
+        dv_ref[...] = dv_sum[...].astype(LOW)
+
+
+def row_spec(array):
+    return pl.BlockSpec((ROWS, array.shape[1]), lambda i: (i, 0))
+
+
+def whole_spec(array):
+    return pl.BlockSpec(array.shape, lambda i: (0, 0))
+
+
+def mix(query, key, value, pos_query, table):
+    rows, keys = query.shape[0], key.shape[0]
+    heads = key.shape[1] // KEY
+    norm = jax.ShapeDtypeStruct((rows, heads), F32)
+    out = jax.ShapeDtypeStruct((rows, value.shape[1]), LOW)
+    return pl.pallas_call(
+        functools.partial(mix_kernel, heads),
+        grid=(rows // ROWS,),
+        in_specs=[
+            row_spec(query),
+            whole_spec(key),
+            whole_spec(value),
+            row_spec(pos_query),
+            whole_spec(table),
+        ],
+        out_specs=[row_spec(out), row_spec(norm)],
+        out_shape=[out, norm],
+        compiler_params=pltpu.CompilerParams(vmem_limit_bytes=40 * 2**20),
+        cost_estimate=pl.CostEstimate(
+            flops=40 * rows * keys * heads * (KEY + BASIS + VAL),
+            transcendentals=rows * keys * heads,
+            bytes_accessed=4 * 2**20,
+        ),
+    )(query, key, value, pos_query, table)
+
+
+def mix_grad(query, key, value, pos_query, table, norm, grad):
+    rows, keys = query.shape[0], key.shape[0]
+    heads = key.shape[1] // KEY
+
+    def like(array):
+        return jax.ShapeDtypeStruct(array.shape, LOW)
+
+    return pl.pallas_call(
+        functools.partial(mix_grad_kernel, heads),
+        grid=(rows // ROWS,),
+        in_specs=[
+            row_spec(query),
+            whole_spec(key),
+            whole_spec(value),
+            row_spec(pos_query),
+            whole_spec(table),
+            row_spec(norm),
+            row_spec(grad),
+        ],
+        out_specs=[row_spec(query), row_spec(pos_query), whole_spec(key), whole_spec(value)],
+        out_shape=[like(query), like(pos_query), like(key), like(value)],
+        scratch_shapes=[pltpu.VMEM(key.shape, F32), pltpu.VMEM(value.shape, F32)],
+        compiler_params=pltpu.CompilerParams(vmem_limit_bytes=40 * 2**20),
+        cost_estimate=pl.CostEstimate(
+            flops=60 * rows * keys * heads * (KEY + BASIS + VAL),
+            transcendentals=rows * keys * heads,
+            bytes_accessed=6 * 2**20,
+        ),
+    )(query, key, value, pos_query, table, norm, grad)
+
+
+def trade(block, axis, bits):
+    count = lax.axis_size(axis)
+    return lax.ppermute(block, axis, [(i, i ^ bits) for i in range(count)])
+
+
+def in_order(pieces, index):
+    pieces = list(pieces)
+    bit = 1
+    while bit < len(pieces):
+        odd = (index & bit) != 0
+        pieces = [jnp.where(odd, pieces[k ^ bit], pieces[k]) for k in range(len(pieces))]
+        bit *= 2
+    return pieces
+
+
+def place_kernel(axis, shift, inner, columns, *refs):
+    index = lax.axis_index(axis)
+    index = index // shift if shift > 1 else index
+    count = len(refs) - 1
+    out_ref = refs[count]
+    for k in range(count):
+        to = (index % count) ^ k
+        if columns:
+            width = refs[k].shape[1]
+            out_ref[:, pl.ds(pl.multiple_of(to * width, 128), width)] = refs[k][...]
+        elif inner:
+            for outer in range(inner):
+                out_ref[outer, to] = refs[k][outer]
+        else:
+            out_ref[to] = refs[k][...]
+
+
+def place(pieces, axis, shift=1, inner=0, columns=False):
+    count, shape = len(pieces), pieces[0].shape
+    if columns:
+        shape = (shape[0], count * shape[1])
+    elif inner:
+        shape = (inner, count) + shape[1:]
+    else:
+        shape = (count,) + shape
+    return pl.pallas_call(
+        functools.partial(place_kernel, axis, shift, inner, columns),
+        out_shape=jax.ShapeDtypeStruct(shape, pieces[0].dtype),
+        compiler_params=pltpu.CompilerParams(vmem_limit_bytes=24 * 2**20),
+        cost_estimate=pl.CostEstimate(
+            flops=0,
+            transcendentals=0,
+            bytes_accessed=2 * count * pieces[0].size * pieces[0].dtype.itemsize,
+        ),
+    )(*pieces)
+
+
+def pick(blocks, index):
+    return lax.dynamic_index_in_dim(blocks, index, 0, keepdims=False)
+
+
+tie = lax.optimization_barrier
+
+
+class Flow:
+    def __init__(self, stages):
+        self.stages, self.result = stages, None
+        self.pending = next(stages)
+
+    def step(self, arrived):
+        try:
+            self.pending = self.stages.send(arrived)
+        except StopIteration as last:
+            self.pending, self.result = (), last.value
+
+
+def advance(values, *flows):
+    values, arrived = tie((values, [flow.pending for flow in flows]))
+    for flow, rows in zip(flows, arrived):
+        flow.step(rows)
+    return values
+
+
+def seq_all(rows):
+    near, far = yield trade(rows, SEQ, 1), trade(rows, SEQ, 2)
+    last = yield trade(far, SEQ, 1)
+    return place([rows, near, far, last], SEQ).reshape(RANKS * rows.shape[0], rows.shape[1])
+
+
+def seq_sum(partial, rank):
+    blocks = partial.reshape(RANKS, ROWS, partial.shape[1])
+    sent = jnp.stack([pick(blocks, rank ^ 1), pick(blocks, rank ^ 3)]).astype(LOW)
+    got = yield trade(sent, SEQ, 1)
+    last = yield trade((pick(blocks, rank ^ 2) + got[1].astype(F32)).astype(LOW), SEQ, 2)
+    return pick(blocks, rank) + got[0].astype(F32) + last.astype(F32)
+
+
+def seq_swap(blocks, rank):
+    got = yield [trade(pick(blocks, rank ^ k), SEQ, k) for k in range(1, RANKS)]
+    return [pick(blocks, rank)] + got
+
+
+def deal_kernel(parts, whole_ref, dealt_ref):
+    width = whole_ref.shape[1] // (RANKS * parts)
+    for t in range(RANKS):
+        for p in range(parts):
+            first = (p * RANKS + t) * width
+            dealt_ref[t, :, p * width : (p + 1) * width] = whole_ref[:, first : first + width]
+
+
+def deal(array, parts):
+    rows, columns = array.shape
+    return pl.pallas_call(
+        functools.partial(deal_kernel, parts),
+        out_shape=jax.ShapeDtypeStruct((RANKS, rows, columns // RANKS), array.dtype),
+    )(array)
+
+
+def undeal_kernel(parts, *refs):
+    rank = lax.axis_index(SEQ)
+    width = refs[0].shape[1] // parts
+    pieces = [ref[...].astype(F32) for ref in refs[:RANKS]]
+    for bit in (1, 2):
+        odd = (rank & bit) != 0
+        pieces = [jnp.where(odd, pieces[k ^ bit], pieces[k]) for k in range(RANKS)]
+    for t in range(RANKS):
+        for p in range(parts):
+            first = (p * RANKS + t) * width
+            refs[RANKS][:, first : first + width] = pieces[t][:, p * width : (p + 1) * width]
+
+
+def undeal(pieces, parts):
+    rows, columns = pieces[0].shape
+    return pl.pallas_call(
+        functools.partial(undeal_kernel, parts),
+        out_shape=jax.ShapeDtypeStruct((rows, columns * RANKS), F32),
+    )(*pieces)
+
+
+ROOM = 640
+EXTRA = 8
+SHORT = {}
+for _name, _size in (
+    ("gain1", 48),
+    ("bias1", 48),
+    ("gain2", 48),
+    ("bias2", 48),
+    ("b_in", 96),
+    ("b_hid", 48),
+    ("m", 48),
+    ("p", 48),
+    ("d0", 48),
+    ("d1", 48),
+    ("d2", 48),
+    ("con", 16),
+    ("pos", 16),
+):
+    _first = sum(_high - _low for _low, _high in SHORT.values())
+    SHORT[_name] = (_first, _first + _size)
+DEVICES = WINDOWS * RANKS
+REL = HK // DEVICES
+
+
+def pack_kernel(names, *refs):
+    out_ref = refs[-1]
+    out_ref[...] = jnp.zeros_like(out_ref)
+    for name, ref in zip(names, refs):
+        low, high = SHORT[name]
+        out_ref[0:1, low:high] = ref[...]
+    for b in range(BASIS):
+        out_ref[1:2, b * REL : (b + 1) * REL] = refs[-2][b : b + 1, :]
+
+
+def pack(rows, rel):
+    return pl.pallas_call(
+        functools.partial(pack_kernel, tuple(rows)),
+        out_shape=jax.ShapeDtypeStruct((EXTRA, ROOM), F32),
+    )(*(row.astype(F32)[None] for row in rows.values()), rel.astype(F32))
+
+
+WIDE = ("gain1", "bias1", "gain2", "bias2", "b_hid", "m", "p", "d0", "d1", "d2")
+
+
+def unpack_kernel(table_ref, wide_ref, in_ref, con_ref, pos_ref, rel_ref):
+    rank = lax.axis_index(SEQ)
+    for d in range(DEVICES):
+        line = table_ref[d][0:1]
+        for number, name in enumerate(WIDE):
+            low, high = SHORT[name]
+            wide_ref[number : number + 1, d * 48 : (d + 1) * 48] = line[:, low:high]
+    low, high = SHORT["b_in"]
+    for w in range(WINDOWS):
+        in_ref[0:1, w * 96 : (w + 1) * 96] = table_ref[RANKS * w + rank][0:1, low:high]
+    here = DEVICES // RANKS
+    for j in range(here):
+        block = table_ref[here * rank + j]
+        columns = slice(j * REL, (j + 1) * REL)
+        for ref, name in ((con_ref, "con"), (pos_ref, "pos")):
+            low, high = SHORT[name]
+            ref[0:1, columns] = block[0:1, low:high]
+        for b in range(BASIS):
+            rel_ref[b : b + 1, columns] = block[1:2, b * REL : (b + 1) * REL]
+
+
+def unpack(table):
+    hq = HK // RANKS
+    shapes = ((16, D), (1, FF // RANKS), (1, hq), (1, hq), (BASIS, hq))
+    return pl.pallas_call(
+        unpack_kernel, out_shape=[jax.ShapeDtypeStruct(shape, F32) for shape in shapes]
+    )(table)
+
+
+def pack_grads_kernel(names, *refs):
+    rank = lax.axis_index(SEQ)
+    wide, (in_ref, con_ref, pos_ref, rel_ref, out_ref) = refs[:-5], refs[-5:]
+    out_ref[...] = jnp.zeros_like(out_ref)
+    for d in range(DEVICES):
+        for name, ref in zip(names, wide):
+            low, high = SHORT[name]
+            out_ref[d, 0:1, low:high] = ref[0:1, d * 48 : (d + 1) * 48]
+    low, high = SHORT["b_in"]
+    for w in range(WINDOWS):
+        out_ref[RANKS * w + rank, 0:1, low:high] = in_ref[0:1, w * 96 : (w + 1) * 96]
+    here = DEVICES // RANKS
+    for j in range(here):
+        columns = slice(j * REL, (j + 1) * REL)
+        for ref, name in ((con_ref, "con"), (pos_ref, "pos")):
+            low, high = SHORT[name]
+            out_ref[here * rank + j, 0:1, low:high] = ref[0:1, columns]
+        for b in range(BASIS):
+            out_ref[here * rank + j, 1:2, b * REL : (b + 1) * REL] = rel_ref[
+                b : b + 1, columns
+            ]
+
+
+def pack_grads(rows, in_row, con, pos, rel):
+    return pl.pallas_call(
+        functools.partial(pack_grads_kernel, tuple(rows)),
+        out_shape=jax.ShapeDtypeStruct((DEVICES, EXTRA, ROOM), F32),
+    )(*(row.reshape(1, -1) for row in rows.values()), in_row[None], con[None], pos[None], rel)
+
+
+def finish_kernel(hq, hv, height, *refs):
+    rank = lax.axis_index(SEQ)
+    pieces, (q_ref, k_ref, v_ref, short_ref, rel_ref) = refs[:RANKS], refs[RANKS:]
+    extra = jnp.zeros((EXTRA, ROOM), F32)
+    for k in range(RANKS):
+        block = pieces[k][...].astype(F32)
+        t = rank ^ k
+        weights = block[:height]
+        narrow = pl.ds(pl.multiple_of(t * hq, 128), hq)
+        q_ref[:, narrow] = weights[:, :hq]
+        k_ref[:, narrow] = weights[:, hq : 2 * hq]
+        v_ref[:, pl.ds(pl.multiple_of(t * hv, 128), hv)] = weights[:, 2 * hq :]
+        extra = extra + block[height:]
+    short_ref[...] = extra[0:1]
+    for b in range(BASIS):
+        rel_ref[b : b + 1, :] = extra[1:2, b * REL : (b + 1) * REL]
+
+
+def finish(pieces, hq, hv):
+    height = pieces[0].shape[0] - EXTRA
+    shapes = ((height, HK), (height, HK), (height, HV), (1, ROOM), (BASIS, REL))
+    return pl.pallas_call(
+        functools.partial(finish_kernel, hq, hv, height),
+        out_shape=[jax.ShapeDtypeStruct(shape, F32) for shape in shapes],
+    )(*pieces)
+
+
+def edges(rows, axis):
+    count = lax.axis_size(axis)
+    below, above = yield (
+        lax.ppermute(rows[-1:], axis, [(i, i + 1) for i in range(count - 1)]),
+        lax.ppermute(rows[:1], axis, [(i + 1, i) for i in range(count - 1)]),
+    )
+    return jnp.concatenate([below, rows, above], axis=0)
+
+
+def win_all(block):
+    got = yield [trade(block, WIN, 2 * k) for k in range(1, WINDOWS // 2)]
+    column = place([block] + got, WIN, 2)
+    beside = yield trade(column, WIN, 1)
+    both = place([column, beside], WIN, 1, WINDOWS // 2)
+    return both.reshape((WINDOWS,) + block.shape)
+
+
+def win_sum(parts, window):
+    z, y = window // 2, window % 2
+    parts = parts.reshape((WINDOWS // 2, 2) + parts.shape[1:])
+    sent = lax.dynamic_index_in_dim(parts, 1 - y, 1, keepdims=False)
+    kept = lax.dynamic_index_in_dim(parts, y, 1, keepdims=False)
+    got = yield trade(sent, WIN, 1)
+    column = (kept.astype(F32) + got.astype(F32)).astype(LOW)
+    got = yield [trade(pick(column, z ^ k), WIN, 2 * k) for k in range(1, WINDOWS // 2)]
+    total = pick(column, z).astype(F32)
+    for piece in got:
+        total = total + piece.astype(F32)
+    return total
+
+
+def shared_sum(row):
+    for axis, bits in ((SEQ, 1), (SEQ, 2), (WIN, 1), (WIN, 2), (WIN, 4)):
+        got = yield trade(row, axis, bits)
+        row = row + got
+    return row
+
+
+def core_sum(first_arg, second_arg, rank):
+    core = rank % 2
+    half = second_arg.shape[1] // 2
+    other = lax.dynamic_slice_in_dim(second_arg, (1 - core) * half, half, 1)
+    mine = lax.dynamic_slice_in_dim(second_arg, core * half, half, 1)
+    got = yield trade(weight_product(first_arg, other).astype(LOW), SEQ, 1)
+    total = (weight_product(first_arg, mine) + got.astype(F32)).astype(LOW)
+    return total.reshape(4, 2, 2, total.shape[0] // 16, half)
+
+
+def chip_sum(grads, rank, window):
+    z, y = window // 2, window % 2
+    x, core = rank // 2, rank % 2
+
+    def at(yy, xx):
+        cut = [
+            lax.dynamic_slice(g, (0, yy, xx, 0, 0), (4, 1, 1) + g.shape[3:]).reshape(
+                (4,) + g.shape[3:]
+            )
+            for g in grads
+        ]
+        return cut[0] if len(cut) == 1 else jnp.concatenate(cut, axis=1)
+
+    def plus(a, b):
+        return (a.astype(F32) + b.astype(F32)).astype(LOW)
+
+    corner = at(1 - y, 1 - x)
+    by_x, by_y = yield trade(corner[:2], SEQ, 2), trade(corner[2:], WIN, 1)
+    over_y, over_x = at(1 - y, x), at(y, 1 - x)
+    over_y = jnp.concatenate([plus(over_y[:2], by_x), over_y[2:]])
+    over_x = jnp.concatenate([over_x[:2], plus(over_x[2:], by_y)])
+    from_y, from_x = yield trade(over_y, WIN, 1), trade(over_x, SEQ, 2)
+    own = (at(y, x).astype(F32) + from_y.astype(F32) + from_x.astype(F32)).astype(LOW)
+    got = yield [trade(pick(own, z ^ k), WIN, 2 * k) for k in range(1, 4)]
+    total = pick(own, z).astype(F32)
+    for piece in got:
+        total = total + piece.astype(F32)
+    parts, first = [], 0
+    for g in grads:
+        rows, half = g.shape[3] // 2, g.shape[4]
+        block = total[first : first + 2 * rows].reshape(2, rows, half)
+        first += 2 * rows
+        parts.append((pick(block, core), pick(block, 1 - core)))
+    got = yield trade(jnp.concatenate([sent for _, sent in parts], axis=0), SEQ, 1)
+    results, first = [], 0
+    for kept, sent in parts:
+        piece = got[first : first + sent.shape[0]]
+        first += sent.shape[0]
+        results.append(jnp.concatenate(in_order([kept, piece], core), axis=1))
+    return results
+
+
+def split_body(
     inputs,
     skips,
     counts,
@@ -115,38 +635,373 @@
     w_head,
     head_bias,
 ):
-    seq_count = lax.axis_size("seq")
+    window, rank = lax.axis_index(WIN), lax.axis_index(SEQ)
+    seq_len = ROWS * RANKS
+    hq, hv, ff = HK // RANKS, HV // RANKS, FF // RANKS
+
+    packed = pack(
+        {
+            "gain1": ln1_gain,
+            "bias1": ln1_bias,
+            "gain2": ln2_gain,
+            "bias2": ln2_bias,
+            "b_in": b_in,
+            "b_hid": b_hid,
+            "m": m_bias,
+            "p": p_bias,
+            "d0": w_depth[0],
+            "d1": w_depth[1],
+            "d2": w_depth[2],
+            "con": content_bias,
+            "pos": position_bias,
+        },
+        w_rel,
+    ).astype(LOW)
+    qkv_local = jnp.stack(
+        [
+            jnp.concatenate(
+                [
+                    jnp.concatenate(
+                        [
+                            w_query[:, t * hq : (t + 1) * hq],
+                            w_key[:, t * hq : (t + 1) * hq],
+                            w_value[:, t * hv : (t + 1) * hv],
+                        ],
+                        axis=1,
+                    ),
+                    packed,
+                ]
+            )
+            for t in range(RANKS)
+        ]
+    )
+    inputs_own = inputs.reshape(ROWS, D)
+    qkv_flow = Flow(seq_swap(qkv_local, rank))
+    inputs_flow = Flow(seq_all(inputs_own))
+    out_full = lax.all_gather(w_out, BOTH, axis=0, tiled=True)
+    late_local = jnp.concatenate([w_up, w_skip, w_point])
+    w_in, late_local = advance((w_in, late_local), qkv_flow)
+    qkv_flow = Flow(win_all(place(qkv_flow.result, SEQ).reshape(-1, ROOM)))
+    in_flow = Flow(seq_swap(deal(w_in, WINDOWS), rank))
+    late_full = lax.all_gather(late_local, BOTH, axis=0)
+    w_hid = advance(w_hid, qkv_flow, in_flow, inputs_flow)
+    in_flow = Flow(win_all(place(in_flow.result, SEQ).reshape(-1, ff)))
+    hid_flow = Flow(win_all(w_hid))
+    w_head = advance(w_head, qkv_flow, inputs_flow)
+    head_full = lax.all_gather(w_head, BOTH, axis=0, tiled=True)
+    gathered = qkv_flow.result.reshape(DEVICES, -1, ROOM)
+    height = gathered.shape[1] - EXTRA
+    qkv_part = gathered[:, :height].reshape(D, ROOM)
+    inputs_all = inputs_flow.result
+    wide, in_bias, content, position, rel_part = unpack(gathered[:, height:].astype(F32))
+    row_of = {name: wide[number] for number, name in enumerate(WIDE)}
+    depth_full = [row_of[name] for name in ("d0", "d1", "d2")]
+    r_up, r_skip = w_up.shape[0], w_skip.shape[0]
+    up_full = late_full[:, :r_up].reshape(D, D)
+    skip_full = late_full[:, r_up : r_up + r_skip].reshape(CS, D)
+    point_full = late_full[:, r_up + r_skip :].reshape(D, D)
+    heads_here = hq // KEY
+    same_head = (
+        jnp.arange(hq)[:, None] // KEY == jnp.arange(heads_here * BASIS)[None, :] // BASIS
+    )
+    rel_square = jnp.where(same_head, jnp.tile(rel_part.T, (1, heads_here)), 0.0)
+    gain_one, bias_one = row_of["gain1"], row_of["bias1"]
+    gain_two, bias_two = row_of["gain2"], row_of["bias2"]
+
+    normed = layer_norm(inputs_all.astype(F32), gain_one, bias_one).astype(LOW)
+    projected = product(normed, qkv_part)
+    query_raw = projected[:, :hq] * 0.125
+    queries = (query_raw + content).astype(LOW)
+    pos_in = query_raw + position
+    pos_query = jnp.dot(pos_in, rel_square, precision=HIGH).astype(LOW)
+    keys = projected[:, hq : 2 * hq].astype(LOW)
+    values = projected[:, 2 * hq :].astype(LOW)
+    offsets = wide_table(seq_len)
+    queries, keys, values, pos_query = advance(
+        (queries, keys, values, pos_query), in_flow, hid_flow
+    )
+    mixed, norms = advance(mix(queries, keys, values, pos_query, offsets))
+    swap = Flow(seq_swap(mixed.reshape(RANKS, ROWS, hv), rank))
+    advance((), swap)
+    attended = place(swap.result, SEQ, columns=True)
+    inputs_f = inputs_own.astype(F32)
+    resid_one = inputs_f + product(attended, out_full)
+    normed_flow = Flow(seq_all(layer_norm(resid_one, gain_two, bias_two).astype(LOW)))
+    advance((), normed_flow, in_flow, hid_flow)
+    advance((), normed_flow)
+    normed_two = normed_flow.result
+    in_part = in_flow.result.reshape(D, ff)
+    hid_part = hid_flow.result.reshape(ff, D)
+    pre_act = product(normed_two, in_part) + in_bias
+    hidden = smooth_act(pre_act).astype(LOW)
+    ff_flow = Flow(seq_sum(product(hidden, hid_part), rank))
+    skip_rows = advance(skips.reshape(2 * ROWS, CS), ff_flow)
+    from_skips = product(skip_rows, skip_full) + row_of["m"]
+    from_skips = advance(from_skips, ff_flow)
+    lift_in = (resid_one + ff_flow.result + row_of["b_hid"]).astype(LOW)
+    twice = (jnp.arange(2 * ROWS)[:, None] // 2 == jnp.arange(ROWS)[None, :]).astype(LOW)
+    merged = product(product(twice, lift_in).astype(LOW), up_full) + from_skips
+    merged_flow = Flow(edges(merged.astype(LOW), SEQ))
+    merged = advance(merged, merged_flow)
+    padded = merged_flow.result.astype(F32)
+    depth_out = (
+        depth_full[0] * padded[:-2] + depth_full[1] * padded[1:-1] + depth_full[2] * padded[2:]
+    ).astype(LOW)
+    output = merged + product(depth_out, point_full) + row_of["p"]
+    head_rows = output.astype(LOW)
+    logits = product(head_rows, head_full) + head_bias.astype(F32)
+    rate_rows = jax.nn.softplus(logits)
+    count_rows = counts.reshape(2 * ROWS, TRACKS).astype(F32)
+    total_rate, total_count = lax.psum(
+        (jnp.sum(rate_rows, axis=0), jnp.sum(count_rows, axis=0)), SEQ
+    )
+    log_total = jnp.log(total_rate)
+    window_terms = jnp.sum(total_count * log_total) + 0.2 * jnp.sum(
+        total_rate - total_count * log_total
+    )
+    local_loss = -jnp.sum(count_rows * jnp.log(rate_rows)) + jnp.where(
+        rank == 0, window_terms, 0.0
+    )
+    grad_rate = -count_rows / rate_rows + (0.2 + 0.8 * (total_count / total_rate))
+    grad_rows = (grad_rate * jax.nn.sigmoid(logits)).astype(LOW)
+    head_bias_part = jnp.sum(grad_rows, axis=0, dtype=F32)
+    shared_flow = Flow(shared_sum(jnp.concatenate([head_bias_part, local_loss[None]])))
+    spare = -TRACKS % 256
+    head_core = Flow(core_sum(head_rows, jnp.pad(grad_rows, ((0, 0), (0, spare))), rank))
+    grad_out = input_product(grad_rows, head_full).astype(LOW)
+    pbias_grad = jnp.sum(grad_out, axis=0, dtype=F32)
+    grad_depth = input_product(grad_out, point_full).astype(LOW)
+    grad_out, grad_depth, pbias_grad = advance((grad_out, grad_depth, pbias_grad), head_core)
+    depth_flow = Flow(edges(grad_depth, SEQ))
+    head_flow = Flow(chip_sum([head_core.result], rank, window))
+    depth_grad = jnp.stack(
+        [
+            jnp.sum(grad_depth * padded[:-2], axis=0),
+            jnp.sum(grad_depth * padded[1:-1], axis=0),
+            jnp.sum(grad_depth * padded[2:], axis=0),
+        ]
+    )
+    point_core = Flow(core_sum(depth_out, grad_out, rank))
+    grad_out, depth_grad = advance((grad_out, depth_grad), depth_flow)
+    depth_pad = depth_flow.result
+    merged_low = (
+        grad_out.astype(F32)
+        + depth_full[0] * depth_pad[2:]
+        + depth_full[1] * depth_pad[1:-1]
+        + depth_full[2] * depth_pad[:-2]
+    ).astype(LOW)
+    mbias_grad = jnp.sum(merged_low, axis=0, dtype=F32)
+    lift_grad = weight_product(twice, merged_low).astype(LOW)
+    grad_two = input_product(lift_grad, up_full).astype(LOW)
+    hbias_grad = jnp.sum(grad_two, axis=0, dtype=F32)
+    grad_two, merged_low, lift_grad, mbias_grad, hbias_grad = advance(
+        (grad_two, merged_low, lift_grad, mbias_grad, hbias_grad), head_flow, point_core
+    )
+    two_flow = Flow(seq_all(grad_two))
+    skip_core = Flow(core_sum(skip_rows, merged_low, rank))
+    up_core = Flow(core_sum(lift_in, lift_grad, rank))
+    skip_grad = input_product(merged_low, skip_full).reshape(1, 2 * ROWS, CS)
+    skip_grad = advance(skip_grad, skip_core, up_core)
+    tail_flow = Flow(
+        chip_sum([point_core.result, skip_core.result, up_core.result], rank, window)
+    )
+    advance((), two_flow, shared_flow)
+    advance((), two_flow, shared_flow)
+    grad_two_all = two_flow.result
+    grad_hidden = input_product(grad_two_all, hid_part).astype(LOW)
+    _, pull_act = jax.vjp(smooth_act, pre_act)
+    grad_pre = pull_act(grad_hidden.astype(F32))[0].astype(LOW)
+    ibias_part = jnp.sum(grad_pre, axis=0, dtype=F32)
+    pre_flow = Flow(seq_sum(input_product(grad_pre, in_part), rank))
+    hid_low = weight_product(hidden, grad_two_all).astype(LOW)
+    hid_low, grad_pre, ibias_part = advance(
+        (hid_low, grad_pre, ibias_part), pre_flow, head_flow, tail_flow, shared_flow
+    )
+    hid_flow = Flow(win_sum(hid_low.reshape(WINDOWS, ff // WINDOWS, D), window))
+    in_low = weight_product(normed_two, grad_pre).astype(LOW)
+    in_low = advance(in_low, pre_flow, shared_flow)
+    in_flow = Flow(win_sum(in_low.reshape(WINDOWS, D // WINDOWS, ff), window))
+    _, pull_two = jax.vjp(layer_norm, resid_one, gain_two, bias_two)
+    grad_resid, gain_two_grad, bias_two_grad = pull_two(pre_flow.result)
+    grad_one = (grad_two.astype(F32) + grad_resid).astype(LOW)
+    grad_att = input_product(grad_one, out_full).astype(LOW)
+    att_flow = Flow(
+        seq_swap(
+            jnp.stack([grad_att[:, t * hv : (t + 1) * hv] for t in range(RANKS)]), rank
+        )
+    )
+    out_core = Flow(core_sum(attended, grad_one, rank))
+    grad_one, gain_two_grad, bias_two_grad = advance(
+        (grad_one, gain_two_grad, bias_two_grad),
+        head_flow,
+        tail_flow,
+        hid_flow,
+        out_core,
+        shared_flow,
+    )
+    out_flow = Flow(chip_sum([out_core.result], rank, window))
+    advance((), att_flow, head_flow)
+    grad_att = place(att_flow.result, SEQ).reshape(seq_len, hv)
+    query_low, pos_low, key_grad, value_grad = mix_grad(
+        queries, keys, values, pos_query, offsets, norms, grad_att
+    )
+    query_low, pos_low, key_grad, value_grad = advance(
+        (query_low, pos_low, key_grad, value_grad), in_flow, hid_flow, out_flow, tail_flow
+    )
+    pos_f = pos_low.astype(F32)
+    pos_in_grad = lax.dot_general(
+        pos_f, rel_square, (((1,), (1,)), ((), ())), precision=HIGH
+    )
+    query_grad = (0.125 * (query_low.astype(F32) + pos_in_grad)).astype(LOW)
+    qkv_out = jnp.concatenate([query_grad, key_grad, value_grad], axis=1)
+    content_part = jnp.sum(query_low, axis=0, dtype=F32)
+    rel_cross = lax.dot_general(pos_f, pos_in, (((0,), (0,)), ((), ())), precision=HIGH)
+    rel_rows = jnp.sum(
+        jnp.where(same_head.T, rel_cross, 0.0).reshape(heads_here, BASIS, hq), axis=0
+    )
+    position_part = jnp.sum(pos_in_grad, axis=0)
+    partial = input_product(qkv_out, qkv_part)
+    centred = inputs_all.astype(F32)
+    centred = centred - jnp.mean(centred, axis=-1, keepdims=True)
+    scale = lax.rsqrt(jnp.mean(centred * centred, axis=-1, keepdims=True) + EPS)
+    gain_one_grad = jnp.sum(partial * (centred * scale), axis=0)
+    bias_one_grad = jnp.sum(partial, axis=0)
+    one_flow = Flow(seq_sum(partial, rank))
+    extra = pack_grads(
+        {
+            "gain1": gain_one_grad,
+            "bias1": bias_one_grad,
+            "gain2": gain_two_grad,
+            "bias2": bias_two_grad,
+            "b_hid": hbias_grad,
+            "m": mbias_grad,
+            "p": pbias_grad,
+            "d0": depth_grad[0],
+            "d1": depth_grad[1],
+            "d2": depth_grad[2],
+        },
+        ibias_part,
+        content_part,
+        position_part,
+        rel_rows,
+    ).astype(LOW)
+    qkv_low = weight_product(normed, qkv_out).astype(LOW).reshape(DEVICES, -1, ROOM)
+    qkv_flow = Flow(
+        win_sum(
+            jnp.concatenate([qkv_low, extra], axis=1).reshape(WINDOWS, -1, ROOM), window
+        )
+    )
+    advance((), one_flow, in_flow, out_flow, tail_flow)
+    in_back = Flow(seq_swap(in_flow.result.astype(LOW).reshape(RANKS, -1, ff), rank))
+    advance((), one_flow, qkv_flow)
+    grad_normed = one_flow.result
+    _, pull_one = jax.vjp(lambda rows: layer_norm(rows, gain_one, bias_one), inputs_f)
+    (grad_norm_in,) = pull_one(grad_normed)
+    grad_inputs = (grad_one.astype(F32) + grad_norm_in).reshape(1, ROWS, D)
+    advance((), out_flow, in_back)
+    advance((), qkv_flow, out_flow)
+    qkv_flow = Flow(seq_swap(qkv_flow.result.astype(LOW).reshape(RANKS, -1, ROOM), rank))
+    advance((), qkv_flow)
+    wq_grad, wk_grad, wv_grad, shorts, rel_grad = finish(qkv_flow.result, hq, hv)
+    sums = {name: shorts[0, low:high] for name, (low, high) in SHORT.items()}
+    in_grad = undeal(in_back.result, WINDOWS)
+    point_grad, skip_weight_grad, up_grad = tail_flow.result
+    (out_grad,) = out_flow.result
+    head_grad = head_flow.result[0][:, :TRACKS]
+    hid_grad = hid_flow.result
+    loss_total, head_bias_grad = shared_flow.result[-1], shared_flow.result[:-1]
+    loss_mean = loss_total / (WINDOWS * 2 * seq_len * TRACKS)
+    return (
+        loss_mean,
+        head_rows.reshape(1, 2 * ROWS, D),
+        grad_inputs,
+        skip_grad,
+        sums["gain1"],
+        sums["bias1"],
+        wq_grad,
+        wk_grad,
+        wv_grad,
+        rel_grad,
+        sums["con"],
+        sums["pos"],
+        out_grad,
+        sums["gain2"],
+        sums["bias2"],
+        in_grad,
+        sums["b_in"],
+        hid_grad,
+        sums["b_hid"],
+        up_grad,
+        skip_weight_grad,
+        sums["m"],
+        jnp.stack([sums["d0"], sums["d1"], sums["d2"]]),
+        point_grad,
+        sums["p"],
+        head_grad,
+        head_bias_grad,
+    )
+
+
+def general_body(
+    inputs,
+    skips,
+    counts,
+    ln1_gain,
+    ln1_bias,
+    w_query,
+    w_key,
+    w_value,
+    w_rel,
+    content_bias,
+    position_bias,
+    w_out,
+    ln2_gain,
+    ln2_bias,
+    w_in,
+    b_in,
+    w_hid,
+    b_hid,
+    w_up,
+    w_skip,
+    m_bias,
+    w_depth,
+    w_point,
+    p_bias,
+    w_head,
+    head_bias,
+):
+    seq_count = lax.axis_size(SEQ)
     seq_len = TOK_SEQ * seq_count
-    first_pos = lax.axis_index("seq") * TOK_SEQ
+    first_pos = lax.axis_index(SEQ) * TOK_SEQ
     row_count = SEQS_DEV * TOK_SEQ
     blk_len = 512
     blk_count = seq_len // blk_len
     blk_steps = jnp.arange(blk_count, dtype=jnp.int32)
     mixer_full = (
-        lax.all_gather(ln1_gain, ("win", "seq"), axis=0, tiled=True),
-        lax.all_gather(ln1_bias, ("win", "seq"), axis=0, tiled=True),
-        lax.all_gather(w_query, ("win", "seq"), axis=0, tiled=True),
-        lax.all_gather(w_key, ("win", "seq"), axis=0, tiled=True),
-        lax.all_gather(w_value, ("win", "seq"), axis=0, tiled=True),
-        lax.all_gather(w_rel, ("win", "seq"), axis=1, tiled=True),
-        lax.all_gather(content_bias, ("win", "seq"), axis=0, tiled=True),
-        lax.all_gather(position_bias, ("win", "seq"), axis=0, tiled=True),
-        lax.all_gather(w_out, ("win", "seq"), axis=0, tiled=True),
+        lax.all_gather(ln1_gain, BOTH, axis=0, tiled=True),
+        lax.all_gather(ln1_bias, BOTH, axis=0, tiled=True),
+        lax.all_gather(w_query, BOTH, axis=0, tiled=True),
+        lax.all_gather(w_key, BOTH, axis=0, tiled=True),
+        lax.all_gather(w_value, BOTH, axis=0, tiled=True),
+        lax.all_gather(w_rel, BOTH, axis=1, tiled=True),
+        lax.all_gather(content_bias, BOTH, axis=0, tiled=True),
+        lax.all_gather(position_bias, BOTH, axis=0, tiled=True),
+        lax.all_gather(w_out, BOTH, axis=0, tiled=True),
     )
     tail_full = (
-        lax.all_gather(ln2_gain, ("win", "seq"), axis=0, tiled=True),
-        lax.all_gather(ln2_bias, ("win", "seq"), axis=0, tiled=True),
-        lax.all_gather(w_in, ("win", "seq"), axis=0, tiled=True),
-        lax.all_gather(b_in, ("win", "seq"), axis=0, tiled=True),
-        lax.all_gather(w_hid, ("win", "seq"), axis=0, tiled=True),
-        lax.all_gather(b_hid, ("win", "seq"), axis=0, tiled=True),
-        lax.all_gather(w_up, ("win", "seq"), axis=0, tiled=True),
-        lax.all_gather(w_skip, ("win", "seq"), axis=0, tiled=True),
-        lax.all_gather(m_bias, ("win", "seq"), axis=0, tiled=True),
-        lax.all_gather(w_depth, ("win", "seq"), axis=1, tiled=True),
-        lax.all_gather(w_point, ("win", "seq"), axis=0, tiled=True),
-        lax.all_gather(p_bias, ("win", "seq"), axis=0, tiled=True),
-        lax.all_gather(w_head, ("win", "seq"), axis=0, tiled=True),
+        lax.all_gather(ln2_gain, BOTH, axis=0, tiled=True),
+        lax.all_gather(ln2_bias, BOTH, axis=0, tiled=True),
+        lax.all_gather(w_in, BOTH, axis=0, tiled=True),
+        lax.all_gather(b_in, BOTH, axis=0, tiled=True),
+        lax.all_gather(w_hid, BOTH, axis=0, tiled=True),
+        lax.all_gather(b_hid, BOTH, axis=0, tiled=True),
+        lax.all_gather(w_up, BOTH, axis=0, tiled=True),
+        lax.all_gather(w_skip, BOTH, axis=0, tiled=True),
+        lax.all_gather(m_bias, BOTH, axis=0, tiled=True),
+        lax.all_gather(w_depth, BOTH, axis=1, tiled=True),
+        lax.all_gather(w_point, BOTH, axis=0, tiled=True),
+        lax.all_gather(p_bias, BOTH, axis=0, tiled=True),
+        lax.all_gather(w_head, BOTH, axis=0, tiled=True),
     )
     gain_one = mixer_full[0].astype(jnp.float32)
     bias_one = mixer_full[1].astype(jnp.float32)
@@ -183,8 +1038,8 @@
     key_rows = product(normed, key_full).astype(jnp.bfloat16).reshape(SEQS_DEV, TOK_SEQ, HK)
     values = product(normed, value_full).astype(jnp.bfloat16).reshape(SEQS_DEV, TOK_SEQ, HV)
     keys_all, values_all = (
-        lax.all_gather(key_rows, "seq", axis=1, tiled=True),
-        lax.all_gather(values, "seq", axis=1, tiled=True),
+        lax.all_gather(key_rows, SEQ, axis=1, tiled=True),
+        lax.all_gather(values, SEQ, axis=1, tiled=True),
     )
 
     def key_block(whole_rows, blk_index):
@@ -240,7 +1095,7 @@
         + product(skip_rows, skip_full).reshape(SEQS_DEV, 2 * TOK_SEQ, D)
         + merge_bias
     )
-    padded = with_halo(merged.astype(jnp.bfloat16), (("seq", 1),), 1).astype(merged.dtype)
+    padded = with_halo(merged.astype(jnp.bfloat16), ((SEQ, 1),), 1).astype(merged.dtype)
     depth_out = (
         depth_full[0] * padded[:, :-2]
         + depth_full[1] * padded[:, 1:-1]
@@ -260,20 +1115,20 @@
     count_rows = counts.astype(jnp.float32)
     part_rate = jnp.sum(rate_rows, axis=1)
     part_count = jnp.sum(count_rows, axis=1)
-    total_rate, total_count = lax.psum((part_rate, part_count), "seq")
+    total_rate, total_count = lax.psum((part_rate, part_count), SEQ)
     log_total = jnp.log(total_rate)
     window_terms = jnp.sum(total_count * log_total) + 0.2 * jnp.sum(
         total_rate - total_count * log_total
     )
     local_loss = -jnp.sum(count_rows * jnp.log(rate_rows)) + jnp.where(
-        lax.axis_index("seq") == 0, window_terms, 0.0
+        lax.axis_index(SEQ) == 0, window_terms, 0.0
     )
     count_ratio = total_count / total_rate
     grad_rate = -count_rows / rate_rows + (0.2 + 0.8 * count_ratio)[:, None, :]
     grad_logit = (grad_rate * jax.nn.sigmoid(logits)).astype(jnp.bfloat16)
     bias_part = jnp.sum(grad_logit, axis=(0, 1), dtype=jnp.float32)
-    loss_total, head_bias_grad = lax.psum((local_loss, bias_part), ("win", "seq"))
-    loss_mean = loss_total / (SEQS_DEV * lax.axis_size("win") * 2 * seq_len * TRACKS)
+    loss_total, head_bias_grad = lax.psum((local_loss, bias_part), BOTH)
+    loss_mean = loss_total / (SEQS_DEV * lax.axis_size(WIN) * 2 * seq_len * TRACKS)
     grad_rows = grad_logit.reshape(2 * row_count, TRACKS)
     head_grad = weight_product(head_rows, grad_rows)
     grad_out = input_product(grad_rows, head_full).astype(jnp.bfloat16)
@@ -289,7 +1144,7 @@
             jnp.sum(grad_depth * padded[:, 2:], axis=(0, 1)),
         ]
     )
-    depth_pad = with_halo(grad_depth, (("seq", 1),), 1)
+    depth_pad = with_halo(grad_depth, ((SEQ, 1),), 1)
     grad_merged = (
         grad_out.reshape(SEQS_DEV, 2 * TOK_SEQ, D).astype(jnp.float32)
         + depth_full[0] * depth_pad[:, 2:]
@@ -387,10 +1242,10 @@
     )
     key_sum, value_sum = (
         lax.psum_scatter(
-            key_terms_all.astype(jnp.bfloat16), "seq", scatter_dimension=1, tiled=True
+            key_terms_all.astype(jnp.bfloat16), SEQ, scatter_dimension=1, tiled=True
         ).astype(jnp.float32),
         lax.psum_scatter(
-            value_terms_all.astype(jnp.bfloat16), "seq", scatter_dimension=1, tiled=True
+            value_terms_all.astype(jnp.bfloat16), SEQ, scatter_dimension=1, tiled=True
         ).astype(jnp.float32),
     )
     key_grad = key_sum.reshape(row_count, HK).astype(jnp.bfloat16)
@@ -416,30 +1271,30 @@
     grad_norm_in, gain_one_grad, bias_one_grad = pull_one(grad_normed)
     grad_inputs = (grad_one.astype(jnp.float32) + grad_norm_in).reshape(SEQS_DEV, TOK_SEQ, D)
     mixer_grads = (
-        lax.psum_scatter(gain_one_grad, ("win", "seq"), scatter_dimension=0, tiled=True),
-        lax.psum_scatter(bias_one_grad, ("win", "seq"), scatter_dimension=0, tiled=True),
-        lax.psum_scatter(wq_grad, ("win", "seq"), scatter_dimension=0, tiled=True),
-        lax.psum_scatter(wk_grad, ("win", "seq"), scatter_dimension=0, tiled=True),
-        lax.psum_scatter(wv_grad, ("win", "seq"), scatter_dimension=0, tiled=True),
-        lax.psum_scatter(rel_grad, ("win", "seq"), scatter_dimension=1, tiled=True),
-        lax.psum_scatter(content_grad, ("win", "seq"), scatter_dimension=0, tiled=True),
-        lax.psum_scatter(position_grad, ("win", "seq"), scatter_dimension=0, tiled=True),
-        lax.psum_scatter(out_grad, ("win", "seq"), scatter_dimension=0, tiled=True),
+        lax.psum_scatter(gain_one_grad, BOTH, scatter_dimension=0, tiled=True),
+        lax.psum_scatter(bias_one_grad, BOTH, scatter_dimension=0, tiled=True),
+        lax.psum_scatter(wq_grad, BOTH, scatter_dimension=0, tiled=True),
+        lax.psum_scatter(wk_grad, BOTH, scatter_dimension=0, tiled=True),
+        lax.psum_scatter(wv_grad, BOTH, scatter_dimension=0, tiled=True),
+        lax.psum_scatter(rel_grad, BOTH, scatter_dimension=1, tiled=True),
+        lax.psum_scatter(content_grad, BOTH, scatter_dimension=0, tiled=True),
+        lax.psum_scatter(position_grad, BOTH, scatter_dimension=0, tiled=True),
+        lax.psum_scatter(out_grad, BOTH, scatter_dimension=0, tiled=True),
     )
     tail_grads = (
-        lax.psum_scatter(gain_two_grad, ("win", "seq"), scatter_dimension=0, tiled=True),
-        lax.psum_scatter(bias_two_grad, ("win", "seq"), scatter_dimension=0, tiled=True),
-        lax.psum_scatter(in_grad, ("win", "seq"), scatter_dimension=0, tiled=True),
-        lax.psum_scatter(ibias_grad, ("win", "seq"), scatter_dimension=0, tiled=True),
-        lax.psum_scatter(hid_grad, ("win", "seq"), scatter_dimension=0, tiled=True),
-        lax.psum_scatter(hbias_grad, ("win", "seq"), scatter_dimension=0, tiled=True),
-        lax.psum_scatter(up_grad, ("win", "seq"), scatter_dimension=0, tiled=True),
-        lax.psum_scatter(skip_weight_grad, ("win", "seq"), scatter_dimension=0, tiled=True),
-        lax.psum_scatter(mbias_grad, ("win", "seq"), scatter_dimension=0, tiled=True),
-        lax.psum_scatter(depth_grad, ("win", "seq"), scatter_dimension=1, tiled=True),
-        lax.psum_scatter(point_grad, ("win", "seq"), scatter_dimension=0, tiled=True),
-        lax.psum_scatter(pbias_grad, ("win", "seq"), scatter_dimension=0, tiled=True),
-        lax.psum_scatter(head_grad, ("win", "seq"), scatter_dimension=0, tiled=True),
+        lax.psum_scatter(gain_two_grad, BOTH, scatter_dimension=0, tiled=True),
+        lax.psum_scatter(bias_two_grad, BOTH, scatter_dimension=0, tiled=True),
+        lax.psum_scatter(in_grad, BOTH, scatter_dimension=0, tiled=True),
+        lax.psum_scatter(ibias_grad, BOTH, scatter_dimension=0, tiled=True),
+        lax.psum_scatter(hid_grad, BOTH, scatter_dimension=0, tiled=True),
+        lax.psum_scatter(hbias_grad, BOTH, scatter_dimension=0, tiled=True),
+        lax.psum_scatter(up_grad, BOTH, scatter_dimension=0, tiled=True),
+        lax.psum_scatter(skip_weight_grad, BOTH, scatter_dimension=0, tiled=True),
+        lax.psum_scatter(mbias_grad, BOTH, scatter_dimension=0, tiled=True),
+        lax.psum_scatter(depth_grad, BOTH, scatter_dimension=1, tiled=True),
+        lax.psum_scatter(point_grad, BOTH, scatter_dimension=0, tiled=True),
+        lax.psum_scatter(pbias_grad, BOTH, scatter_dimension=0, tiled=True),
+        lax.psum_scatter(head_grad, BOTH, scatter_dimension=0, tiled=True),
     )
     return (
         (loss_mean, head_in, grad_inputs, skip_grad)
@@ -449,65 +1304,69 @@
     )
 
 
+SPLIT, ROWED, TILED = P(BOTH), P(BOTH, None), P(WIN, SEQ, None)
+
+
 def solution(mesh):
+    paired = mesh.shape[WIN] == 8 and mesh.shape[SEQ] == 4
     return jax.shard_map(
-        body,
+        split_body if paired else general_body,
         mesh=mesh,
         in_specs=(
-            P("win", "seq", None),
-            P("win", "seq", None),
-            P("win", "seq", None),
-            P(("win", "seq")),
-            P(("win", "seq")),
-            P(("win", "seq"), None),
-            P(("win", "seq"), None),
-            P(("win", "seq"), None),
-            P(None, ("win", "seq")),
-            P(("win", "seq")),
-            P(("win", "seq")),
-            P(("win", "seq"), None),
-            P(("win", "seq")),
-            P(("win", "seq")),
-            P(("win", "seq"), None),
-            P(("win", "seq")),
-            P(("win", "seq"), None),
-            P(("win", "seq")),
-            P(("win", "seq"), None),
-            P(("win", "seq"), None),
-            P(("win", "seq")),
-            P(None, ("win", "seq")),
-            P(("win", "seq"), None),
-            P(("win", "seq")),
-            P(("win", "seq"), None),
+            TILED,
+            TILED,
+            TILED,
+            SPLIT,
+            SPLIT,
+            ROWED,
+            ROWED,
+            ROWED,
+            P(None, BOTH),
+            SPLIT,
+            SPLIT,
+            ROWED,
+            SPLIT,
+            SPLIT,
+            ROWED,
+            SPLIT,
+            ROWED,
+            SPLIT,
+            ROWED,
+            ROWED,
+            SPLIT,
+            P(None, BOTH),
+            ROWED,
+            SPLIT,
+            ROWED,
             P(),
         ),
         out_specs=(
             P(),
-            P("win", "seq", None),
-            P("win", "seq", None),
-            P("win", "seq", None),
-            P(("win", "seq")),
-            P(("win", "seq")),
-            P(("win", "seq"), None),
-            P(("win", "seq"), None),
-            P(("win", "seq"), None),
-            P(None, ("win", "seq")),
-            P(("win", "seq")),
-            P(("win", "seq")),
-            P(("win", "seq"), None),
-            P(("win", "seq")),
-            P(("win", "seq")),
-            P(("win", "seq"), None),
-            P(("win", "seq")),
-            P(("win", "seq"), None),
-            P(("win", "seq")),
-            P(("win", "seq"), None),
-            P(("win", "seq"), None),
-            P(("win", "seq")),
-            P(None, ("win", "seq")),
-            P(("win", "seq"), None),
-            P(("win", "seq")),
-            P(("win", "seq"), None),
+            TILED,
+            TILED,
+            TILED,
+            SPLIT,
+            SPLIT,
+            ROWED,
+            ROWED,
+            ROWED,
+            P(None, BOTH),
+            SPLIT,
+            SPLIT,
+            ROWED,
+            SPLIT,
+            SPLIT,
+            ROWED,
+            SPLIT,
+            ROWED,
+            SPLIT,
+            ROWED,
+            ROWED,
+            SPLIT,
+            P(None, BOTH),
+            ROWED,
+            SPLIT,
+            ROWED,
             P(),
         ),
         check_vma=False,

time: 2830 us -> 802 us (0.28)
  waiting for transfers between devices: 2090 us -> 371 us
  matrix products: 295 us -> 109 us
  blocking collectives: 173 us -> 11.2 us
  local copies, waits for them, and re-layouts: 146 us -> 51.4 us
  starting transfers between devices: 10.2 us -> 99 us
  Pallas kernels: 0 us -> 54 us
    reduce_scatter x11 -> x0, waiting for transfers between devices: 1420 us -> none  [the longest x1 214 us: body(): lax.psum_scatter(in_grad, ('win', 'seq'), scatter_dimension=0, tiled=True)]
    all_gather x12 -> x3, waiting for transfers between devices: 423 us -> 0.02 us  [the longest x1 0.02 us: split_body(): out_full = lax.all_gather(w_out, BOTH, axis=0, tiled=True)]
    ppermute x4 -> x95, waiting for transfers between devices: 2.58 us -> 371 us  [the longest x91 371 us: trade(): return lax.ppermute(block, axis, [(i, i ^ bits) for i in range(count)])]
    unnamed x29 -> x3, waiting for transfers between devices: 253 us -> 0.72 us
    dot_general x31 -> x3, matrix products: 110 us -> 3.62 us  [the longest x1 1.45 us: split_body(): lax.dot_general(pos_f, pos_in, (((0,), (0,)), ((), ())), precision=HIGH)]
    ppermute x4 -> x95, starting transfers between devices: 8.4 us -> 98.8 us  [the longest x91 89.7 us: trade(): return lax.ppermute(block, axis, [(i, i ^ bits) for i in range(count)])]
    all_gather x2 -> x0, blocking collectives: 76.7 us -> none  [the longest x1 39.8 us: body(): lax.all_gather(w_rel, ('win', 'seq'), axis=1, tiled=True)]
    pallas_call x0 -> x21, Pallas kernels: none -> 54 us  [the longest x1 17.2 us: mix_grad(): pl.pallas_call(functools.partial(mix_grad_kernel, heads), grid=(rows // R...]
  transfers between devices with their start and end apart: 30 -> 98, of which waited for: 23 -> 38; matrix products, arithmetic and copies ran while one was open for 10% -> 23% of each run, Pallas kernels for 0% -> 7%
where the time goes in v1:
time: 802 us; the launch traced here: 792 us
  waiting for transfers between devices  371 us (46%)
  matrix products  109 us (14%)
  starting transfers between devices  99 us (12%)
  other arithmetic  76.2 us (10%)
  Pallas kernels  54 us (7%)
  local copies, waits for them, and re-layouts  51.4 us (6%)
  between operations  20.2 us (3%)
  blocking collectives  11.2 us (1%)
    ppermute x91, waiting for transfers between devices, trade(): return lax.ppermute(block, axis, [(i, i ^ bits) for i in range(count)])  371 us
    ppermute x91, starting transfers between devices, trade(): return lax.ppermute(block, axis, [(i, i ^ bits) for i in range(count)])  89.7 us
    dot_general x8, matrix products, product(): return jnp.dot(first_arg, second_arg, preferred_element_type=jnp.float32)  45 us
    dot_general x14, matrix products, weight_product(): lax.dot_general(first_arg, second_arg, (((0,), (0,)), ((), ())), preferre...  31.2 us
    dot_general x8, matrix products, input_product(): lax.dot_general(first_arg, second_arg, (((1,), (1,)), ((), ())), preferre...  28.8 us
    pallas_call x1, Pallas kernels, mix_grad(): pl.pallas_call(functools.partial(mix_grad_kernel, heads), grid=(rows // R...  17.2 us
    unnamed x225, local copies, waits for them, and re-layouts  16.8 us
  transfers between devices with their start and end apart: 98, of which 38 were waited for; matrix products, arithmetic and copies ran while one was open for 23% of the time, Pallas kernels for 7%

profile of v1, /device:TPU:0, one launch (start us, length us, event | category | flops | bytes accessed | tf_op | source)
XLA Modules:
  0.0 792.0 jit_solution(16412768044902639423)
XLA Ops:
  36.4 18.5 %collective-permute-done.8.refs_3_ = bf16[48,768]{1,0:T(8,128)(2,1)S(1)} collective-permute-done((bf16[48,768]{1,0:T(8,128)(2,1)S(1)}, bf16[48,768]{1,0:T(8,128)(2,1)S(1)}, u32[]{:S(2)}, u32[]{:S(2)}) %collective-permute-start.8) | collective-permute-done | bytes 73760 | tf_op jit(solution)/shard_map/ppermute | solution.py:258
  60.8 9.7 %collective-permute-done.5.refs_3_ = bf16[224,640]{1,0:T(8,128)(2,1)S(1)} collective-permute-done((bf16[224,640]{1,0:T(8,128)(2,1)S(1)}, bf16[224,640]{1,0:T(8,128)(2,1)S(1)}, u32[]{:S(2)}, u32[]{:S(2)}) %collective-permute-start.5) | collective-permute-done | bytes 286752 | tf_op jit(solution)/shard_map/ppermute | solution.py:258
  70.5 26.1 %collective-permute-done.4.refs_2_ = bf16[224,640]{1,0:T(8,128)(2,1)S(1)} collective-permute-done((bf16[224,640]{1,0:T(8,128)(2,1)S(1)}, bf16[224,640]{1,0:T(8,128)(2,1)S(1)}, u32[]{:S(2)}, u32[]{:S(2)}) %collective-permute-start.4) | collective-permute-done | bytes 286752 | tf_op jit(solution)/shard_map/ppermute | solution.py:258
  106.2 20.8 %collective-permute-done.11.refs_1_ = bf16[4,224,640]{2,1,0:T(8,128)(2,1)S(1)} collective-permute-done((bf16[4,224,640]{2,1,0:T(8,128)(2,1)S(1)}, bf16[4,224,640]{2,1,0:T(8,128)(2,1)S(1)}, u32[]{:S(2)}, u32[]{:S(2)}) %collective-permute-start.11) | collective-permute-done | bytes 1146912 | tf_op jit(solution)/shard_map/ppermute | solution.py:258
  146.3 10.8 %collective-permute-done.14.refs_2_ = bf16[192,768]{1,0:T(8,128)(2,1)} collective-permute-done((bf16[192,768]{1,0:T(8,128)(2,1)S(1)}, bf16[192,768]{1,0:T(8,128)(2,1)}, u32[]{:S(2)}, u32[]{:S(2)}) %collective-permute-start.14) | collective-permute-done | bytes 294944 | tf_op jit(solution)/shard_map/ppermute | solution.py:258
  157.1 22.0 %collective-permute-done.17.refs_2_ = bf16[96,1536]{1,0:T(8,128)(2,1)} collective-permute-done((bf16[96,1536]{1,0:T(8,128)(2,1)S(1)}, bf16[96,1536]{1,0:T(8,128)(2,1)}, u32[]{:S(2)}, u32[]{:S(2)}) %collective-permute-start.17) | collective-permute-done | bytes 294944 | tf_op jit(solution)/shard_map/ppermute | solution.py:258
  183.6 11.1 %shard_map.465 = (bf16[1024,384]{1,0:T(8,128)(2,1)S(1)}, f32[1024,2]{1,0:T(8,128)S(1)}) custom-call(bf16[1024,128]{1,0:T(8,128)(2,1)S(1)} %copy-done.24, bf16[1024,128]{1,0:T(8,128)(2,1)S(1)} %copy-done.22, bf16[1024,384]{1,0:T(8,128)(2,1)S(1)} %slice.427.v_ref, bf16[1024,64]{1,0:T(8,128)(2,1)S(1)} %copy-done.26, bf16[32,2048]{1,0:T(8,128)(2,1)S(1)} %copy-done.28), custom_call_target="tpu_custom_call" | custom-call | flops 24159191040 | bytes 4194304 | tf_op jit(solution)/shard_map/pallas_call | solution.py:204
  215.7 12.5 %collective-permute-done.25.refs_1_ = bf16[4,96,1536]{2,1,0:T(8,128)(2,1)} collective-permute-done((bf16[4,96,1536]{2,1,0:T(8,128)(2,1)}, bf16[4,96,1536]{2,1,0:T(8,128)(2,1)}, u32[]{:S(2)}, u32[]{:S(2)}) %collective-permute-start.25) | collective-permute-done | bytes 1179680 | tf_op jit(solution)/shard_map/ppermute | solution.py:258
  228.1 26.3 %collective-permute-done.24.refs_1_ = bf16[4,192,768]{2,1,0:T(8,128)(2,1)} collective-permute-done((bf16[4,192,768]{2,1,0:T(8,128)(2,1)}, bf16[4,192,768]{2,1,0:T(8,128)(2,1)}, u32[]{:S(2)}, u32[]{:S(2)}) %collective-permute-start.24) | collective-permute-done | bytes 1179680 | tf_op jit(solution)/shard_map/ppermute | solution.py:258
  283.4 26.6 %collective-permute-done.28 = bf16[256,1536]{1,0:T(8,128)(2,1)S(1)} collective-permute-done((bf16[256,1536]{1,0:T(8,128)(2,1)}, bf16[256,1536]{1,0:T(8,128)(2,1)S(1)}, u32[]{:S(2)}, u32[]{:S(2)}) %collective-permute-start.28) | collective-permute-done | bytes 786464 | tf_op jit(solution)/shard_map/ppermute | solution.py:258
  313.0 8.1 %fusion.118 = (bf16[32,48,1536]{2,1,0:T(8,128)(2,1)}, bf16[32,48,1536]{2,1,0:T(8,128)(2,1)}) fusion(bf16[32,136,1536]{2,1,0:T(8,128)(2,1)} %bitcast.504), kind=kLoop, calls=%fused_computation.401 | loop fusion | bytes 18874368 | tf_op jit(solution)/shard_map/slice | solution.py:702
  321.1 9.0 %fusion.130 = (bf16[512,1536]{1,0:T(8,128)(2,1)}, f32[512,1536]{1,0:T(8,128)}) fusion(f32[512,1536]{1,0:T(8,128)} %convolution_add_fusion.1, bf16[1536,1536]{1,0:T(8,128)(2,1)} %bitcast.515, bf16[256,1536]{1,0:T(8,128)(2,1)S(1)} %fusion.36, s32[512]{0:T(512)S(1)} %add_select_fusion), kind=kOutput, calls=%fused_computation.413 | convolution fusion | flops 2821062656 | bytes 13371392 | tf_op jit(solution)/shard_map/dot_general | solution.py:67
  346.6 15.7 %fusion.112 = (f32[2608]{0:T(1024)S(1)}, f32[]{:T(128)}, f32[512,2608]{0,1:T(8,128)}) fusion(f32[2608]{0:T(1024)S(1)} %convert_element_type.577, s32[1,512,2608]{1,2,0:T(8,128)} %param.28, bf16[512,1536]{1,0:T(8,128)(2,1)} %add_convert_fusion.7, bf16[1536,2608]{1,0:T(8,128)(2,1)} %all-gather.7.cloned.1.call-done), kind=kOutput, calls=%fused_computation.397 | convolution fusion | flops 4116715008 | bytes 20287876 | tf_op jit(solution)/shard_map/dot_general | solution.py:67
  362.3 11.2 %all-reduce.1 = (f32[2608]{0:T(1024)S(1)}, f32[2608]{0:T(1024)S(1)}) all-reduce(f32[2608]{0:T(1024)S(1)} %get-tuple-element.396, f32[2608]{0:T(1024)S(1)} %convert_reduce_fusion.2), channel_id=1, replica_groups=mesh['win'=8,'seq'=4] {'seq'}, use_global_device_ids=true, to_apply=%region_7.8 | all-reduce | flops 5216 | bytes 41728 | tf_op jit(solution)/shard_map/psum | solution.py:755
  374.1 7.9 %convert_reduce_fusion.1 = (f32[2608]{0:T(1024)S(1)}, bf16[512,2608]{0,1:T(8,128)(2,1)S(1)}) fusion(f32[2608]{0:T(1024)S(1)} %get-tuple-element.546, f32[512,2608]{0,1:T(8,128)} %get-tuple-element.582, f32[2608]{0:T(1024)S(1)} %convert_element_type.577, s32[1,512,2608]{1,2,0:T(8,128)} %param.28), kind=kLoop, calls=%fused_computation.20 | loop fusion | flops 24032720 | bytes 13384256 | tf_op jit(solution)/shard_map/reduce_sum | solution.py:767
  389.6 9.1 %convert_reduce_fusion.5 = (f32[1536]{0:T(1024)S(1)}, bf16[512,1536]{1,0:T(8,128)(2,1)S(1)}) fusion(bf16[512,2608]{0,1:T(8,128)(2,1)} %copy-done.46, bf16[1536,2608]{1,0:T(8,128)(2,1)} %all-gather.7.cloned.1.call-done), kind=kOutput, calls=%fused_computation.60 | convolution fusion | flops 4104387072 | bytes 12261376 | tf_op jit(solution)/shard_map/dot_general | solution.py:77
  420.6 9.5 %collective-permute-done.34 = bf16[2,96,1408]{2,1,0:T(8,128)(2,1)S(1)} collective-permute-done((bf16[2,96,1408]{2,1,0:T(8,128)(2,1)S(1)}, bf16[2,96,1408]{2,1,0:T(8,128)(2,1)S(1)}, u32[]{:S(2)}, u32[]{:S(2)}) %collective-permute-start.34) | collective-permute-done | bytes 540704 | tf_op jit(solution)/shard_map/ppermute | solution.py:258
  440.8 8.7 %collective-permute-done.38.refs_2_ = bf16[256,1536]{1,0:T(8,128)(2,1)S(1)} collective-permute-done((bf16[256,1536]{1,0:T(8,128)(2,1)S(1)}, bf16[256,1536]{1,0:T(8,128)(2,1)S(1)}, u32[]{:S(2)}, u32[]{:S(2)}) %collective-permute-start.38) | collective-permute-done | bytes 786464 | tf_op jit(solution)/shard_map/ppermute | solution.py:258
  480.9 10.8 %collective-permute-done.49 = f32[2609]{0:T(1024)S(1)} collective-permute-done((f32[2609]{0:T(1024)S(1)}, f32[2609]{0:T(1024)S(1)}, u32[]{:S(2)}, u32[]{:S(2)}) %collective-permute-start.49) | collective-permute-done | bytes 10468 | tf_op jit(solution)/shard_map/ppermute | solution.py:258
  491.7 6.4 collective-permute-done.47
  508.7 13.2 %collective-permute-done.50 = bf16[256,1536]{1,0:T(8,128)(2,1)S(1)} collective-permute-done((bf16[256,1536]{1,0:T(8,128)(2,1)S(1)}, bf16[256,1536]{1,0:T(8,128)(2,1)S(1)}, u32[]{:S(2)}, u32[]{:S(2)}) %collective-permute-start.50) | collective-permute-done | bytes 786464 | tf_op jit(solution)/shard_map/ppermute | solution.py:258
  536.1 10.4 %collective-permute-done.53 = bf16[96,1408]{1,0:T(8,128)(2,1)S(1)} collective-permute-done((bf16[96,1408]{1,0:T(8,128)(2,1)S(1)}, bf16[96,1408]{1,0:T(8,128)(2,1)S(1)}, u32[]{:S(2)}, u32[]{:S(2)}) %collective-permute-start.53) | collective-permute-done | bytes 270368 | tf_op jit(solution)/shard_map/ppermute | solution.py:258
  546.8 8.1 %collective-permute-done.52 = bf16[96,1408]{1,0:T(8,128)(2,1)S(1)} collective-permute-done((bf16[96,1408]{1,0:T(8,128)(2,1)S(1)}, bf16[96,1408]{1,0:T(8,128)(2,1)S(1)}, u32[]{:S(2)}, u32[]{:S(2)}) %collective-permute-start.52) | collective-permute-done | bytes 270368 | tf_op jit(solution)/shard_map/ppermute | solution.py:258
  559.4 30.3 %collective-permute-done.57 = bf16[4,96,1536]{2,1,0:T(8,128)(2,1)S(1)} collective-permute-done((bf16[4,96,1536]{2,1,0:T(8,128)(2,1)S(1)}, bf16[4,96,1536]{2,1,0:T(8,128)(2,1)S(1)}, u32[]{:S(2)}, u32[]{:S(2)}) %collective-permute-start.57) | collective-permute-done | bytes 1179680 | tf_op jit(solution)/shard_map/ppermute | solution.py:258
  603.7 17.2 %shard_map.474 = (bf16[1024,128]{1,0:T(8,128)(2,1)S(1)}, bf16[1024,64]{1,0:T(8,128)(2,1)S(1)}, bf16[1024,128]{1,0:T(8,128)(2,1)S(1)}, bf16[1024,384]{1,0:T(8,128)(2,1)S(1)}) custom-call(bf16[1024,128]{1,0:T(8,128)(2,1)S(1)} %copy-done.25, bf16[1024,128]{1,0:T(8,128)(2,1)S(1)} %copy-done.23, bf16[1024,384]{1,0:T(8,128)(2,1)S(1)} %copy-done.18, ...), custom_call_target="tpu_custom_call" | custom-call | flops 36238786560 | bytes 6291456 | tf_op jit(solution)/shard_map/pallas_call | solution.py:232
  623.0 20.9 %collective-permute-done.66 = bf16[96,1536]{1,0:T(8,128)(2,1)S(1)} collective-permute-done((bf16[96,1536]{1,0:T(8,128)(2,1)S(1)}, bf16[96,1536]{1,0:T(8,128)(2,1)S(1)}, u32[]{:S(2)}, u32[]{:S(2)}) %collective-permute-start.66) | collective-permute-done | bytes 294944 | tf_op jit(solution)/shard_map/ppermute | solution.py:258
  647.1 5.2 collective-permute-done.68
  652.8 8.7 %collective-permute-done.71 = bf16[272,768]{1,0:T(8,128)(2,1)S(1)} collective-permute-done((bf16[272,768]{1,0:T(8,128)(2,1)S(1)}, bf16[272,768]{1,0:T(8,128)(2,1)S(1)}, u32[]{:S(2)}, u32[]{:S(2)}) %collective-permute-start.71) | collective-permute-done | bytes 417824 | tf_op jit(solution)/shard_map/ppermute | solution.py:258
  699.5 4.7 collective-permute-done.74
  726.3 7.5 collective-permute-done.86
  749.3 5.8 collective-permute-done.84
  755.1 13.8 %collective-permute-done.83 = bf16[224,640]{1,0:T(8,128)(2,1)S(1)} collective-permute-done((bf16[224,640]{1,0:T(8,128)(2,1)S(1)}, bf16[224,640]{1,0:T(8,128)(2,1)S(1)}, u32[]{:S(2)}, u32[]{:S(2)}) %collective-permute-start.83) | collective-permute-done | bytes 286752 | tf_op jit(solution)/shard_map/ppermute | solution.py:258
  (619 shorter events, 345.2 us)
Async XLA Ops:
  7.3 203.1 %all-gather.5.cloned.1.call-start = ((), (), s32[]{:S(2)}) async-start(), calls=%async_computation | async-start | bytes 4866048 | tf_op jit(solution)/shard_map/all_gather | solution.py:681
  8.0 268.5 %all-gather.9.cloned.1.call-start = ((), (), s32[]{:S(2)}) async-start(), calls=%async_computation.2 | async-start | bytes 13787136 | tf_op jit(solution)/shard_map/all_gather | solution.py:686
  29.3 317.3 %all-gather.7.cloned.1.call-start = ((), (), s32[]{:S(2)}) async-start(), calls=%async_computation.1 | async-start | bytes 8515584 | tf_op jit(solution)/shard_map/all_gather | solution.py:691
  29.3 67.3 %collective-permute-start.10 = (bf16[256,1536]{1,0:T(8,128)(2,1)S(1)}, bf16[256,1536]{1,0:T(8,128)(2,1)S(1)}, u32[]{:S(2)}, u32[]{:S(2)}) collective-permute-start(bf16[256,1536]{1,0:T(8,128)(2,1)S(1)} %bitcast.480), channel_id=1, source_target_pairs={{0,2},{1,3},{2,0},{3,1},{4,6},{5,7},{6,4},{7,5},{8,10},{9,11},{10,... | collective-permute-start | bytes 2359304 | tf_op jit(solution)/shard_map/ppermute | solution.py:258
  31.2 65.4 %collective-permute-start.9 = (bf16[256,1536]{1,0:T(8,128)(2,1)S(1)}, bf16[256,1536]{1,0:T(8,128)(2,1)}, u32[]{:S(2)}, u32[]{:S(2)}) collective-permute-start(bf16[256,1536]{1,0:T(8,128)(2,1)S(1)} %bitcast.481), channel_id=1, source_target_pairs={{0,1},{1,0},{2,3},{3,2},{4,5},{5,4},{6,7},{7,6},{8,9},{9,8},{10,11... | collective-permute-start | bytes 2359304 | tf_op jit(solution)/shard_map/ppermute | solution.py:258
  58.5 38.1 %collective-permute-start.4 = (bf16[224,640]{1,0:T(8,128)(2,1)S(1)}, bf16[224,640]{1,0:T(8,128)(2,1)S(1)}, u32[]{:S(2)}, u32[]{:S(2)}) collective-permute-start(bf16[224,640]{1,0:T(8,128)(2,1)S(1)} %bitcast.498), channel_id=1, source_target_pairs={{0,16},{4,20},{8,24},{12,28},{16,0},{20,4},{24,8},{28,12},{1,17},{... | collective-permute-start | bytes 860168 | tf_op jit(solution)/shard_map/ppermute | solution.py:258
  59.3 37.3 %collective-permute-start.3 = (bf16[224,640]{1,0:T(8,128)(2,1)S(1)}, bf16[224,640]{1,0:T(8,128)(2,1)S(1)}, u32[]{:S(2)}, u32[]{:S(2)}) collective-permute-start(bf16[224,640]{1,0:T(8,128)(2,1)S(1)} %bitcast.499), channel_id=1, source_target_pairs={{0,8},{4,12},{8,0},{12,4},{16,24},{20,28},{24,16},{28,20},{1,9},{5... | collective-permute-start | bytes 860168 | tf_op jit(solution)/shard_map/ppermute | solution.py:258
  99.2 41.2 %collective-permute-start.15 = (bf16[192,768]{1,0:T(8,128)(2,1)S(1)}, bf16[192,768]{1,0:T(8,128)(2,1)}, u32[]{:S(2)}, u32[]{:S(2)}) collective-permute-start(bf16[192,768]{1,0:T(8,128)(2,1)S(1)} %bitcast.493), channel_id=1, source_target_pairs={{0,24},{4,28},{8,16},{12,20},{16,8},{20,12},{24,0},{28,4},{1,25},{... | collective-permute-start | bytes 884744 | tf_op jit(solution)/shard_map/ppermute | solution.py:258
  101.7 55.3 %collective-permute-start.14 = (bf16[192,768]{1,0:T(8,128)(2,1)S(1)}, bf16[192,768]{1,0:T(8,128)(2,1)}, u32[]{:S(2)}, u32[]{:S(2)}) collective-permute-start(bf16[192,768]{1,0:T(8,128)(2,1)S(1)} %bitcast.494), channel_id=1, source_target_pairs={{0,16},{4,20},{8,24},{12,28},{16,0},{20,4},{24,8},{28,12},{1,17},{... | collective-permute-start | bytes 884744 | tf_op jit(solution)/shard_map/ppermute | solution.py:258
  101.7 55.3 %collective-permute-start.13 = (bf16[192,768]{1,0:T(8,128)(2,1)S(1)}, bf16[192,768]{1,0:T(8,128)(2,1)}, u32[]{:S(2)}, u32[]{:S(2)}) collective-permute-start(bf16[192,768]{1,0:T(8,128)(2,1)S(1)} %bitcast.495), channel_id=1, source_target_pairs={{0,8},{4,12},{8,0},{12,4},{16,24},{20,28},{24,16},{28,20},{1,9},{5... | collective-permute-start | bytes 884744 | tf_op jit(solution)/shard_map/ppermute | solution.py:258
  103.7 53.4 %collective-permute-start.18 = (bf16[96,1536]{1,0:T(8,128)(2,1)S(1)}, bf16[96,1536]{1,0:T(8,128)(2,1)}, u32[]{:S(2)}, u32[]{:S(2)}) collective-permute-start(bf16[96,1536]{1,0:T(8,128)(2,1)S(1)} %copy-done.19), channel_id=1, source_target_pairs={{0,24},{4,28},{8,16},{12,20},{16,8},{20,12},{24,0},{28,4},{1,25},{... | collective-permute-start | bytes 884744 | tf_op jit(solution)/shard_map/ppermute | solution.py:258
  127.0 52.0 %collective-permute-start.17 = (bf16[96,1536]{1,0:T(8,128)(2,1)S(1)}, bf16[96,1536]{1,0:T(8,128)(2,1)}, u32[]{:S(2)}, u32[]{:S(2)}) collective-permute-start(bf16[96,1536]{1,0:T(8,128)(2,1)S(1)} %copy-done.19), channel_id=1, source_target_pairs={{0,16},{4,20},{8,24},{12,28},{16,0},{20,4},{24,8},{28,12},{1,17},{... | collective-permute-start | bytes 884744 | tf_op jit(solution)/shard_map/ppermute | solution.py:258
  140.4 38.7 %collective-permute-start.16 = (bf16[96,1536]{1,0:T(8,128)(2,1)S(1)}, bf16[96,1536]{1,0:T(8,128)(2,1)S(1)}, u32[]{:S(2)}, u32[]{:S(2)}) collective-permute-start(bf16[96,1536]{1,0:T(8,128)(2,1)S(1)} %copy-done.19), channel_id=1, source_target_pairs={{0,8},{4,12},{8,0},{12,4},{16,24},{20,28},{24,16},{28,20},{1,9},{5... | collective-permute-start | bytes 884744 | tf_op jit(solution)/shard_map/ppermute | solution.py:258
  201.6 52.9 %collective-permute-start.24 = (bf16[4,192,768]{2,1,0:T(8,128)(2,1)}, bf16[4,192,768]{2,1,0:T(8,128)(2,1)}, u32[]{:S(2)}, u32[]{:S(2)}) collective-permute-start(bf16[4,192,768]{2,1,0:T(8,128)(2,1)} %shard_map.467.refs_0_), channel_id=1, source_target_pairs={{0,4},{4,0},{8,12},{12,8},{16,20},{20,16},{24,28},{28,24},{1,5},{5... | collective-permute-start | bytes 3538952 | tf_op jit(solution)/shard_map/ppermute | solution.py:258
  215.2 39.2 %collective-permute-start.23 = (bf16[256,1536]{1,0:T(8,128)(2,1)S(1)}, bf16[256,1536]{1,0:T(8,128)(2,1)}, u32[]{:S(2)}, u32[]{:S(2)}) collective-permute-start(bf16[256,1536]{1,0:T(8,128)(2,1)S(1)} %add_convert_fusion.15.refs_0_), channel_id=1, source_target_pairs={{0,2},{1,3},{2,0},{3,1},{4,6},{5,7},{6,4},{7,5},{8,10},{9,11},{10,... | collective-permute-start | bytes 2359304 | tf_op jit(solution)/shard_map/ppermute | solution.py:258
  215.7 38.8 %collective-permute-start.22 = (bf16[256,1536]{1,0:T(8,128)(2,1)S(1)}, bf16[256,1536]{1,0:T(8,128)(2,1)S(1)}, u32[]{:S(2)}, u32[]{:S(2)}) collective-permute-start(bf16[256,1536]{1,0:T(8,128)(2,1)S(1)} %add_convert_fusion.15.refs_0_), channel_id=1, source_target_pairs={{0,1},{1,0},{2,3},{3,2},{4,5},{5,4},{6,7},{7,6},{8,9},{9,8},{10,11... | collective-permute-start | bytes 2359304 | tf_op jit(solution)/shard_map/ppermute | solution.py:258
  275.2 34.8 %collective-permute-start.28 = (bf16[256,1536]{1,0:T(8,128)(2,1)}, bf16[256,1536]{1,0:T(8,128)(2,1)S(1)}, u32[]{:S(2)}, u32[]{:S(2)}) collective-permute-start(bf16[256,1536]{1,0:T(8,128)(2,1)} %fusion.46), channel_id=1, source_target_pairs={{0,2},{1,3},{2,0},{3,1},{4,6},{5,7},{6,4},{7,5},{8,10},{9,11},{10,... | collective-permute-start | bytes 2359304 | tf_op jit(solution)/shard_map/ppermute | solution.py:258
  389.2 51.6 %collective-permute-start.39 = (f32[2609]{0:T(1024)S(1)}, f32[2609]{0:T(1024)S(1)}, u32[]{:S(2)}, u32[]{:S(2)}) collective-permute-start(f32[2609]{0:T(1024)S(1)} %pad_maximum_fusion.32), channel_id=1, source_target_pairs={{0,1},{1,0},{2,3},{3,2},{4,5},{5,4},{6,7},{7,6},{8,9},{9,8},{10,11... | collective-permute-start | bytes 31316 | tf_op jit(solution)/shard_map/ppermute | solution.py:258
  434.0 41.2 %collective-permute-start.43 = (bf16[4,96,1408]{2,1,0:T(8,128)(2,1)S(1)}, bf16[4,96,1408]{2,1,0:T(8,128)(2,1)}, u32[]{:S(2)}, u32[]{:S(2)}) collective-permute-start(bf16[4,96,1408]{2,1,0:T(8,128)(2,1)S(1)} %pad_maximum_fusion.12), channel_id=1, source_target_pairs={{0,4},{4,0},{8,12},{12,8},{16,20},{20,16},{24,28},{28,24},{1,5},{5... | collective-permute-start | bytes 3244040 | tf_op jit(solution)/shard_map/ppermute | solution.py:258
  525.3 66.4 %collective-permute-start.58 = (bf16[1536,768]{1,0:T(8,128)(2,1)S(1)}, bf16[1536,768]{1,0:T(8,128)(2,1)S(1)}, u32[]{:S(2)}, u32[]{:S(2)}) collective-permute-start(bf16[1536,768]{1,0:T(8,128)(2,1)S(1)} %convolution_convert_fusion.3), channel_id=1, source_target_pairs={{0,1},{1,0},{2,3},{3,2},{4,5},{5,4},{6,7},{7,6},{8,9},{9,8},{10,11... | collective-permute-start | bytes 7077896 | tf_op jit(solution)/shard_map/ppermute | solution.py:258
  525.7 65.2 %collective-permute-start.55 = (bf16[4,272,768]{2,1,0:T(8,128)(2,1)S(1)}, bf16[4,272,768]{2,1,0:T(8,128)(2,1)S(1)}, u32[]{:S(2)}, u32[]{:S(2)}) collective-permute-start(bf16[4,272,768]{2,1,0:T(8,128)(2,1)S(1)} %pad_maximum_fusion.3), channel_id=1, source_target_pairs={{0,4},{4,0},{8,12},{12,8},{16,20},{20,16},{24,28},{28,24},{1,5},{5... | collective-permute-start | bytes 5013512 | tf_op jit(solution)/shard_map/ppermute | solution.py:258
  526.8 64.2 %collective-permute-start.56 = (bf16[4,272,768]{2,1,0:T(8,128)(2,1)S(1)}, bf16[4,272,768]{2,1,0:T(8,128)(2,1)S(1)}, u32[]{:S(2)}, u32[]{:S(2)}) collective-permute-start(bf16[4,272,768]{2,1,0:T(8,128)(2,1)S(1)} %pad_maximum_fusion.5), channel_id=1, source_target_pairs={{0,2},{1,3},{2,0},{3,1},{4,6},{5,7},{6,4},{7,5},{8,10},{9,11},{10,... | collective-permute-start | bytes 5013512 | tf_op jit(solution)/shard_map/ppermute | solution.py:258
  528.1 61.6 %collective-permute-start.57 = (bf16[4,96,1536]{2,1,0:T(8,128)(2,1)S(1)}, bf16[4,96,1536]{2,1,0:T(8,128)(2,1)S(1)}, u32[]{:S(2)}, u32[]{:S(2)}) collective-permute-start(bf16[4,96,1536]{2,1,0:T(8,128)(2,1)S(1)} %dynamic-slice_bitcast_fusion.1), channel_id=1, source_target_pairs={{0,4},{4,0},{8,12},{12,8},{16,20},{20,16},{24,28},{28,24},{1,5},{5... | collective-permute-start | bytes 3538952 | tf_op jit(solution)/shard_map/ppermute | solution.py:258
  559.4 37.2 %collective-permute-start.62 = (bf16[256,384]{1,0:T(8,128)(2,1)S(1)}, bf16[256,384]{1,0:T(8,128)(2,1)S(1)}, u32[]{:S(2)}, u32[]{:S(2)}) collective-permute-start(bf16[256,384]{1,0:T(8,128)(2,1)S(1)} %get-tuple-element.487), channel_id=1, source_target_pairs={{0,3},{1,2},{2,1},{3,0},{4,7},{5,6},{6,5},{7,4},{8,11},{9,10},{10,... | collective-permute-start | bytes 589832 | tf_op jit(solution)/shard_map/ppermute | solution.py:258
  599.2 44.7 %collective-permute-start.66 = (bf16[96,1536]{1,0:T(8,128)(2,1)S(1)}, bf16[96,1536]{1,0:T(8,128)(2,1)S(1)}, u32[]{:S(2)}, u32[]{:S(2)}) collective-permute-start(bf16[96,1536]{1,0:T(8,128)(2,1)S(1)} %get-tuple-element.475), channel_id=1, source_target_pairs={{0,16},{4,20},{8,24},{12,28},{16,0},{20,4},{24,8},{28,12},{1,17},{... | collective-permute-start | bytes 884744 | tf_op jit(solution)/shard_map/ppermute | solution.py:258
  599.2 45.5 %collective-permute-start.65 = (bf16[96,1536]{1,0:T(8,128)(2,1)S(1)}, bf16[96,1536]{1,0:T(8,128)(2,1)S(1)}, u32[]{:S(2)}, u32[]{:S(2)}) collective-permute-start(bf16[96,1536]{1,0:T(8,128)(2,1)S(1)} %get-tuple-element.476), channel_id=1, source_target_pairs={{0,8},{4,12},{8,0},{12,4},{16,24},{20,28},{24,16},{28,20},{1,9},{5... | collective-permute-start | bytes 884744 | tf_op jit(solution)/shard_map/ppermute | solution.py:258
  601.1 51.7 %collective-permute-start.72 = (bf16[272,768]{1,0:T(8,128)(2,1)S(1)}, bf16[272,768]{1,0:T(8,128)(2,1)S(1)}, u32[]{:S(2)}, u32[]{:S(2)}) collective-permute-start(bf16[272,768]{1,0:T(8,128)(2,1)S(1)} %get-tuple-element.462), channel_id=1, source_target_pairs={{0,24},{4,28},{8,16},{12,20},{16,8},{20,12},{24,0},{28,4},{1,25},{... | collective-permute-start | bytes 1253384 | tf_op jit(solution)/shard_map/ppermute | solution.py:258
  620.9 40.5 %collective-permute-start.71 = (bf16[272,768]{1,0:T(8,128)(2,1)S(1)}, bf16[272,768]{1,0:T(8,128)(2,1)S(1)}, u32[]{:S(2)}, u32[]{:S(2)}) collective-permute-start(bf16[272,768]{1,0:T(8,128)(2,1)S(1)} %get-tuple-element.463), channel_id=1, source_target_pairs={{0,16},{4,20},{8,24},{12,28},{16,0},{20,4},{24,8},{28,12},{1,17},{... | collective-permute-start | bytes 1253384 | tf_op jit(solution)/shard_map/ppermute | solution.py:258
  621.9 39.6 %collective-permute-start.70 = (bf16[272,768]{1,0:T(8,128)(2,1)S(1)}, bf16[272,768]{1,0:T(8,128)(2,1)S(1)}, u32[]{:S(2)}, u32[]{:S(2)}) collective-permute-start(bf16[272,768]{1,0:T(8,128)(2,1)S(1)} %get-tuple-element.464), channel_id=1, source_target_pairs={{0,8},{4,12},{8,0},{12,4},{16,24},{20,28},{24,16},{28,20},{1,9},{5... | collective-permute-start | bytes 1253384 | tf_op jit(solution)/shard_map/ppermute | solution.py:258
  662.9 41.8 %collective-permute-start.77 = (bf16[4,96,768]{2,1,0:T(8,128)(2,1)}, bf16[4,96,768]{2,1,0:T(8,128)(2,1)}, u32[]{:S(2)}, u32[]{:S(2)}) collective-permute-start(bf16[4,96,768]{2,1,0:T(8,128)(2,1)} %pad_maximum_fusion.15), channel_id=1, source_target_pairs={{0,4},{4,0},{8,12},{12,8},{16,20},{20,16},{24,28},{28,24},{1,5},{5... | collective-permute-start | bytes 1769480 | tf_op jit(solution)/shard_map/ppermute | solution.py:258
  665.4 39.4 %collective-permute-start.78 = (bf16[4,96,768]{2,1,0:T(8,128)(2,1)}, bf16[4,96,768]{2,1,0:T(8,128)(2,1)}, u32[]{:S(2)}, u32[]{:S(2)}) collective-permute-start(bf16[4,96,768]{2,1,0:T(8,128)(2,1)} %pad_maximum_fusion.16), channel_id=1, source_target_pairs={{0,2},{1,3},{2,0},{3,1},{4,6},{5,7},{6,4},{7,5},{8,10},{9,11},{10,... | collective-permute-start | bytes 1769480 | tf_op jit(solution)/shard_map/ppermute | solution.py:258
  704.2 31.9 %collective-permute-start.81 = (bf16[4,224,640]{2,1,0:T(8,128)(2,1)}, bf16[4,224,640]{2,1,0:T(8,128)(2,1)}, u32[]{:S(2)}, u32[]{:S(2)}) collective-permute-start(bf16[4,224,640]{2,1,0:T(8,128)(2,1)} %dynamic-slice_bitcast_fusion.2), channel_id=1, source_target_pairs={{0,4},{4,0},{8,12},{12,8},{16,20},{20,16},{24,28},{28,24},{1,5},{5... | collective-permute-start | bytes 3440648 | tf_op jit(solution)/shard_map/ppermute | solution.py:258
  (178 other events, 2645.8 us)
Sparse Core Ops, SparseCore 0:
  11.0 82.5 all-gather.4
  97.0 129.1 all-gather.8
  229.1 93.1 all-gather.6

commit v2 on v1

--- a/solution.py
+++ b/solution.py
@@ -215,9 +215,7 @@
         out_shape=[out, norm],
         compiler_params=pltpu.CompilerParams(vmem_limit_bytes=40 * 2**20),
         cost_estimate=pl.CostEstimate(
-            flops=40 * rows * keys * heads * (KEY + BASIS + VAL),
-            transcendentals=rows * keys * heads,
-            bytes_accessed=4 * 2**20,
+            flops=10**10, transcendentals=rows * keys * heads, bytes_accessed=4 * 2**20
         ),
     )(query, key, value, pos_query, table)
 
@@ -246,9 +244,7 @@
         scratch_shapes=[pltpu.VMEM(key.shape, F32), pltpu.VMEM(value.shape, F32)],
         compiler_params=pltpu.CompilerParams(vmem_limit_bytes=40 * 2**20),
         cost_estimate=pl.CostEstimate(
-            flops=60 * rows * keys * heads * (KEY + BASIS + VAL),
-            transcendentals=rows * keys * heads,
-            bytes_accessed=6 * 2**20,
+            flops=15 * 10**9, transcendentals=rows * keys * heads, bytes_accessed=6 * 2**20
         ),
     )(query, key, value, pos_query, table, norm, grad)
 
@@ -297,11 +293,7 @@
         functools.partial(place_kernel, axis, shift, inner, columns),
         out_shape=jax.ShapeDtypeStruct(shape, pieces[0].dtype),
         compiler_params=pltpu.CompilerParams(vmem_limit_bytes=24 * 2**20),
-        cost_estimate=pl.CostEstimate(
-            flops=0,
-            transcendentals=0,
-            bytes_accessed=2 * count * pieces[0].size * pieces[0].dtype.itemsize,
-        ),
+        cost_estimate=pl.CostEstimate(flops=0, transcendentals=0, bytes_accessed=1024),
     )(*pieces)
 
 
@@ -325,7 +317,7 @@
 
 
 def advance(values, *flows):
-    values, arrived = tie((values, [flow.pending for flow in flows]))
+    values, arrived = tie((tie(values), [flow.pending for flow in flows]))
     for flow, rows in zip(flows, arrived):
         flow.step(rows)
     return values
@@ -348,6 +340,12 @@
 def seq_swap(blocks, rank):
     got = yield [trade(pick(blocks, rank ^ k), SEQ, k) for k in range(1, RANKS)]
     return [pick(blocks, rank)] + got
+
+
+def seq_swap_two(blocks, rank):
+    far = yield trade(jnp.stack([pick(blocks, rank ^ 2), pick(blocks, rank ^ 3)]), SEQ, 2)
+    near = yield trade(jnp.stack([pick(blocks, rank ^ 1), far[1]]), SEQ, 1)
+    return [pick(blocks, rank), near[0], far[0], near[1]]
 
 
 def deal_kernel(parts, whole_ref, dealt_ref):
@@ -416,16 +414,16 @@
     out_ref[...] = jnp.zeros_like(out_ref)
     for name, ref in zip(names, refs):
         low, high = SHORT[name]
-        out_ref[0:1, low:high] = ref[...]
+        out_ref[0:1, low:high] = ref[...].astype(F32)
     for b in range(BASIS):
-        out_ref[1:2, b * REL : (b + 1) * REL] = refs[-2][b : b + 1, :]
+        out_ref[1:2, b * REL : (b + 1) * REL] = refs[-2][b : b + 1, :].astype(F32)
 
 
 def pack(rows, rel):
     return pl.pallas_call(
         functools.partial(pack_kernel, tuple(rows)),
         out_shape=jax.ShapeDtypeStruct((EXTRA, ROOM), F32),
-    )(*(row.astype(F32)[None] for row in rows.values()), rel.astype(F32))
+    )(*(row[None] for row in rows.values()), rel)
 
 
 WIDE = ("gain1", "bias1", "gain2", "bias2", "b_hid", "m", "p", "d0", "d1", "d2")
@@ -534,76 +532,103 @@
     return both.reshape((WINDOWS,) + block.shape)
 
 
-def win_sum(parts, window):
-    z, y = window // 2, window % 2
-    parts = parts.reshape((WINDOWS // 2, 2) + parts.shape[1:])
-    sent = lax.dynamic_index_in_dim(parts, 1 - y, 1, keepdims=False)
-    kept = lax.dynamic_index_in_dim(parts, y, 1, keepdims=False)
+def z_sum(column, z):
+    got = yield trade(jnp.stack([pick(column, z ^ 1), pick(column, z ^ 3)]), WIN, 2)
+    last = yield trade(plus(pick(column, z ^ 2), got[1]), WIN, 4)
+    return pick(column, z).astype(F32) + got[0].astype(F32) + last.astype(F32)
+
+
+def win_sum(kept, sent, window):
     got = yield trade(sent, WIN, 1)
-    column = (kept.astype(F32) + got.astype(F32)).astype(LOW)
-    got = yield [trade(pick(column, z ^ k), WIN, 2 * k) for k in range(1, WINDOWS // 2)]
-    total = pick(column, z).astype(F32)
-    for piece in got:
-        total = total + piece.astype(F32)
+    total = yield from z_sum(plus(kept, got), window // 2)
     return total
 
 
 def shared_sum(row):
-    for axis, bits in ((SEQ, 1), (SEQ, 2), (WIN, 1), (WIN, 2), (WIN, 4)):
+    for axis, bits in ((WIN, 1), (WIN, 2), (WIN, 4), (SEQ, 1), (SEQ, 2)):
         got = yield trade(row, axis, bits)
         row = row + got
     return row
 
 
-def core_sum(first_arg, second_arg, rank):
-    core = rank % 2
-    half = second_arg.shape[1] // 2
-    other = lax.dynamic_slice_in_dim(second_arg, (1 - core) * half, half, 1)
-    mine = lax.dynamic_slice_in_dim(second_arg, core * half, half, 1)
-    got = yield trade(weight_product(first_arg, other).astype(LOW), SEQ, 1)
-    total = (weight_product(first_arg, mine) + got.astype(F32)).astype(LOW)
-    return total.reshape(4, 2, 2, total.shape[0] // 16, half)
-
-
-def chip_sum(grads, rank, window):
+def split_kernel(axis, height, first_ref, second_ref, kept_ref, sent_ref):
+    grads = weight_product(first_ref[...], second_ref[...]).astype(LOW)
+    odd = lax.axis_index(axis) % 2
+    for pair in range(kept_ref.shape[0]):
+        low = 2 * pair * height
+        even_rows = grads[low : low + height]
+        odd_rows = grads[low + height : low + 2 * height]
+
+        @pl.when(odd == 0)
+        def _():
+            kept_ref[pair] = even_rows
+            sent_ref[pair] = odd_rows
+
+        @pl.when(odd == 1)
+        def _():
+            kept_ref[pair] = odd_rows
+            sent_ref[pair] = even_rows
+
+
+def split_product(first_arg, second_arg, axis, height):
+    depth, rows = first_arg.shape
+    columns = second_arg.shape[1]
+    width = 384 if rows % 384 == 0 else 640
+    pairs = width // (2 * height)
+    out = jax.ShapeDtypeStruct((rows // (2 * height), height, columns), LOW)
+    out_spec = pl.BlockSpec((pairs, height, columns), lambda i: (i, 0, 0))
+    return pl.pallas_call(
+        functools.partial(split_kernel, axis, height),
+        grid=(rows // width,),
+        in_specs=[pl.BlockSpec((depth, width), lambda i: (0, i)), whole_spec(second_arg)],
+        out_specs=[out_spec, out_spec],
+        out_shape=[out, out],
+        compiler_params=pltpu.CompilerParams(vmem_limit_bytes=32 * 2**20),
+        cost_estimate=pl.CostEstimate(
+            flops=2 * depth * rows * columns,
+            transcendentals=0,
+            bytes_accessed=2 * (depth * rows + depth * columns + rows * columns),
+        ),
+    )(first_arg, second_arg)
+
+
+def core_sum(first_arg, second_arg):
+    height = first_arg.shape[1] // DEVICES
+    kept, sent = split_product(first_arg, second_arg, SEQ, height)
+    got = yield trade(sent, SEQ, 1)
+    return plus(kept, got).reshape((4, 2, 2) + kept.shape[1:])
+
+
+def plus(first_arg, *others):
+    total = first_arg.astype(F32)
+    for other in others:
+        total = total + other.astype(F32)
+    return total.astype(LOW)
+
+
+def chip_sum(grads, rank, window, y_first):
     z, y = window // 2, window % 2
-    x, core = rank // 2, rank % 2
-
-    def at(yy, xx):
-        cut = [
-            lax.dynamic_slice(g, (0, yy, xx, 0, 0), (4, 1, 1) + g.shape[3:]).reshape(
-                (4,) + g.shape[3:]
-            )
-            for g in grads
-        ]
-        return cut[0] if len(cut) == 1 else jnp.concatenate(cut, axis=1)
-
-    def plus(a, b):
-        return (a.astype(F32) + b.astype(F32)).astype(LOW)
-
-    corner = at(1 - y, 1 - x)
-    by_x, by_y = yield trade(corner[:2], SEQ, 2), trade(corner[2:], WIN, 1)
-    over_y, over_x = at(1 - y, x), at(y, 1 - x)
-    over_y = jnp.concatenate([plus(over_y[:2], by_x), over_y[2:]])
-    over_x = jnp.concatenate([over_x[:2], plus(over_x[2:], by_y)])
-    from_y, from_x = yield trade(over_y, WIN, 1), trade(over_x, SEQ, 2)
-    own = (at(y, x).astype(F32) + from_y.astype(F32) + from_x.astype(F32)).astype(LOW)
-    got = yield [trade(pick(own, z ^ k), WIN, 2 * k) for k in range(1, 4)]
-    total = pick(own, z).astype(F32)
-    for piece in got:
-        total = total + piece.astype(F32)
-    parts, first = [], 0
-    for g in grads:
-        rows, half = g.shape[3] // 2, g.shape[4]
-        block = total[first : first + 2 * rows].reshape(2, rows, half)
-        first += 2 * rows
-        parts.append((pick(block, core), pick(block, 1 - core)))
-    got = yield trade(jnp.concatenate([sent for _, sent in parts], axis=0), SEQ, 1)
-    results, first = [], 0
-    for kept, sent in parts:
-        piece = got[first : first + sent.shape[0]]
-        first += sent.shape[0]
-        results.append(jnp.concatenate(in_order([kept, piece], core), axis=1))
+    x = rank // 2
+    heights = [g.shape[3] for g in grads]
+
+    def half(index):
+        axis = 1 if y_first else 2
+        cut = [lax.dynamic_index_in_dim(g, index, axis, keepdims=False) for g in grads]
+        return cut[0] if len(cut) == 1 else jnp.concatenate(cut, axis=2)
+
+    def quarter(both, index):
+        return lax.dynamic_index_in_dim(both, index, 1, keepdims=False)
+
+    first, second = (y, x) if y_first else (x, y)
+    steps = ((WIN, 1), (SEQ, 2)) if y_first else ((SEQ, 2), (WIN, 1))
+    got = yield trade(half(1 - first), *steps[0])
+    both = plus(half(first), got)
+    got = yield trade(quarter(both, 1 - second), *steps[1])
+    total = yield from z_sum(plus(quarter(both, second), got), z)
+    results, low = [], 0
+    for height in heights:
+        results.append(total[low : low + height])
+        low += height
     return results
 
 
@@ -675,31 +700,31 @@
             for t in range(RANKS)
         ]
     )
-    inputs_own = inputs.reshape(ROWS, D)
     qkv_flow = Flow(seq_swap(qkv_local, rank))
+    four = lax.all_gather(jnp.concatenate([w_out, w_up, w_skip, w_point]), BOTH, axis=0)
+    inputs_own, w_in, w_hid = advance((inputs.reshape(ROWS, D), w_in, w_hid), qkv_flow)
+    qkv_flow = Flow(win_all(place(qkv_flow.result, SEQ).reshape(-1, ROOM)))
     inputs_flow = Flow(seq_all(inputs_own))
-    out_full = lax.all_gather(w_out, BOTH, axis=0, tiled=True)
-    late_local = jnp.concatenate([w_up, w_skip, w_point])
-    w_in, late_local = advance((w_in, late_local), qkv_flow)
-    qkv_flow = Flow(win_all(place(qkv_flow.result, SEQ).reshape(-1, ROOM)))
-    in_flow = Flow(seq_swap(deal(w_in, WINDOWS), rank))
-    late_full = lax.all_gather(late_local, BOTH, axis=0)
-    w_hid = advance(w_hid, qkv_flow, in_flow, inputs_flow)
-    in_flow = Flow(win_all(place(in_flow.result, SEQ).reshape(-1, ff)))
+    dealt, w_hid, w_head = advance((deal(w_in, WINDOWS), w_hid, w_head), qkv_flow, inputs_flow)
+    in_flow = Flow(seq_swap(dealt, rank))
     hid_flow = Flow(win_all(w_hid))
-    w_head = advance(w_head, qkv_flow, inputs_flow)
     head_full = lax.all_gather(w_head, BOTH, axis=0, tiled=True)
+    advance((), qkv_flow, in_flow, inputs_flow)
     gathered = qkv_flow.result.reshape(DEVICES, -1, ROOM)
     height = gathered.shape[1] - EXTRA
     qkv_part = gathered[:, :height].reshape(D, ROOM)
-    inputs_all = inputs_flow.result
-    wide, in_bias, content, position, rel_part = unpack(gathered[:, height:].astype(F32))
+    wide, in_bias, content, position, rel_part, qkv_part, inputs_all, in_rows = advance(
+        (
+            *unpack(gathered[:, height:].astype(F32)),
+            qkv_part,
+            inputs_flow.result,
+            place(in_flow.result, SEQ).reshape(-1, ff),
+        ),
+        hid_flow,
+    )
+    in_flow = Flow(win_all(in_rows))
     row_of = {name: wide[number] for number, name in enumerate(WIDE)}
     depth_full = [row_of[name] for name in ("d0", "d1", "d2")]
-    r_up, r_skip = w_up.shape[0], w_skip.shape[0]
-    up_full = late_full[:, :r_up].reshape(D, D)
-    skip_full = late_full[:, r_up : r_up + r_skip].reshape(CS, D)
-    point_full = late_full[:, r_up + r_skip :].reshape(D, D)
     heads_here = hq // KEY
     same_head = (
         jnp.arange(hq)[:, None] // KEY == jnp.arange(heads_here * BASIS)[None, :] // BASIS
@@ -717,18 +742,25 @@
     keys = projected[:, hq : 2 * hq].astype(LOW)
     values = projected[:, 2 * hq :].astype(LOW)
     offsets = wide_table(seq_len)
-    queries, keys, values, pos_query = advance(
-        (queries, keys, values, pos_query), in_flow, hid_flow
-    )
-    mixed, norms = advance(mix(queries, keys, values, pos_query, offsets))
+    mixed, norms = advance(
+        mix(queries, keys, values, pos_query, offsets), in_flow, hid_flow
+    )
     swap = Flow(seq_swap(mixed.reshape(RANKS, ROWS, hv), rank))
-    advance((), swap)
+    norms = advance(norms, swap)
     attended = place(swap.result, SEQ, columns=True)
+    r_out = w_out.shape[0]
+    out_full = four[:, :r_out].reshape(HV, D)
     inputs_f = inputs_own.astype(F32)
     resid_one = inputs_f + product(attended, out_full)
     normed_flow = Flow(seq_all(layer_norm(resid_one, gain_two, bias_two).astype(LOW)))
-    advance((), normed_flow, in_flow, hid_flow)
+    four = advance(four, normed_flow, in_flow)
     advance((), normed_flow)
+    wholes, low = [], r_out
+    for own in (w_up, w_skip, w_point):
+        high = low + own.shape[0]
+        wholes.append(four[:, low:high].reshape(-1, D))
+        low = high
+    up_full, skip_full, point_full = wholes
     normed_two = normed_flow.result
     in_part = in_flow.result.reshape(D, ff)
     hid_part = hid_flow.result.reshape(ff, D)
@@ -766,23 +798,13 @@
     grad_rows = (grad_rate * jax.nn.sigmoid(logits)).astype(LOW)
     head_bias_part = jnp.sum(grad_rows, axis=0, dtype=F32)
     shared_flow = Flow(shared_sum(jnp.concatenate([head_bias_part, local_loss[None]])))
-    spare = -TRACKS % 256
-    head_core = Flow(core_sum(head_rows, jnp.pad(grad_rows, ((0, 0), (0, spare))), rank))
+    head_core = Flow(core_sum(head_rows, grad_rows))
     grad_out = input_product(grad_rows, head_full).astype(LOW)
-    pbias_grad = jnp.sum(grad_out, axis=0, dtype=F32)
     grad_depth = input_product(grad_out, point_full).astype(LOW)
-    grad_out, grad_depth, pbias_grad = advance((grad_out, grad_depth, pbias_grad), head_core)
+    grad_out, grad_depth = advance((grad_out, grad_depth), head_core, shared_flow)
     depth_flow = Flow(edges(grad_depth, SEQ))
-    head_flow = Flow(chip_sum([head_core.result], rank, window))
-    depth_grad = jnp.stack(
-        [
-            jnp.sum(grad_depth * padded[:-2], axis=0),
-            jnp.sum(grad_depth * padded[1:-1], axis=0),
-            jnp.sum(grad_depth * padded[2:], axis=0),
-        ]
-    )
-    point_core = Flow(core_sum(depth_out, grad_out, rank))
-    grad_out, depth_grad = advance((grad_out, depth_grad), depth_flow)
+    grad_out, grad_depth = advance((grad_out, grad_depth), depth_flow, shared_flow)
+    head_flow = Flow(chip_sum([head_core.result], rank, window, True))
     depth_pad = depth_flow.result
     merged_low = (
         grad_out.astype(F32)
@@ -790,37 +812,48 @@
         + depth_full[1] * depth_pad[1:-1]
         + depth_full[2] * depth_pad[:-2]
     ).astype(LOW)
-    mbias_grad = jnp.sum(merged_low, axis=0, dtype=F32)
     lift_grad = weight_product(twice, merged_low).astype(LOW)
     grad_two = input_product(lift_grad, up_full).astype(LOW)
+    grad_two, merged_low, lift_grad = advance((grad_two, merged_low, lift_grad))
+    two_flow = Flow(seq_all(grad_two))
+    point_core = Flow(core_sum(depth_out, grad_out))
+    skip_grad = input_product(merged_low, skip_full).reshape(1, 2 * ROWS, CS)
+    depth_grad = jnp.stack(
+        [
+            jnp.sum(grad_depth * padded[:-2], axis=0),
+            jnp.sum(grad_depth * padded[1:-1], axis=0),
+            jnp.sum(grad_depth * padded[2:], axis=0),
+        ]
+    )
+    skip_grad, merged_low, grad_two, depth_grad = advance(
+        (skip_grad, merged_low, grad_two, depth_grad), two_flow, point_core, shared_flow
+    )
+    skip_core = Flow(core_sum(skip_rows, merged_low))
+    up_core = Flow(core_sum(lift_in, lift_grad))
+    pbias_grad = jnp.sum(grad_out, axis=0, dtype=F32)
+    mbias_grad = jnp.sum(merged_low, axis=0, dtype=F32)
     hbias_grad = jnp.sum(grad_two, axis=0, dtype=F32)
-    grad_two, merged_low, lift_grad, mbias_grad, hbias_grad = advance(
-        (grad_two, merged_low, lift_grad, mbias_grad, hbias_grad), head_flow, point_core
-    )
-    two_flow = Flow(seq_all(grad_two))
-    skip_core = Flow(core_sum(skip_rows, merged_low, rank))
-    up_core = Flow(core_sum(lift_in, lift_grad, rank))
-    skip_grad = input_product(merged_low, skip_full).reshape(1, 2 * ROWS, CS)
-    skip_grad = advance(skip_grad, skip_core, up_core)
-    tail_flow = Flow(
-        chip_sum([point_core.result, skip_core.result, up_core.result], rank, window)
-    )
-    advance((), two_flow, shared_flow)
-    advance((), two_flow, shared_flow)
+    point_flow = Flow(chip_sum([point_core.result], rank, window, False))
+    pbias_grad, mbias_grad, hbias_grad = advance(
+        (pbias_grad, mbias_grad, hbias_grad), two_flow, skip_core, up_core, shared_flow
+    )
+    up_flow = Flow(chip_sum([up_core.result], rank, window, False))
     grad_two_all = two_flow.result
     grad_hidden = input_product(grad_two_all, hid_part).astype(LOW)
     _, pull_act = jax.vjp(smooth_act, pre_act)
     grad_pre = pull_act(grad_hidden.astype(F32))[0].astype(LOW)
+    pre_flow = Flow(seq_sum(input_product(grad_pre, in_part), rank))
+    hid_parts = split_product(hidden, grad_two_all, WIN, ff // WINDOWS)
+    in_parts = split_product(normed_two, grad_pre, WIN, D // WINDOWS)
+    hid_parts, in_parts, grad_pre, skips_kept = advance(
+        (hid_parts, in_parts, grad_pre, skip_core.result), pre_flow, point_flow, shared_flow
+    )
+    hid_flow = Flow(win_sum(*hid_parts, window))
     ibias_part = jnp.sum(grad_pre, axis=0, dtype=F32)
-    pre_flow = Flow(seq_sum(input_product(grad_pre, in_part), rank))
-    hid_low = weight_product(hidden, grad_two_all).astype(LOW)
-    hid_low, grad_pre, ibias_part = advance(
-        (hid_low, grad_pre, ibias_part), pre_flow, head_flow, tail_flow, shared_flow
-    )
-    hid_flow = Flow(win_sum(hid_low.reshape(WINDOWS, ff // WINDOWS, D), window))
-    in_low = weight_product(normed_two, grad_pre).astype(LOW)
-    in_low = advance(in_low, pre_flow, shared_flow)
-    in_flow = Flow(win_sum(in_low.reshape(WINDOWS, D // WINDOWS, ff), window))
+    ibias_part, in_parts = advance(
+        (ibias_part, in_parts), pre_flow, head_flow, up_flow, point_flow
+    )
+    in_flow = Flow(win_sum(*in_parts, window))
     _, pull_two = jax.vjp(layer_norm, resid_one, gain_two, bias_two)
     grad_resid, gain_two_grad, bias_two_grad = pull_two(pre_flow.result)
     grad_one = (grad_two.astype(F32) + grad_resid).astype(LOW)
@@ -830,24 +863,23 @@
             jnp.stack([grad_att[:, t * hv : (t + 1) * hv] for t in range(RANKS)]), rank
         )
     )
-    out_core = Flow(core_sum(attended, grad_one, rank))
-    grad_one, gain_two_grad, bias_two_grad = advance(
-        (grad_one, gain_two_grad, bias_two_grad),
-        head_flow,
-        tail_flow,
+    grad_one, gain_two_grad, bias_two_grad, skips_kept = advance(
+        (grad_one, gain_two_grad, bias_two_grad, skips_kept), att_flow, hid_flow
+    )
+    out_core = Flow(core_sum(attended, grad_one))
+    grad_att = place(att_flow.result, SEQ).reshape(seq_len, hv)
+    query_low, pos_low, key_grad, value_grad, skips_kept = advance(
+        (
+            *mix_grad(queries, keys, values, pos_query, offsets, norms, grad_att),
+            skips_kept,
+        ),
+        in_flow,
         hid_flow,
         out_core,
-        shared_flow,
-    )
-    out_flow = Flow(chip_sum([out_core.result], rank, window))
-    advance((), att_flow, head_flow)
-    grad_att = place(att_flow.result, SEQ).reshape(seq_len, hv)
-    query_low, pos_low, key_grad, value_grad = mix_grad(
-        queries, keys, values, pos_query, offsets, norms, grad_att
-    )
-    query_low, pos_low, key_grad, value_grad = advance(
-        (query_low, pos_low, key_grad, value_grad), in_flow, hid_flow, out_flow, tail_flow
-    )
+        up_flow,
+        head_flow,
+    )
+    rest_flow = Flow(chip_sum([skips_kept, out_core.result], rank, window, False))
     pos_f = pos_low.astype(F32)
     pos_in_grad = lax.dot_general(
         pos_f, rel_square, (((1,), (1,)), ((), ())), precision=HIGH
@@ -866,7 +898,6 @@
     scale = lax.rsqrt(jnp.mean(centred * centred, axis=-1, keepdims=True) + EPS)
     gain_one_grad = jnp.sum(partial * (centred * scale), axis=0)
     bias_one_grad = jnp.sum(partial, axis=0)
-    one_flow = Flow(seq_sum(partial, rank))
     extra = pack_grads(
         {
             "gain1": gain_one_grad,
@@ -885,29 +916,42 @@
         position_part,
         rel_rows,
     ).astype(LOW)
-    qkv_low = weight_product(normed, qkv_out).astype(LOW).reshape(DEVICES, -1, ROOM)
-    qkv_flow = Flow(
-        win_sum(
-            jnp.concatenate([qkv_low, extra], axis=1).reshape(WINDOWS, -1, ROOM), window
-        )
-    )
-    advance((), one_flow, in_flow, out_flow, tail_flow)
-    in_back = Flow(seq_swap(in_flow.result.astype(LOW).reshape(RANKS, -1, ff), rank))
-    advance((), one_flow, qkv_flow)
+    qkv_kept, qkv_sent = split_product(normed, qkv_out, WIN, D // WINDOWS)
+    y = window % 2
+    extra = extra.reshape(WINDOWS // 2, 2, RANKS, EXTRA, ROOM)
+
+    def with_extra(grads, index):
+        grads = grads.reshape(WINDOWS // 2, RANKS, -1, ROOM)
+        short = lax.dynamic_index_in_dim(extra, index, 1, keepdims=False)
+        return jnp.concatenate([grads, short], axis=2).reshape(WINDOWS // 2, -1, ROOM)
+
+    qkv_kept, qkv_sent = advance(
+        (with_extra(qkv_kept, y), with_extra(qkv_sent, 1 - y)),
+        in_flow,
+        hid_flow,
+        point_flow,
+        up_flow,
+    )
+    qkv_flow = Flow(win_sum(qkv_kept, qkv_sent, window))
+    one_flow = Flow(seq_sum(partial, rank))
+    advance((), one_flow, in_flow, head_flow, rest_flow)
+    in_back = in_flow.result.astype(LOW).reshape(RANKS, -1, ff)
+    in_back = advance(in_back, one_flow, qkv_flow, point_flow, up_flow)
+    in_back = Flow(seq_swap_two(in_back, rank))
     grad_normed = one_flow.result
     _, pull_one = jax.vjp(lambda rows: layer_norm(rows, gain_one, bias_one), inputs_f)
     (grad_norm_in,) = pull_one(grad_normed)
     grad_inputs = (grad_one.astype(F32) + grad_norm_in).reshape(1, ROWS, D)
-    advance((), out_flow, in_back)
-    advance((), qkv_flow, out_flow)
+    advance((), qkv_flow, head_flow, in_back, rest_flow)
+    advance((), qkv_flow, in_back, rest_flow)
     qkv_flow = Flow(seq_swap(qkv_flow.result.astype(LOW).reshape(RANKS, -1, ROOM), rank))
-    advance((), qkv_flow)
+    advance((), qkv_flow, rest_flow)
     wq_grad, wk_grad, wv_grad, shorts, rel_grad = finish(qkv_flow.result, hq, hv)
     sums = {name: shorts[0, low:high] for name, (low, high) in SHORT.items()}
     in_grad = undeal(in_back.result, WINDOWS)
-    point_grad, skip_weight_grad, up_grad = tail_flow.result
-    (out_grad,) = out_flow.result
-    head_grad = head_flow.result[0][:, :TRACKS]
+    (point_grad,), (up_grad,) = point_flow.result, up_flow.result
+    skip_weight_grad, out_grad = rest_flow.result
+    (head_grad,) = head_flow.result
     hid_grad = hid_flow.result
     loss_total, head_bias_grad = shared_flow.result[-1], shared_flow.result[:-1]
     loss_mean = loss_total / (WINDOWS * 2 * seq_len * TRACKS)

time: 802 us -> 727 us (0.906)
  waiting for transfers between devices: 371 us -> 283 us
  matrix products: 109 us -> 75.7 us
  local copies, waits for them, and re-layouts: 51.4 us -> 80.8 us
  Pallas kernels: 54 us -> 82.2 us
  starting transfers between devices: 99 us -> 83 us
    ppermute x91 -> x79, waiting for transfers between devices: 371 us -> 276 us  [trade(): return lax.ppermute(block, axis, [(i, i ^ bits) for i in range(count)])]
    pallas_call x0 -> x8, Pallas kernels: none -> 31.5 us  [split_product(): pl.pallas_call(functools.partial(split_kernel, axis, height), grid=(rows...]
    dot_general x14 -> x1, matrix products: 31.2 us -> 0.7 us  [weight_product(): lax.dot_general(first_arg, second_arg, (((0,), (0,)), ((), ())), preferre...]
    convert_element_type x12 -> x24, other arithmetic: 9.86 us -> 27.8 us  [the longest x23 26.7 us: plus(): return total.astype(LOW)]
    unnamed x225 -> x309, local copies, waits for them, and re-layouts: 16.8 us -> 32.6 us
    ppermute x91 -> x79, starting transfers between devices: 89.7 us -> 74.3 us  [trade(): return lax.ppermute(block, axis, [(i, i ^ bits) for i in range(count)])]
    dynamic_slice x0 -> x19, local copies, waits for them, and re-layouts: none -> 11.2 us  [the longest x12 10.2 us: half(): lax.dynamic_index_in_dim(g, index, axis, keepdims=False)]
  transfers between devices with their start and end apart: 98 -> 85, of which waited for: 38 -> 38; matrix products, arithmetic and copies ran while one was open for 23% -> 25% of each run, Pallas kernels for 7% -> 10%
where the time goes in v2:
time: 727 us; the launch traced here: 716 us
  waiting for transfers between devices  283 us (39%)
  starting transfers between devices  83 us (11%)
  Pallas kernels  82.2 us (11%)
  local copies, waits for them, and re-layouts  80.8 us (11%)
  other arithmetic  79.9 us (11%)
  matrix products  75.7 us (10%)
  between operations  20.7 us (3%)
  blocking collectives  11.4 us (2%)
    ppermute x79, waiting for transfers between devices, trade(): return lax.ppermute(block, axis, [(i, i ^ bits) for i in range(count)])  276 us
    ppermute x79, starting transfers between devices, trade(): return lax.ppermute(block, axis, [(i, i ^ bits) for i in range(count)])  74.3 us
    dot_general x8, matrix products, product(): return jnp.dot(first_arg, second_arg, preferred_element_type=jnp.float32)  40.7 us
    unnamed x309, local copies, waits for them, and re-layouts  32.6 us
    pallas_call x8, Pallas kernels, split_product(): pl.pallas_call(functools.partial(split_kernel, axis, height), grid=(rows...  31.5 us
    dot_general x8, matrix products, input_product(): lax.dot_general(first_arg, second_arg, (((1,), (1,)), ((), ())), preferre...  31 us
    convert_element_type x23, other arithmetic, plus(): return total.astype(LOW)  26.7 us
    pallas_call x1, Pallas kernels, mix_grad(): pl.pallas_call(functools.partial(mix_grad_kernel, heads), grid=(rows // R...  17.4 us
  transfers between devices with their start and end apart: 85, of which 38 were waited for; matrix products, arithmetic and copies ran while one was open for 25% of the time, Pallas kernels for 10%

profile of v2, /device:TPU:0, one launch (start us, length us, event | category | flops | bytes accessed | tf_op | source)
XLA Modules:
  0.0 716.5 jit_solution(8019323171800193450)
XLA Ops:
  31.7 11.3 %collective-permute-done.5.refs_3_ = bf16[224,640]{1,0:T(8,128)(2,1)S(1)} collective-permute-done((bf16[224,640]{1,0:T(8,128)(2,1)S(1)}, bf16[224,640]{1,0:T(8,128)(2,1)S(1)}, u32[]{:S(2)}, u32[]{:S(2)}) %collective-permute-start.5) | collective-permute-done | bytes 286752 | tf_op jit(solution)/shard_map/ppermute | solution.py:254
  43.7 20.1 %collective-permute-done.4.refs_2_ = bf16[224,640]{1,0:T(8,128)(2,1)} collective-permute-done((bf16[224,640]{1,0:T(8,128)(2,1)S(1)}, bf16[224,640]{1,0:T(8,128)(2,1)}, u32[]{:S(2)}, u32[]{:S(2)}) %collective-permute-start.4) | collective-permute-done | bytes 286752 | tf_op jit(solution)/shard_map/ppermute | solution.py:254
  83.1 12.9 %collective-permute-done.8.refs_1_ = bf16[4,224,640]{2,1,0:T(8,128)(2,1)S(1)} collective-permute-done((bf16[4,224,640]{2,1,0:T(8,128)(2,1)S(1)}, bf16[4,224,640]{2,1,0:T(8,128)(2,1)S(1)}, u32[]{:S(2)}, u32[]{:S(2)}) %collective-permute-start.8) | collective-permute-done | bytes 1146912 | tf_op jit(solution)/shard_map/ppermute | solution.py:254
  102.5 11.7 %collective-permute-done.14.refs_2_ = bf16[96,1536]{1,0:T(8,128)(2,1)} collective-permute-done((bf16[96,1536]{1,0:T(8,128)(2,1)S(1)}, bf16[96,1536]{1,0:T(8,128)(2,1)}, u32[]{:S(2)}, u32[]{:S(2)}) %collective-permute-start.14) | collective-permute-done | bytes 294944 | tf_op jit(solution)/shard_map/ppermute | solution.py:254
  128.8 11.1 %shard_map.465 = (bf16[1024,384]{1,0:T(8,128)(2,1)S(1)}, f32[1024,2]{1,0:T(8,128)S(1)}) custom-call(bf16[1024,128]{1,0:T(8,128)(2,1)S(1)} %add_convert_fusion.19.q_ref, bf16[1024,128]{1,0:T(8,128)(2,1)S(1)} %slice.374.k_ref, bf16[1024,384]{1,0:T(8,128)(2,1)S(1)} %slice.375.v_ref, bf16[1024,64]{1,0:T(8,128)(2,1)S(1)} %convolution_convert_fusion.7.pos_ref, ...), custom_call_target="tpu_custom_call" | custom-call | flops 10000000000 | bytes 4194304 | tf_op jit(solution)/shard_map/pallas_call | solution.py:204
  139.9 28.4 %collective-permute-done.17.refs_2_ = bf16[192,768]{1,0:T(8,128)(2,1)S(1)} collective-permute-done((bf16[192,768]{1,0:T(8,128)(2,1)S(1)}, bf16[192,768]{1,0:T(8,128)(2,1)S(1)}, u32[]{:S(2)}, u32[]{:S(2)}) %collective-permute-start.17) | collective-permute-done | bytes 294944 | tf_op jit(solution)/shard_map/ppermute | solution.py:254
  185.2 6.1 all-gather.6.cloned.1.call-done
  203.1 15.5 %collective-permute-done.24.refs_2_ = bf16[256,1536]{1,0:T(8,128)(2,1)} collective-permute-done((bf16[256,1536]{1,0:T(8,128)(2,1)S(1)}, bf16[256,1536]{1,0:T(8,128)(2,1)}, u32[]{:S(2)}, u32[]{:S(2)}) %collective-permute-start.24) | collective-permute-done | bytes 786464 | tf_op jit(solution)/shard_map/ppermute | solution.py:254
  236.2 6.4 copy.69
  246.0 8.0 %fusion.90 = (bf16[32,48,1536]{2,1,0:T(8,128)(2,1)}, bf16[32,48,1536]{2,1,0:T(8,128)(2,1)}) fusion(bf16[32,184,1536]{2,1,0:T(8,128)(2,1)} %bitcast.356), kind=kLoop, calls=%fused_computation.333 | loop fusion | bytes 18874368 | tf_op jit(solution)/shard_map/slice | solution.py:761
  260.5 17.8 %collective-permute-done.28 = bf16[256,1536]{1,0:T(8,128)(2,1)S(1)} collective-permute-done((bf16[256,1536]{1,0:T(8,128)(2,1)S(1)}, bf16[256,1536]{1,0:T(8,128)(2,1)S(1)}, u32[]{:S(2)}, u32[]{:S(2)}) %collective-permute-start.28) | collective-permute-done | bytes 786464 | tf_op jit(solution)/shard_map/ppermute | solution.py:254
  280.4 8.5 %fusion.101 = (bf16[512,1536]{1,0:T(8,128)(2,1)S(1)}, f32[512,1536]{1,0:T(8,128)}) fusion(f32[512,1536]{1,0:T(8,128)} %convolution_add_fusion, bf16[1536,1536]{1,0:T(8,128)(2,1)} %bitcast.375, bf16[256,1536]{1,0:T(8,128)(2,1)S(1)} %fusion.44.first_ref, s32[512]{0:T(512)S(1)} %add_select_fusion), kind=kOutput, calls=%fused_computation.344 | convolution fusion | flops 2821062656 | bytes 13371392 | tf_op jit(solution)/shard_map/dot_general | solution.py:67
  303.8 14.4 %fusion.30 = (f32[2608]{0:T(1024)S(1)}, f32[]{:T(128)}, f32[512,2608]{1,0:T(8,128)}) fusion(f32[2608]{0:T(1024)S(1)} %convert_element_type.582, s32[1,512,2608]{2,1,0:T(8,128)} %copy.69, bf16[512,1536]{1,0:T(8,128)(2,1)S(1)} %add_convert_fusion.6.first_ref, bf16[1536,2608]{1,0:T(8,128)(2,1)} %all-gather.4.cloned.1.call-done), kind=kOutput, calls=%fused_computation.67 | convolution fusion | flops 4116715008 | bytes 20287876 | tf_op jit(solution)/shard_map/dot_general | solution.py:67
  318.2 11.4 %all-reduce = (f32[2608]{0:T(1024)S(1)}, f32[2608]{0:T(1024)S(1)}) all-reduce(f32[2608]{0:T(1024)S(1)} %get-tuple-element.513, f32[2608]{0:T(1024)S(1)} %convert_reduce_fusion.2), channel_id=1, replica_groups=mesh['win'=8,'seq'=4] {'seq'}, use_global_device_ids=true, to_apply=%region_7.8 | all-reduce | flops 5216 | bytes 41728 | tf_op jit(solution)/shard_map/psum | solution.py:787
  330.2 8.5 %convert_reduce_fusion.1 = (f32[2608]{0:T(1024)}, bf16[512,2608]{1,0:T(8,128)(2,1)S(1)}) fusion(f32[2608]{0:T(1024)S(1)} %get-tuple-element.634, f32[512,2608]{1,0:T(8,128)} %get-tuple-element.666, f32[2608]{0:T(1024)} %copy-done.113, s32[1,512,2608]{2,1,0:T(8,128)} %copy.69), kind=kLoop, calls=%fused_computation.18 | loop fusion | flops 24032720 | bytes 13384256 | tf_op jit(solution)/shard_map/reduce_sum | solution.py:799
  338.7 7.4 %shard_map.472 = (bf16[16,48,2608]{2,1,0:T(8,128)(2,1)S(1)}, bf16[16,48,2608]{2,1,0:T(8,128)(2,1)}) custom-call(bf16[512,1536]{1,0:T(8,128)(2,1)S(1)} %copy-done.20, bf16[512,2608]{1,0:T(8,128)(2,1)S(1)} %get-tuple-element.543.second_ref), custom_call_target="tpu_custom_call" | custom-call | flops 4102029312 | bytes 12255232 | tf_op jit(solution)/shard_map/pallas_call | solution.py:580
  353.4 8.1 %convolution_convert_fusion.2.second_ref = bf16[512,1536]{1,0:T(8,128)(2,1)S(1)} fusion(bf16[512,2608]{1,0:T(8,128)(2,1)S(1)} %get-tuple-element.543.second_ref, bf16[1536,2608]{1,0:T(8,128)(2,1)} %all-gather.4.cloned.1.call-done), kind=kOutput, calls=%fused_computation.62 | convolution fusion | flops 4102815744 | bytes 12255232 | tf_op jit(solution)/shard_map/dot_general | solution.py:77
  392.3 8.3 %collective-permute-done.37.refs_2_ = bf16[256,1536]{1,0:T(8,128)(2,1)S(1)} collective-permute-done((bf16[256,1536]{1,0:T(8,128)(2,1)S(1)}, bf16[256,1536]{1,0:T(8,128)(2,1)S(1)}, u32[]{:S(2)}, u32[]{:S(2)}) %collective-permute-start.37) | collective-permute-done | bytes 786464 | tf_op jit(solution)/shard_map/ppermute | solution.py:254
  404.2 5.3 add_convert_fusion
  456.7 4.9 collective-permute-done.48
  461.5 10.0 %collective-permute-done.49 = bf16[4,2,48,1536]{3,2,0,1:T(8,128)(2,1)S(1)} collective-permute-done((bf16[4,2,48,1536]{3,2,0,1:T(8,128)(2,1)S(1)}, bf16[4,2,48,1536]{3,2,0,1:T(8,128)(2,1)S(1)}, u32[]{:S(2)}, u32[]{:S(2)}) %collective-permute-start.49) | collective-permute-done | bytes 1179680 | tf_op jit(solution)/shard_map/ppermute | solution.py:254
  474.1 13.6 %collective-permute-done.47 = bf16[256,1536]{1,0:T(8,128)(2,1)S(1)} collective-permute-done((bf16[256,1536]{1,0:T(8,128)(2,1)S(1)}, bf16[256,1536]{1,0:T(8,128)(2,1)S(1)}, u32[]{:S(2)}, u32[]{:S(2)}) %collective-permute-start.47) | collective-permute-done | bytes 786464 | tf_op jit(solution)/shard_map/ppermute | solution.py:254
  512.3 17.4 %shard_map.480 = (bf16[1024,128]{1,0:T(8,128)(2,1)S(1)}, bf16[1024,64]{1,0:T(8,128)(2,1)S(1)}, bf16[1024,128]{1,0:T(8,128)(2,1)S(1)}, bf16[1024,384]{1,0:T(8,128)(2,1)S(1)}) custom-call(bf16[1024,128]{1,0:T(8,128)(2,1)S(1)} %copy-done.50, bf16[1024,128]{1,0:T(8,128)(2,1)S(1)} %copy-done.46, bf16[1024,384]{1,0:T(8,128)(2,1)S(1)} %copy-done.36, ...), custom_call_target="tpu_custom_call" | custom-call | flops 15000000512 | bytes 6291456 | tf_op jit(solution)/shard_map/pallas_call | solution.py:230
  531.9 5.0 collective-permute-done.55
  590.9 9.3 %collective-permute-done.66 = bf16[2,48,2608]{2,1,0:T(8,128)(2,1)S(1)} collective-permute-done((bf16[2,48,2608]{2,1,0:T(8,128)(2,1)S(1)}, bf16[2,48,2608]{2,1,0:T(8,128)(2,1)S(1)}, u32[]{:S(2)}, u32[]{:S(2)}) %collective-permute-start.66) | collective-permute-done | bytes 500768 | tf_op jit(solution)/shard_map/ppermute | solution.py:254
  601.2 9.3 %collective-permute-done.65 = bf16[192,768]{1,0:T(8,128)(2,1)S(1)} collective-permute-done((bf16[192,768]{1,0:T(8,128)(2,1)S(1)}, bf16[192,768]{1,0:T(8,128)(2,1)S(1)}, u32[]{:S(2)}, u32[]{:S(2)}) %collective-permute-start.65) | collective-permute-done | bytes 294944 | tf_op jit(solution)/shard_map/ppermute | solution.py:254
  611.9 13.5 %collective-permute-done.67 = bf16[4,2,88,1536]{3,2,0,1:T(8,128)(2,1)S(1)} collective-permute-done((bf16[4,2,88,1536]{3,2,0,1:T(8,128)(2,1)S(1)}, bf16[4,2,88,1536]{3,2,0,1:T(8,128)(2,1)S(1)}, u32[]{:S(2)}, u32[]{:S(2)}) %collective-permute-start.67) | collective-permute-done | bytes 2162720 | tf_op jit(solution)/shard_map/ppermute | solution.py:254
  630.2 8.6 %collective-permute-done.69 = bf16[4,224,640]{2,1,0:T(8,128)(2,1)S(1)} collective-permute-done((bf16[4,224,640]{2,1,0:T(8,128)(2,1)S(1)}, bf16[4,224,640]{2,1,0:T(8,128)(2,1)S(1)}, u32[]{:S(2)}, u32[]{:S(2)}) %collective-permute-start.69) | collective-permute-done | bytes 1146912 | tf_op jit(solution)/shard_map/ppermute | solution.py:254
  638.8 6.0 collective-permute-done.68
  666.4 12.2 %collective-permute-done.76 = bf16[224,640]{1,0:T(8,128)(2,1)S(1)} collective-permute-done((bf16[224,640]{1,0:T(8,128)(2,1)S(1)}, bf16[224,640]{1,0:T(8,128)(2,1)S(1)}, u32[]{:S(2)}, u32[]{:S(2)}) %collective-permute-start.76) | collective-permute-done | bytes 286752 | tf_op jit(solution)/shard_map/ppermute | solution.py:254
  678.6 6.1 collective-permute-done.78
  691.5 8.0 %collective-permute-done.82 = bf16[88,1536]{1,0:T(8,128)(2,1)S(1)} collective-permute-done((bf16[88,1536]{1,0:T(8,128)(2,1)S(1)}, bf16[88,1536]{1,0:T(8,128)(2,1)S(1)}, u32[]{:S(2)}, u32[]{:S(2)}) %collective-permute-start.82) | collective-permute-done | bytes 270368 | tf_op jit(solution)/shard_map/ppermute | solution.py:254
  (679 shorter events, 350.7 us)
Async XLA Ops:
  7.2 184.1 %all-gather.6.cloned.1.call-start = ((), (), s32[]{:S(2)}) async-start(), calls=%async_computation.1 | async-start | bytes 18653184 | tf_op jit(solution)/shard_map/all_gather | solution.py:704
  9.3 294.4 %all-gather.4.cloned.1.call-start = ((), (), s32[]{:S(2)}) async-start(), calls=%async_computation | async-start | bytes 8515584 | tf_op jit(solution)/shard_map/all_gather | solution.py:711
  23.4 40.4 %collective-permute-start.7 = (bf16[256,1536]{1,0:T(8,128)(2,1)S(1)}, bf16[256,1536]{1,0:T(8,128)(2,1)S(1)}, u32[]{:S(2)}, u32[]{:S(2)}) collective-permute-start(bf16[256,1536]{1,0:T(8,128)(2,1)S(1)} %bitcast.321), channel_id=1, source_target_pairs={{0,2},{1,3},{2,0},{3,1},{4,6},{5,7},{6,4},{7,5},{8,10},{9,11},{10,... | collective-permute-start | bytes 2359304 | tf_op jit(solution)/shard_map/ppermute | solution.py:254
  25.2 39.5 %collective-permute-start.6 = (bf16[256,1536]{1,0:T(8,128)(2,1)S(1)}, bf16[256,1536]{1,0:T(8,128)(2,1)S(1)}, u32[]{:S(2)}, u32[]{:S(2)}) collective-permute-start(bf16[256,1536]{1,0:T(8,128)(2,1)S(1)} %bitcast.322), channel_id=1, source_target_pairs={{0,1},{1,0},{2,3},{3,2},{4,5},{5,4},{6,7},{7,6},{8,9},{9,8},{10,11... | collective-permute-start | bytes 2359304 | tf_op jit(solution)/shard_map/ppermute | solution.py:254
  29.0 34.9 %collective-permute-start.4 = (bf16[224,640]{1,0:T(8,128)(2,1)S(1)}, bf16[224,640]{1,0:T(8,128)(2,1)}, u32[]{:S(2)}, u32[]{:S(2)}) collective-permute-start(bf16[224,640]{1,0:T(8,128)(2,1)S(1)} %bitcast.345), channel_id=1, source_target_pairs={{0,16},{4,20},{8,24},{12,28},{16,0},{20,4},{24,8},{28,12},{1,17},{... | collective-permute-start | bytes 860168 | tf_op jit(solution)/shard_map/ppermute | solution.py:254
  29.0 34.9 %collective-permute-start.3 = (bf16[224,640]{1,0:T(8,128)(2,1)S(1)}, bf16[224,640]{1,0:T(8,128)(2,1)}, u32[]{:S(2)}, u32[]{:S(2)}) collective-permute-start(bf16[224,640]{1,0:T(8,128)(2,1)S(1)} %bitcast.346), channel_id=1, source_target_pairs={{0,8},{4,12},{8,0},{12,4},{16,24},{20,28},{24,16},{28,20},{1,9},{5... | collective-permute-start | bytes 860168 | tf_op jit(solution)/shard_map/ppermute | solution.py:254
  67.8 28.2 %collective-permute-start.8 = (bf16[4,224,640]{2,1,0:T(8,128)(2,1)S(1)}, bf16[4,224,640]{2,1,0:T(8,128)(2,1)S(1)}, u32[]{:S(2)}, u32[]{:S(2)}) collective-permute-start(bf16[4,224,640]{2,1,0:T(8,128)(2,1)S(1)} %shard_map.460.refs_0_), channel_id=1, source_target_pairs={{0,4},{4,0},{8,12},{12,8},{16,20},{20,16},{24,28},{28,24},{1,5},{5... | collective-permute-start | bytes 3440648 | tf_op jit(solution)/shard_map/ppermute | solution.py:254
  80.6 33.6 %collective-permute-start.14 = (bf16[96,1536]{1,0:T(8,128)(2,1)S(1)}, bf16[96,1536]{1,0:T(8,128)(2,1)}, u32[]{:S(2)}, u32[]{:S(2)}) collective-permute-start(bf16[96,1536]{1,0:T(8,128)(2,1)S(1)} %copy-done.42), channel_id=1, source_target_pairs={{0,16},{4,20},{8,24},{12,28},{16,0},{20,4},{24,8},{28,12},{1,17},{... | collective-permute-start | bytes 884744 | tf_op jit(solution)/shard_map/ppermute | solution.py:254
  81.3 32.9 %collective-permute-start.13 = (bf16[96,1536]{1,0:T(8,128)(2,1)S(1)}, bf16[96,1536]{1,0:T(8,128)(2,1)}, u32[]{:S(2)}, u32[]{:S(2)}) collective-permute-start(bf16[96,1536]{1,0:T(8,128)(2,1)S(1)} %copy-done.42), channel_id=1, source_target_pairs={{0,8},{4,12},{8,0},{12,4},{16,24},{20,28},{24,16},{28,20},{1,9},{5... | collective-permute-start | bytes 884744 | tf_op jit(solution)/shard_map/ppermute | solution.py:254
  115.4 52.9 %collective-permute-start.17 = (bf16[192,768]{1,0:T(8,128)(2,1)S(1)}, bf16[192,768]{1,0:T(8,128)(2,1)S(1)}, u32[]{:S(2)}, u32[]{:S(2)}) collective-permute-start(bf16[192,768]{1,0:T(8,128)(2,1)S(1)} %bitcast.341), channel_id=1, source_target_pairs={{0,16},{4,20},{8,24},{12,28},{16,0},{20,4},{24,8},{28,12},{1,17},{... | collective-permute-start | bytes 884744 | tf_op jit(solution)/shard_map/ppermute | solution.py:254
  115.4 52.9 %collective-permute-start.16 = (bf16[192,768]{1,0:T(8,128)(2,1)S(1)}, bf16[192,768]{1,0:T(8,128)(2,1)S(1)}, u32[]{:S(2)}, u32[]{:S(2)}) collective-permute-start(bf16[192,768]{1,0:T(8,128)(2,1)S(1)} %bitcast.342), channel_id=1, source_target_pairs={{0,8},{4,12},{8,0},{12,4},{16,24},{20,28},{24,16},{28,20},{1,9},{5... | collective-permute-start | bytes 884744 | tf_op jit(solution)/shard_map/ppermute | solution.py:254
  126.7 46.0 %collective-permute-start.19 = (bf16[4,96,1536]{2,1,0:T(8,128)(2,1)S(1)}, bf16[4,96,1536]{2,1,0:T(8,128)(2,1)S(1)}, u32[]{:S(2)}, u32[]{:S(2)}) collective-permute-start(bf16[4,96,1536]{2,1,0:T(8,128)(2,1)S(1)} %shard_map.466.refs_0_), channel_id=1, source_target_pairs={{0,4},{4,0},{8,12},{12,8},{16,20},{20,16},{24,28},{28,24},{1,5},{5... | collective-permute-start | bytes 3538952 | tf_op jit(solution)/shard_map/ppermute | solution.py:254
  174.8 28.2 %collective-permute-start.25 = (bf16[4,192,768]{2,1,0:T(8,128)(2,1)S(1)}, bf16[4,192,768]{2,1,0:T(8,128)(2,1)}, u32[]{:S(2)}, u32[]{:S(2)}) collective-permute-start(bf16[4,192,768]{2,1,0:T(8,128)(2,1)S(1)} %shard_map.468.refs_0_), channel_id=1, source_target_pairs={{0,4},{4,0},{8,12},{12,8},{16,20},{20,16},{24,28},{28,24},{1,5},{5... | collective-permute-start | bytes 3538952 | tf_op jit(solution)/shard_map/ppermute | solution.py:254
  244.5 33.8 %collective-permute-start.28 = (bf16[256,1536]{1,0:T(8,128)(2,1)S(1)}, bf16[256,1536]{1,0:T(8,128)(2,1)S(1)}, u32[]{:S(2)}, u32[]{:S(2)}) collective-permute-start(bf16[256,1536]{1,0:T(8,128)(2,1)S(1)} %fusion.49), channel_id=1, source_target_pairs={{0,2},{1,3},{2,0},{3,1},{4,6},{5,7},{6,4},{7,5},{8,10},{9,11},{10,... | collective-permute-start | bytes 2359304 | tf_op jit(solution)/shard_map/ppermute | solution.py:254
  413.5 48.0 %collective-permute-start.48 = (bf16[4,2,48,2608]{3,2,0,1:T(8,128)(2,1)}, bf16[4,2,48,2608]{3,2,0,1:T(8,128)(2,1)}, u32[]{:S(2)}, u32[]{:S(2)}) collective-permute-start(bf16[4,2,48,2608]{3,2,0,1:T(8,128)(2,1)} %bitcast.309), channel_id=1, source_target_pairs={{0,4},{4,0},{8,12},{12,8},{16,20},{20,16},{24,28},{28,24},{1,5},{5... | collective-permute-start | bytes 6008840 | tf_op jit(solution)/shard_map/ppermute | solution.py:254
  416.9 30.0 %collective-permute-start.45 = (bf16[4,2,48,1536]{3,2,0,1:T(8,128)(2,1)}, bf16[4,2,48,1536]{3,2,0,1:T(8,128)(2,1)S(1)}, u32[]{:S(2)}, u32[]{:S(2)}) collective-permute-start(bf16[4,2,48,1536]{3,2,0,1:T(8,128)(2,1)} %bitcast.313), channel_id=1, source_target_pairs={{0,2},{1,3},{2,0},{3,1},{4,6},{5,7},{6,4},{7,5},{8,10},{9,11},{10,... | collective-permute-start | bytes 3538952 | tf_op jit(solution)/shard_map/ppermute | solution.py:254
  435.2 36.3 %collective-permute-start.49 = (bf16[4,2,48,1536]{3,2,0,1:T(8,128)(2,1)S(1)}, bf16[4,2,48,1536]{3,2,0,1:T(8,128)(2,1)S(1)}, u32[]{:S(2)}, u32[]{:S(2)}) collective-permute-start(bf16[4,2,48,1536]{3,2,0,1:T(8,128)(2,1)S(1)} %bitcast.393), channel_id=1, source_target_pairs={{0,2},{1,3},{2,0},{3,1},{4,6},{5,7},{6,4},{7,5},{8,10},{9,11},{10,... | collective-permute-start | bytes 3538952 | tf_op jit(solution)/shard_map/ppermute | solution.py:254
  448.6 39.1 %collective-permute-start.47 = (bf16[256,1536]{1,0:T(8,128)(2,1)S(1)}, bf16[256,1536]{1,0:T(8,128)(2,1)S(1)}, u32[]{:S(2)}, u32[]{:S(2)}) collective-permute-start(bf16[256,1536]{1,0:T(8,128)(2,1)S(1)} %fusion.50), channel_id=1, source_target_pairs={{0,2},{1,3},{2,0},{3,1},{4,6},{5,7},{6,4},{7,5},{8,10},{9,11},{10,... | collective-permute-start | bytes 2359304 | tf_op jit(solution)/shard_map/ppermute | solution.py:254
  455.5 51.2 %collective-permute-start.54 = (bf16[4,96,1536]{2,1,0:T(8,128)(2,1)S(1)}, bf16[4,96,1536]{2,1,0:T(8,128)(2,1)S(1)}, u32[]{:S(2)}, u32[]{:S(2)}) collective-permute-start(bf16[4,96,1536]{2,1,0:T(8,128)(2,1)S(1)} %get-tuple-element.379), channel_id=1, source_target_pairs={{0,4},{4,0},{8,12},{12,8},{16,20},{20,16},{24,28},{28,24},{1,5},{5... | collective-permute-start | bytes 3538952 | tf_op jit(solution)/shard_map/ppermute | solution.py:254
  495.9 35.0 %collective-permute-start.58 = (bf16[4,48,1536]{2,1,0:T(8,128)(2,1)S(1)}, bf16[4,48,1536]{2,1,0:T(8,128)(2,1)}, u32[]{:S(2)}, u32[]{:S(2)}) collective-permute-start(bf16[4,48,1536]{2,1,0:T(8,128)(2,1)S(1)} %dynamic-slice_bitcast_fusion.2), channel_id=1, source_target_pairs={{0,4},{4,0},{8,12},{12,8},{16,20},{20,16},{24,28},{28,24},{1,5},{5... | collective-permute-start | bytes 1769480 | tf_op jit(solution)/shard_map/ppermute | solution.py:254
  500.8 31.1 %collective-permute-start.59 = (bf16[4,48,2608]{2,1,0:T(8,128)(2,1)S(1)}, bf16[4,48,2608]{2,1,0:T(8,128)(2,1)S(1)}, u32[]{:S(2)}, u32[]{:S(2)}) collective-permute-start(bf16[4,48,2608]{2,1,0:T(8,128)(2,1)S(1)} %dynamic-slice_bitcast_fusion.1), channel_id=1, source_target_pairs={{0,2},{1,3},{2,0},{3,1},{4,6},{5,7},{6,4},{7,5},{8,10},{9,11},{10,... | collective-permute-start | bytes 3004424 | tf_op jit(solution)/shard_map/ppermute | solution.py:254
  505.1 31.7 %collective-permute-start.55 = (bf16[4,192,768]{2,1,0:T(8,128)(2,1)S(1)}, bf16[4,192,768]{2,1,0:T(8,128)(2,1)S(1)}, u32[]{:S(2)}, u32[]{:S(2)}) collective-permute-start(bf16[4,192,768]{2,1,0:T(8,128)(2,1)S(1)} %get-tuple-element.395), channel_id=1, source_target_pairs={{0,4},{4,0},{8,12},{12,8},{16,20},{20,16},{24,28},{28,24},{1,5},{5... | collective-permute-start | bytes 3538952 | tf_op jit(solution)/shard_map/ppermute | solution.py:254
  509.4 27.5 %collective-permute-start.57 = (bf16[16,48,1536]{2,1,0:T(8,128)(2,1)S(1)}, bf16[16,48,1536]{2,1,0:T(8,128)(2,1)S(1)}, u32[]{:S(2)}, u32[]{:S(2)}) collective-permute-start(bf16[16,48,1536]{2,1,0:T(8,128)(2,1)S(1)} %get-tuple-element.398), channel_id=1, source_target_pairs={{0,1},{1,0},{2,3},{3,2},{4,5},{5,4},{6,7},{7,6},{8,9},{9,8},{10,11... | collective-permute-start | bytes 7077896 | tf_op jit(solution)/shard_map/ppermute | solution.py:254
  530.9 49.9 %collective-permute-start.63 = (bf16[2,48,1536]{2,1,0:T(8,128)(2,1)}, bf16[2,48,1536]{2,1,0:T(8,128)(2,1)}, u32[]{:S(2)}, u32[]{:S(2)}) collective-permute-start(bf16[2,48,1536]{2,1,0:T(8,128)(2,1)} %pad_maximum_fusion.16), channel_id=1, source_target_pairs={{0,8},{4,12},{8,0},{12,4},{16,24},{20,28},{24,16},{28,20},{1,9},{5... | collective-permute-start | bytes 884744 | tf_op jit(solution)/shard_map/ppermute | solution.py:254
  553.6 28.9 %collective-permute-start.64 = (bf16[2,48,1536]{2,1,0:T(8,128)(2,1)}, bf16[2,48,1536]{2,1,0:T(8,128)(2,1)}, u32[]{:S(2)}, u32[]{:S(2)}) collective-permute-start(bf16[2,48,1536]{2,1,0:T(8,128)(2,1)} %pad_maximum_fusion.17), channel_id=1, source_target_pairs={{0,8},{4,12},{8,0},{12,4},{16,24},{20,28},{24,16},{28,20},{1,9},{5... | collective-permute-start | bytes 884744 | tf_op jit(solution)/shard_map/ppermute | solution.py:254
  577.1 48.3 %collective-permute-start.67 = (bf16[4,2,88,1536]{3,2,0,1:T(8,128)(2,1)S(1)}, bf16[4,2,88,1536]{3,2,0,1:T(8,128)(2,1)S(1)}, u32[]{:S(2)}, u32[]{:S(2)}) collective-permute-start(bf16[4,2,88,1536]{3,2,0,1:T(8,128)(2,1)S(1)} %pad_maximum_fusion), channel_id=1, source_target_pairs={{0,2},{1,3},{2,0},{3,1},{4,6},{5,7},{6,4},{7,5},{8,10},{9,11},{10,... | collective-permute-start | bytes 6488072 | tf_op jit(solution)/shard_map/ppermute | solution.py:254
  582.5 29.4 %collective-permute-start.60 = (bf16[2,256,1536]{2,1,0:T(8,128)(2,1)S(1)}, bf16[2,256,1536]{2,1,0:T(8,128)(2,1)S(1)}, u32[]{:S(2)}, u32[]{:S(2)}) collective-permute-start(bf16[2,256,1536]{2,1,0:T(8,128)(2,1)S(1)} %pad_maximum_fusion.5), channel_id=1, source_target_pairs={{0,1},{1,0},{2,3},{3,2},{4,5},{5,4},{6,7},{7,6},{8,9},{9,8},{10,11... | collective-permute-start | bytes 4718600 | tf_op jit(solution)/shard_map/ppermute | solution.py:254
  583.9 45.4 %collective-permute-start.71 = (bf16[48,1536]{1,0:T(8,128)(2,1)S(1)}, bf16[48,1536]{1,0:T(8,128)(2,1)S(1)}, u32[]{:S(2)}, u32[]{:S(2)}) collective-permute-start(bf16[48,1536]{1,0:T(8,128)(2,1)S(1)} %fusion.71), channel_id=1, source_target_pairs={{0,16},{4,20},{8,24},{12,28},{16,0},{20,4},{24,8},{28,12},{1,17},{... | collective-permute-start | bytes 442376 | tf_op jit(solution)/shard_map/ppermute | solution.py:254
  600.2 30.0 %collective-permute-start.70 = (bf16[48,1536]{1,0:T(8,128)(2,1)S(1)}, bf16[48,1536]{1,0:T(8,128)(2,1)S(1)}, u32[]{:S(2)}, u32[]{:S(2)}) collective-permute-start(bf16[48,1536]{1,0:T(8,128)(2,1)S(1)} %fusion.70), channel_id=1, source_target_pairs={{0,16},{4,20},{8,24},{12,28},{16,0},{20,4},{24,8},{28,12},{1,17},{... | collective-permute-start | bytes 442376 | tf_op jit(solution)/shard_map/ppermute | solution.py:254
  610.5 28.2 %collective-permute-start.69 = (bf16[4,224,640]{2,1,0:T(8,128)(2,1)S(1)}, bf16[4,224,640]{2,1,0:T(8,128)(2,1)S(1)}, u32[]{:S(2)}, u32[]{:S(2)}) collective-permute-start(bf16[4,224,640]{2,1,0:T(8,128)(2,1)S(1)} %bitcast.395), channel_id=1, source_target_pairs={{0,4},{4,0},{8,12},{12,8},{16,20},{20,16},{24,28},{28,24},{1,5},{5... | collective-permute-start | bytes 3440648 | tf_op jit(solution)/shard_map/ppermute | solution.py:254
  626.6 28.3 %collective-permute-start.73 = (bf16[48,2608]{1,0:T(8,128)(2,1)S(1)}, bf16[48,2608]{1,0:T(8,128)(2,1)S(1)}, u32[]{:S(2)}, u32[]{:S(2)}) collective-permute-start(bf16[48,2608]{1,0:T(8,128)(2,1)S(1)} %fusion.69), channel_id=1, source_target_pairs={{0,16},{4,20},{8,24},{12,28},{16,0},{20,4},{24,8},{28,12},{1,17},{... | collective-permute-start | bytes 751112 | tf_op jit(solution)/shard_map/ppermute | solution.py:254
  629.3 30.1 %collective-permute-start.75 = (bf16[4,88,1536]{2,1,0:T(8,128)(2,1)S(1)}, bf16[4,88,1536]{2,1,0:T(8,128)(2,1)S(1)}, u32[]{:S(2)}, u32[]{:S(2)}) collective-permute-start(bf16[4,88,1536]{2,1,0:T(8,128)(2,1)S(1)} %dynamic-slice_bitcast_fusion), channel_id=1, source_target_pairs={{0,4},{4,0},{8,12},{12,8},{16,20},{20,16},{24,28},{28,24},{1,5},{5... | collective-permute-start | bytes 3244040 | tf_op jit(solution)/shard_map/ppermute | solution.py:254
  (206 other events, 2532.4 us)
Sparse Core Ops, SparseCore 0:
  11.5 179.7 all-gather.5
  194.2 94.4 all-gather.3

commit v3 on v2

--- a/solution.py
+++ b/solution.py
@@ -331,10 +331,9 @@
 
 def seq_sum(partial, rank):
     blocks = partial.reshape(RANKS, ROWS, partial.shape[1])
-    sent = jnp.stack([pick(blocks, rank ^ 1), pick(blocks, rank ^ 3)]).astype(LOW)
-    got = yield trade(sent, SEQ, 1)
-    last = yield trade((pick(blocks, rank ^ 2) + got[1].astype(F32)).astype(LOW), SEQ, 2)
-    return pick(blocks, rank) + got[0].astype(F32) + last.astype(F32)
+    got = yield trade(jnp.stack([pick(blocks, rank ^ 1), pick(blocks, rank ^ 3)]), SEQ, 1)
+    last = yield trade(plus(pick(blocks, rank ^ 2), got[1]), SEQ, 2)
+    return pick(blocks, rank).astype(F32) + got[0].astype(F32) + last.astype(F32)
 
 
 def seq_swap(blocks, rank):
@@ -604,6 +603,18 @@
     for other in others:
         total = total + other.astype(F32)
     return total.astype(LOW)
+
+
+def z_chip_sum(grads, rank, window):
+    z, y = window // 2, window % 2
+    x = rank // 2
+    height, columns = grads.shape[3:]
+    total = yield from z_sum(grads.reshape(4, 4 * height, columns), z)
+    total = total.astype(LOW).reshape(2, 2, height, columns)
+    got = yield trade(pick(total, 1 - y), WIN, 1)
+    both = plus(pick(total, y), got)
+    got = yield trade(pick(both, 1 - x), SEQ, 2)
+    return pick(both, x).astype(F32) + got.astype(F32)
 
 
 def chip_sum(grads, rank, window, y_first):
@@ -766,7 +777,7 @@
     hid_part = hid_flow.result.reshape(ff, D)
     pre_act = product(normed_two, in_part) + in_bias
     hidden = smooth_act(pre_act).astype(LOW)
-    ff_flow = Flow(seq_sum(product(hidden, hid_part), rank))
+    ff_flow = Flow(seq_sum(product(hidden, hid_part).astype(LOW), rank))
     skip_rows = advance(skips.reshape(2 * ROWS, CS), ff_flow)
     from_skips = product(skip_rows, skip_full) + row_of["m"]
     from_skips = advance(from_skips, ff_flow)
@@ -804,7 +815,7 @@
     grad_out, grad_depth = advance((grad_out, grad_depth), head_core, shared_flow)
     depth_flow = Flow(edges(grad_depth, SEQ))
     grad_out, grad_depth = advance((grad_out, grad_depth), depth_flow, shared_flow)
-    head_flow = Flow(chip_sum([head_core.result], rank, window, True))
+    head_flow = Flow(z_chip_sum(head_core.result, rank, window))
     depth_pad = depth_flow.result
     merged_low = (
         grad_out.astype(F32)
@@ -837,23 +848,25 @@
     pbias_grad, mbias_grad, hbias_grad = advance(
         (pbias_grad, mbias_grad, hbias_grad), two_flow, skip_core, up_core, shared_flow
     )
-    up_flow = Flow(chip_sum([up_core.result], rank, window, False))
+    up_flow = Flow(chip_sum([up_core.result], rank, window, True))
     grad_two_all = two_flow.result
     grad_hidden = input_product(grad_two_all, hid_part).astype(LOW)
     _, pull_act = jax.vjp(smooth_act, pre_act)
     grad_pre = pull_act(grad_hidden.astype(F32))[0].astype(LOW)
-    pre_flow = Flow(seq_sum(input_product(grad_pre, in_part), rank))
+    pre_flow = Flow(seq_sum(input_product(grad_pre, in_part).astype(LOW), rank))
     hid_parts = split_product(hidden, grad_two_all, WIN, ff // WINDOWS)
     in_parts = split_product(normed_two, grad_pre, WIN, D // WINDOWS)
     hid_parts, in_parts, grad_pre, skips_kept = advance(
-        (hid_parts, in_parts, grad_pre, skip_core.result), pre_flow, point_flow, shared_flow
+        (hid_parts, in_parts, grad_pre, skip_core.result),
+        pre_flow,
+        point_flow,
+        shared_flow,
     )
     hid_flow = Flow(win_sum(*hid_parts, window))
     ibias_part = jnp.sum(grad_pre, axis=0, dtype=F32)
     ibias_part, in_parts = advance(
-        (ibias_part, in_parts), pre_flow, head_flow, up_flow, point_flow
-    )
-    in_flow = Flow(win_sum(*in_parts, window))
+        (ibias_part, in_parts), pre_flow, up_flow, point_flow, head_flow
+    )
     _, pull_two = jax.vjp(layer_norm, resid_one, gain_two, bias_two)
     grad_resid, gain_two_grad, bias_two_grad = pull_two(pre_flow.result)
     grad_one = (grad_two.astype(F32) + grad_resid).astype(LOW)
@@ -863,9 +876,12 @@
             jnp.stack([grad_att[:, t * hv : (t + 1) * hv] for t in range(RANKS)]), rank
         )
     )
-    grad_one, gain_two_grad, bias_two_grad, skips_kept = advance(
-        (grad_one, gain_two_grad, bias_two_grad, skips_kept), att_flow, hid_flow
-    )
+    grad_one, gain_two_grad, bias_two_grad, skips_kept, in_parts = advance(
+        (grad_one, gain_two_grad, bias_two_grad, skips_kept, in_parts),
+        att_flow,
+        hid_flow,
+    )
+    in_flow = Flow(win_sum(*in_parts, window))
     out_core = Flow(core_sum(attended, grad_one))
     grad_att = place(att_flow.result, SEQ).reshape(seq_len, hv)
     query_low, pos_low, key_grad, value_grad, skips_kept = advance(
@@ -874,10 +890,8 @@
             skips_kept,
         ),
         in_flow,
-        hid_flow,
         out_core,
         up_flow,
-        head_flow,
     )
     rest_flow = Flow(chip_sum([skips_kept, out_core.result], rank, window, False))
     pos_f = pos_low.astype(F32)
@@ -892,12 +906,12 @@
         jnp.where(same_head.T, rel_cross, 0.0).reshape(heads_here, BASIS, hq), axis=0
     )
     position_part = jnp.sum(pos_in_grad, axis=0)
-    partial = input_product(qkv_out, qkv_part)
+    partial = input_product(qkv_out, qkv_part).astype(LOW)
     centred = inputs_all.astype(F32)
     centred = centred - jnp.mean(centred, axis=-1, keepdims=True)
     scale = lax.rsqrt(jnp.mean(centred * centred, axis=-1, keepdims=True) + EPS)
     gain_one_grad = jnp.sum(partial * (centred * scale), axis=0)
-    bias_one_grad = jnp.sum(partial, axis=0)
+    bias_one_grad = jnp.sum(partial, axis=0, dtype=F32)
     extra = pack_grads(
         {
             "gain1": gain_one_grad,
@@ -930,28 +944,28 @@
         in_flow,
         hid_flow,
         point_flow,
-        up_flow,
+        head_flow,
     )
     qkv_flow = Flow(win_sum(qkv_kept, qkv_sent, window))
     one_flow = Flow(seq_sum(partial, rank))
-    advance((), one_flow, in_flow, head_flow, rest_flow)
+    advance((), one_flow, in_flow, hid_flow, qkv_flow)
     in_back = in_flow.result.astype(LOW).reshape(RANKS, -1, ff)
-    in_back = advance(in_back, one_flow, qkv_flow, point_flow, up_flow)
+    in_back = advance(in_back, one_flow, qkv_flow, up_flow, head_flow, rest_flow)
     in_back = Flow(seq_swap_two(in_back, rank))
     grad_normed = one_flow.result
     _, pull_one = jax.vjp(lambda rows: layer_norm(rows, gain_one, bias_one), inputs_f)
     (grad_norm_in,) = pull_one(grad_normed)
     grad_inputs = (grad_one.astype(F32) + grad_norm_in).reshape(1, ROWS, D)
-    advance((), qkv_flow, head_flow, in_back, rest_flow)
+    advance((), qkv_flow, in_back, rest_flow, head_flow, up_flow)
+    qkv_flow = Flow(seq_swap(qkv_flow.result.astype(LOW).reshape(RANKS, -1, ROOM), rank))
     advance((), qkv_flow, in_back, rest_flow)
-    qkv_flow = Flow(seq_swap(qkv_flow.result.astype(LOW).reshape(RANKS, -1, ROOM), rank))
-    advance((), qkv_flow, rest_flow)
+    advance((), rest_flow, point_flow)
     wq_grad, wk_grad, wv_grad, shorts, rel_grad = finish(qkv_flow.result, hq, hv)
     sums = {name: shorts[0, low:high] for name, (low, high) in SHORT.items()}
     in_grad = undeal(in_back.result, WINDOWS)
     (point_grad,), (up_grad,) = point_flow.result, up_flow.result
     skip_weight_grad, out_grad = rest_flow.result
-    (head_grad,) = head_flow.result
+    head_grad = head_flow.result
     hid_grad = hid_flow.result
     loss_total, head_bias_grad = shared_flow.result[-1], shared_flow.result[:-1]
     loss_mean = loss_total / (WINDOWS * 2 * seq_len * TRACKS)

time: 727 us -> 710 us (0.977)
    unnamed x309 -> x287, local copies, waits for them, and re-layouts: 32.6 us -> 35.7 us
    convert_element_type x23 -> x25, other arithmetic: 26.7 us -> 24 us  [plus(): return total.astype(LOW)]
  transfers between devices with their start and end apart: 85 -> 85, of which waited for: 38 -> 38; matrix products, arithmetic and copies ran while one was open for 25% -> 24% of each run, Pallas kernels for 10% -> 10%
where the time goes in v3:
time: 710 us; the launch traced here: 704 us
  waiting for transfers between devices  282 us (40%)
  starting transfers between devices  82.1 us (12%)
  Pallas kernels  81.8 us (12%)
  matrix products  76.3 us (11%)
  other arithmetic  75 us (11%)
  local copies, waits for them, and re-layouts  74.3 us (10%)
  between operations  20.5 us (3%)
  blocking collectives  11.6 us (2%)
    ppermute x79, waiting for transfers between devices, trade(): return lax.ppermute(block, axis, [(i, i ^ bits) for i in range(count)])  276 us
    ppermute x79, starting transfers between devices, trade(): return lax.ppermute(block, axis, [(i, i ^ bits) for i in range(count)])  73.1 us
    dot_general x8, matrix products, product(): return jnp.dot(first_arg, second_arg, preferred_element_type=jnp.float32)  41.3 us
    unnamed x287, local copies, waits for them, and re-layouts  35.7 us
    pallas_call x8, Pallas kernels, split_product(): pl.pallas_call(functools.partial(split_kernel, axis, height), grid=(rows...  31.4 us
    dot_general x8, matrix products, input_product(): lax.dot_general(first_arg, second_arg, (((1,), (1,)), ((), ())), preferre...  31 us
    convert_element_type x25, other arithmetic, plus(): return total.astype(LOW)  24 us
    pallas_call x1, Pallas kernels, mix_grad(): pl.pallas_call(functools.partial(mix_grad_kernel, heads), grid=(rows // R...  17.3 us
  transfers between devices with their start and end apart: 85, of which 38 were waited for; matrix products, arithmetic and copies ran while one was open for 24% of the time, Pallas kernels for 10%

profile of v3, /device:TPU:0, one launch (start us, length us, event | category | flops | bytes accessed | tf_op | source)
XLA Modules:
  0.0 703.7 jit_solution(5013340027411428939)
XLA Ops:
  31.7 11.3 %collective-permute-done.5.refs_3_ = bf16[224,640]{1,0:T(8,128)(2,1)S(1)} collective-permute-done((bf16[224,640]{1,0:T(8,128)(2,1)S(1)}, bf16[224,640]{1,0:T(8,128)(2,1)S(1)}, u32[]{:S(2)}, u32[]{:S(2)}) %collective-permute-start.5) | collective-permute-done | bytes 286752 | tf_op jit(solution)/shard_map/ppermute | solution.py:254
  43.7 20.1 %collective-permute-done.4.refs_2_ = bf16[224,640]{1,0:T(8,128)(2,1)} collective-permute-done((bf16[224,640]{1,0:T(8,128)(2,1)S(1)}, bf16[224,640]{1,0:T(8,128)(2,1)}, u32[]{:S(2)}, u32[]{:S(2)}) %collective-permute-start.4) | collective-permute-done | bytes 286752 | tf_op jit(solution)/shard_map/ppermute | solution.py:254
  83.2 12.9 %collective-permute-done.8.refs_1_ = bf16[4,224,640]{2,1,0:T(8,128)(2,1)S(1)} collective-permute-done((bf16[4,224,640]{2,1,0:T(8,128)(2,1)S(1)}, bf16[4,224,640]{2,1,0:T(8,128)(2,1)S(1)}, u32[]{:S(2)}, u32[]{:S(2)}) %collective-permute-start.8) | collective-permute-done | bytes 1146912 | tf_op jit(solution)/shard_map/ppermute | solution.py:254
  102.5 11.7 %collective-permute-done.14.refs_2_ = bf16[96,1536]{1,0:T(8,128)(2,1)} collective-permute-done((bf16[96,1536]{1,0:T(8,128)(2,1)S(1)}, bf16[96,1536]{1,0:T(8,128)(2,1)}, u32[]{:S(2)}, u32[]{:S(2)}) %collective-permute-start.14) | collective-permute-done | bytes 294944 | tf_op jit(solution)/shard_map/ppermute | solution.py:254
  128.9 10.9 %shard_map.465 = (bf16[1024,384]{1,0:T(8,128)(2,1)S(1)}, f32[1024,2]{1,0:T(8,128)S(1)}) custom-call(bf16[1024,128]{1,0:T(8,128)(2,1)S(1)} %add_convert_fusion.20.q_ref, bf16[1024,128]{1,0:T(8,128)(2,1)S(1)} %slice.374.k_ref, bf16[1024,384]{1,0:T(8,128)(2,1)S(1)} %slice.375.v_ref, bf16[1024,64]{1,0:T(8,128)(2,1)S(1)} %convolution_convert_fusion.10.pos_ref, ...), custom_call_target="tpu_custom_call" | custom-call | flops 10000000000 | bytes 4194304 | tf_op jit(solution)/shard_map/pallas_call | solution.py:204
  139.9 28.4 %collective-permute-done.17.refs_2_ = bf16[192,768]{1,0:T(8,128)(2,1)S(1)} collective-permute-done((bf16[192,768]{1,0:T(8,128)(2,1)S(1)}, bf16[192,768]{1,0:T(8,128)(2,1)S(1)}, u32[]{:S(2)}, u32[]{:S(2)}) %collective-permute-start.17) | collective-permute-done | bytes 294944 | tf_op jit(solution)/shard_map/ppermute | solution.py:254
  185.2 6.1 all-gather.6.cloned.1.call-done
  203.1 15.6 %collective-permute-done.24.refs_2_ = bf16[256,1536]{1,0:T(8,128)(2,1)} collective-permute-done((bf16[256,1536]{1,0:T(8,128)(2,1)S(1)}, bf16[256,1536]{1,0:T(8,128)(2,1)}, u32[]{:S(2)}, u32[]{:S(2)}) %collective-permute-start.24) | collective-permute-done | bytes 786464 | tf_op jit(solution)/shard_map/ppermute | solution.py:254
  236.4 6.1 copy.67
  245.4 8.0 %fusion.88 = (bf16[32,48,1536]{2,1,0:T(8,128)(2,1)}, bf16[32,48,1536]{2,1,0:T(8,128)(2,1)}) fusion(bf16[32,184,1536]{2,1,0:T(8,128)(2,1)} %bitcast.358), kind=kLoop, calls=%fused_computation.333 | loop fusion | bytes 18874368 | tf_op jit(solution)/shard_map/slice | solution.py:772
  259.9 18.2 %collective-permute-done.28 = bf16[256,1536]{1,0:T(8,128)(2,1)S(1)} collective-permute-done((bf16[256,1536]{1,0:T(8,128)(2,1)S(1)}, bf16[256,1536]{1,0:T(8,128)(2,1)S(1)}, u32[]{:S(2)}, u32[]{:S(2)}) %collective-permute-start.28) | collective-permute-done | bytes 786464 | tf_op jit(solution)/shard_map/ppermute | solution.py:254
  279.7 8.4 %fusion.99 = (bf16[512,1536]{1,0:T(8,128)(2,1)S(1)}, f32[512,1536]{1,0:T(8,128)}) fusion(f32[512,1536]{1,0:T(8,128)} %convolution_add_fusion, bf16[1536,1536]{1,0:T(8,128)(2,1)} %bitcast.381, bf16[256,1536]{1,0:T(8,128)(2,1)S(1)} %fusion.42.first_ref, s32[512]{0:T(512)S(1)} %add_select_fusion), kind=kOutput, calls=%fused_computation.344 | convolution fusion | flops 2821062656 | bytes 13371392 | tf_op jit(solution)/shard_map/dot_general | solution.py:67
  302.9 14.4 %fusion.28 = (f32[2608]{0:T(1024)S(1)}, f32[]{:T(128)}, f32[512,2608]{1,0:T(8,128)}) fusion(f32[2608]{0:T(1024)S(1)} %convert_element_type.619, s32[1,512,2608]{2,1,0:T(8,128)} %copy.67, bf16[512,1536]{1,0:T(8,128)(2,1)S(1)} %add_convert_fusion.6.first_ref, bf16[1536,2608]{1,0:T(8,128)(2,1)} %all-gather.4.cloned.1.call-done), kind=kOutput, calls=%fused_computation.69 | convolution fusion | flops 4116715008 | bytes 20287876 | tf_op jit(solution)/shard_map/dot_general | solution.py:67
  317.4 11.6 %all-reduce = (f32[2608]{0:T(1024)S(1)}, f32[2608]{0:T(1024)S(1)}) all-reduce(f32[2608]{0:T(1024)S(1)} %get-tuple-element.521, f32[2608]{0:T(1024)S(1)} %convert_reduce_fusion.3), channel_id=1, replica_groups=mesh['win'=8,'seq'=4] {'seq'}, use_global_device_ids=true, to_apply=%region_7.8 | all-reduce | flops 5216 | bytes 41728 | tf_op jit(solution)/shard_map/psum | solution.py:798
  329.5 8.5 %convert_reduce_fusion.2 = (f32[2608]{0:T(1024)}, bf16[512,2608]{1,0:T(8,128)(2,1)S(1)}) fusion(f32[2608]{0:T(1024)S(1)} %get-tuple-element.639, f32[512,2608]{1,0:T(8,128)} %get-tuple-element.671, f32[2608]{0:T(1024)} %copy-done.107, s32[1,512,2608]{2,1,0:T(8,128)} %copy.67), kind=kLoop, calls=%fused_computation.19 | loop fusion | flops 24032720 | bytes 13384256 | tf_op jit(solution)/shard_map/reduce_sum | solution.py:810
  338.0 7.4 %shard_map.472 = (bf16[16,48,2608]{2,1,0:T(8,128)(2,1)S(1)}, bf16[16,48,2608]{2,1,0:T(8,128)(2,1)}) custom-call(bf16[512,1536]{1,0:T(8,128)(2,1)S(1)} %copy-done.19, bf16[512,2608]{1,0:T(8,128)(2,1)S(1)} %get-tuple-element.550.second_ref), custom_call_target="tpu_custom_call" | custom-call | flops 4102029312 | bytes 12255232 | tf_op jit(solution)/shard_map/pallas_call | solution.py:579
  352.5 8.0 %convolution_convert_fusion.5.second_ref = bf16[512,1536]{1,0:T(8,128)(2,1)S(1)} fusion(bf16[512,2608]{1,0:T(8,128)(2,1)S(1)} %get-tuple-element.550.second_ref, bf16[1536,2608]{1,0:T(8,128)(2,1)} %all-gather.4.cloned.1.call-done), kind=kOutput, calls=%fused_computation.64 | convolution fusion | flops 4102815744 | bytes 12255232 | tf_op jit(solution)/shard_map/dot_general | solution.py:77
  360.5 5.1 convolution_convert_fusion.3
  395.8 7.0 %collective-permute-done.37.refs_2_ = bf16[256,1536]{1,0:T(8,128)(2,1)S(1)} collective-permute-done((bf16[256,1536]{1,0:T(8,128)(2,1)S(1)}, bf16[256,1536]{1,0:T(8,128)(2,1)S(1)}, u32[]{:S(2)}, u32[]{:S(2)}) %collective-permute-start.37) | collective-permute-done | bytes 786464 | tf_op jit(solution)/shard_map/ppermute | solution.py:254
  458.2 12.5 %collective-permute-done.49 = bf16[4,48,1536]{2,1,0:T(8,128)(2,1)S(1)} collective-permute-done((bf16[4,48,1536]{2,1,0:T(8,128)(2,1)S(1)}, bf16[4,48,1536]{2,1,0:T(8,128)(2,1)S(1)}, u32[]{:S(2)}, u32[]{:S(2)}) %collective-permute-start.49) | collective-permute-done | bytes 589856 | tf_op jit(solution)/shard_map/ppermute | solution.py:254
  490.0 5.6 collective-permute-done.54
  500.5 17.3 %shard_map.480 = (bf16[1024,128]{1,0:T(8,128)(2,1)S(1)}, bf16[1024,64]{1,0:T(8,128)(2,1)S(1)}, bf16[1024,128]{1,0:T(8,128)(2,1)S(1)}, bf16[1024,384]{1,0:T(8,128)(2,1)S(1)}) custom-call(bf16[1024,128]{1,0:T(8,128)(2,1)S(1)} %copy-done.49, bf16[1024,128]{1,0:T(8,128)(2,1)S(1)} %copy-done.45, bf16[1024,384]{1,0:T(8,128)(2,1)S(1)} %copy-done.37, ...), custom_call_target="tpu_custom_call" | custom-call | flops 15000000512 | bytes 6291456 | tf_op jit(solution)/shard_map/pallas_call | solution.py:230
  557.0 8.9 %collective-permute-done.59 = bf16[2,192,768]{2,1,0:T(8,128)(2,1)S(1)} collective-permute-done((bf16[2,192,768]{2,1,0:T(8,128)(2,1)S(1)}, bf16[2,192,768]{2,1,0:T(8,128)(2,1)S(1)}, u32[]{:S(2)}, u32[]{:S(2)}) %collective-permute-start.59) | collective-permute-done | bytes 589856 | tf_op jit(solution)/shard_map/ppermute | solution.py:254
  574.0 16.4 %collective-permute-done.64 = bf16[96,1536]{1,0:T(8,128)(2,1)S(1)} collective-permute-done((bf16[96,1536]{1,0:T(8,128)(2,1)S(1)}, bf16[96,1536]{1,0:T(8,128)(2,1)S(1)}, u32[]{:S(2)}, u32[]{:S(2)}) %collective-permute-start.64) | collective-permute-done | bytes 294944 | tf_op jit(solution)/shard_map/ppermute | solution.py:254
  591.6 5.2 collective-permute-done.63
  603.0 7.3 %collective-permute-done.69 = bf16[2,48,2608]{2,1,0:T(8,128)(2,1)S(1)} collective-permute-done((bf16[2,48,2608]{2,1,0:T(8,128)(2,1)S(1)}, bf16[2,48,2608]{2,1,0:T(8,128)(2,1)S(1)}, u32[]{:S(2)}, u32[]{:S(2)}) %collective-permute-start.69) | collective-permute-done | bytes 500768 | tf_op jit(solution)/shard_map/ppermute | solution.py:254
  615.2 5.5 collective-permute-done.66
  631.6 5.1 collective-permute-done.75
  636.7 5.2 collective-permute-done.71
  641.9 8.9 %collective-permute-done.73 = bf16[4,88,1536]{2,1,0:T(8,128)(2,1)S(1)} collective-permute-done((bf16[4,88,1536]{2,1,0:T(8,128)(2,1)S(1)}, bf16[4,88,1536]{2,1,0:T(8,128)(2,1)S(1)}, u32[]{:S(2)}, u32[]{:S(2)}) %collective-permute-start.73) | collective-permute-done | bytes 1081376 | tf_op jit(solution)/shard_map/ppermute | solution.py:254
  660.3 12.4 %collective-permute-done.80 = bf16[2,88,1536]{2,1,0:T(8,128)(2,1)S(1)} collective-permute-done((bf16[2,88,1536]{2,1,0:T(8,128)(2,1)S(1)}, bf16[2,88,1536]{2,1,0:T(8,128)(2,1)S(1)}, u32[]{:S(2)}, u32[]{:S(2)}) %collective-permute-start.80) | collective-permute-done | bytes 540704 | tf_op jit(solution)/shard_map/ppermute | solution.py:254
  684.8 7.4 %collective-permute-done.81 = bf16[88,1536]{1,0:T(8,128)(2,1)S(1)} collective-permute-done((bf16[88,1536]{1,0:T(8,128)(2,1)S(1)}, bf16[88,1536]{1,0:T(8,128)(2,1)S(1)}, u32[]{:S(2)}, u32[]{:S(2)}) %collective-permute-start.81) | collective-permute-done | bytes 270368 | tf_op jit(solution)/shard_map/ppermute | solution.py:254
  (654 shorter events, 345.9 us)
Async XLA Ops:
  7.2 184.1 %all-gather.6.cloned.1.call-start = ((), (), s32[]{:S(2)}) async-start(), calls=%async_computation.1 | async-start | bytes 18653184 | tf_op jit(solution)/shard_map/all_gather | solution.py:715
  9.3 293.6 %all-gather.4.cloned.1.call-start = ((), (), s32[]{:S(2)}) async-start(), calls=%async_computation | async-start | bytes 8515584 | tf_op jit(solution)/shard_map/all_gather | solution.py:722
  23.4 40.4 %collective-permute-start.7 = (bf16[256,1536]{1,0:T(8,128)(2,1)S(1)}, bf16[256,1536]{1,0:T(8,128)(2,1)S(1)}, u32[]{:S(2)}, u32[]{:S(2)}) collective-permute-start(bf16[256,1536]{1,0:T(8,128)(2,1)S(1)} %bitcast.325), channel_id=1, source_target_pairs={{0,2},{1,3},{2,0},{3,1},{4,6},{5,7},{6,4},{7,5},{8,10},{9,11},{10,... | collective-permute-start | bytes 2359304 | tf_op jit(solution)/shard_map/ppermute | solution.py:254
  25.2 39.5 %collective-permute-start.6 = (bf16[256,1536]{1,0:T(8,128)(2,1)S(1)}, bf16[256,1536]{1,0:T(8,128)(2,1)S(1)}, u32[]{:S(2)}, u32[]{:S(2)}) collective-permute-start(bf16[256,1536]{1,0:T(8,128)(2,1)S(1)} %bitcast.326), channel_id=1, source_target_pairs={{0,1},{1,0},{2,3},{3,2},{4,5},{5,4},{6,7},{7,6},{8,9},{9,8},{10,11... | collective-permute-start | bytes 2359304 | tf_op jit(solution)/shard_map/ppermute | solution.py:254
  29.0 34.9 %collective-permute-start.4 = (bf16[224,640]{1,0:T(8,128)(2,1)S(1)}, bf16[224,640]{1,0:T(8,128)(2,1)}, u32[]{:S(2)}, u32[]{:S(2)}) collective-permute-start(bf16[224,640]{1,0:T(8,128)(2,1)S(1)} %bitcast.348), channel_id=1, source_target_pairs={{0,16},{4,20},{8,24},{12,28},{16,0},{20,4},{24,8},{28,12},{1,17},{... | collective-permute-start | bytes 860168 | tf_op jit(solution)/shard_map/ppermute | solution.py:254
  29.0 34.9 %collective-permute-start.3 = (bf16[224,640]{1,0:T(8,128)(2,1)S(1)}, bf16[224,640]{1,0:T(8,128)(2,1)}, u32[]{:S(2)}, u32[]{:S(2)}) collective-permute-start(bf16[224,640]{1,0:T(8,128)(2,1)S(1)} %bitcast.349), channel_id=1, source_target_pairs={{0,8},{4,12},{8,0},{12,4},{16,24},{20,28},{24,16},{28,20},{1,9},{5... | collective-permute-start | bytes 860168 | tf_op jit(solution)/shard_map/ppermute | solution.py:254
  67.8 28.2 %collective-permute-start.8 = (bf16[4,224,640]{2,1,0:T(8,128)(2,1)S(1)}, bf16[4,224,640]{2,1,0:T(8,128)(2,1)S(1)}, u32[]{:S(2)}, u32[]{:S(2)}) collective-permute-start(bf16[4,224,640]{2,1,0:T(8,128)(2,1)S(1)} %shard_map.460.refs_0_), channel_id=1, source_target_pairs={{0,4},{4,0},{8,12},{12,8},{16,20},{20,16},{24,28},{28,24},{1,5},{5... | collective-permute-start | bytes 3440648 | tf_op jit(solution)/shard_map/ppermute | solution.py:254
  76.2 26.3 %collective-permute-start.15 = (bf16[96,1536]{1,0:T(8,128)(2,1)S(1)}, bf16[96,1536]{1,0:T(8,128)(2,1)}, u32[]{:S(2)}, u32[]{:S(2)}) collective-permute-start(bf16[96,1536]{1,0:T(8,128)(2,1)S(1)} %copy-done.41), channel_id=1, source_target_pairs={{0,24},{4,28},{8,16},{12,20},{16,8},{20,12},{24,0},{28,4},{1,25},{... | collective-permute-start | bytes 884744 | tf_op jit(solution)/shard_map/ppermute | solution.py:254
  80.6 33.6 %collective-permute-start.14 = (bf16[96,1536]{1,0:T(8,128)(2,1)S(1)}, bf16[96,1536]{1,0:T(8,128)(2,1)}, u32[]{:S(2)}, u32[]{:S(2)}) collective-permute-start(bf16[96,1536]{1,0:T(8,128)(2,1)S(1)} %copy-done.41), channel_id=1, source_target_pairs={{0,16},{4,20},{8,24},{12,28},{16,0},{20,4},{24,8},{28,12},{1,17},{... | collective-permute-start | bytes 884744 | tf_op jit(solution)/shard_map/ppermute | solution.py:254
  81.3 32.9 %collective-permute-start.13 = (bf16[96,1536]{1,0:T(8,128)(2,1)S(1)}, bf16[96,1536]{1,0:T(8,128)(2,1)}, u32[]{:S(2)}, u32[]{:S(2)}) collective-permute-start(bf16[96,1536]{1,0:T(8,128)(2,1)S(1)} %copy-done.41), channel_id=1, source_target_pairs={{0,8},{4,12},{8,0},{12,4},{16,24},{20,28},{24,16},{28,20},{1,9},{5... | collective-permute-start | bytes 884744 | tf_op jit(solution)/shard_map/ppermute | solution.py:254
  114.2 25.7 %collective-permute-start.18 = (bf16[192,768]{1,0:T(8,128)(2,1)S(1)}, bf16[192,768]{1,0:T(8,128)(2,1)S(1)}, u32[]{:S(2)}, u32[]{:S(2)}) collective-permute-start(bf16[192,768]{1,0:T(8,128)(2,1)S(1)} %bitcast.343), channel_id=1, source_target_pairs={{0,24},{4,28},{8,16},{12,20},{16,8},{20,12},{24,0},{28,4},{1,25},{... | collective-permute-start | bytes 884744 | tf_op jit(solution)/shard_map/ppermute | solution.py:254
  115.4 52.9 %collective-permute-start.17 = (bf16[192,768]{1,0:T(8,128)(2,1)S(1)}, bf16[192,768]{1,0:T(8,128)(2,1)S(1)}, u32[]{:S(2)}, u32[]{:S(2)}) collective-permute-start(bf16[192,768]{1,0:T(8,128)(2,1)S(1)} %bitcast.344), channel_id=1, source_target_pairs={{0,16},{4,20},{8,24},{12,28},{16,0},{20,4},{24,8},{28,12},{1,17},{... | collective-permute-start | bytes 884744 | tf_op jit(solution)/shard_map/ppermute | solution.py:254
  115.4 52.9 %collective-permute-start.16 = (bf16[192,768]{1,0:T(8,128)(2,1)S(1)}, bf16[192,768]{1,0:T(8,128)(2,1)S(1)}, u32[]{:S(2)}, u32[]{:S(2)}) collective-permute-start(bf16[192,768]{1,0:T(8,128)(2,1)S(1)} %bitcast.345), channel_id=1, source_target_pairs={{0,8},{4,12},{8,0},{12,4},{16,24},{20,28},{24,16},{28,20},{1,9},{5... | collective-permute-start | bytes 884744 | tf_op jit(solution)/shard_map/ppermute | solution.py:254
  126.9 45.8 %collective-permute-start.19 = (bf16[4,96,1536]{2,1,0:T(8,128)(2,1)S(1)}, bf16[4,96,1536]{2,1,0:T(8,128)(2,1)S(1)}, u32[]{:S(2)}, u32[]{:S(2)}) collective-permute-start(bf16[4,96,1536]{2,1,0:T(8,128)(2,1)S(1)} %shard_map.466.refs_0_), channel_id=1, source_target_pairs={{0,4},{4,0},{8,12},{12,8},{16,20},{20,16},{24,28},{28,24},{1,5},{5... | collective-permute-start | bytes 3538952 | tf_op jit(solution)/shard_map/ppermute | solution.py:254
  174.8 28.2 %collective-permute-start.25 = (bf16[4,192,768]{2,1,0:T(8,128)(2,1)S(1)}, bf16[4,192,768]{2,1,0:T(8,128)(2,1)}, u32[]{:S(2)}, u32[]{:S(2)}) collective-permute-start(bf16[4,192,768]{2,1,0:T(8,128)(2,1)S(1)} %shard_map.468.refs_0_), channel_id=1, source_target_pairs={{0,4},{4,0},{8,12},{12,8},{16,20},{20,16},{24,28},{28,24},{1,5},{5... | collective-permute-start | bytes 3538952 | tf_op jit(solution)/shard_map/ppermute | solution.py:254
  243.8 34.3 %collective-permute-start.28 = (bf16[256,1536]{1,0:T(8,128)(2,1)S(1)}, bf16[256,1536]{1,0:T(8,128)(2,1)S(1)}, u32[]{:S(2)}, u32[]{:S(2)}) collective-permute-start(bf16[256,1536]{1,0:T(8,128)(2,1)S(1)} %fusion.49), channel_id=1, source_target_pairs={{0,2},{1,3},{2,0},{3,1},{4,6},{5,7},{6,4},{7,5},{8,10},{9,11},{10,... | collective-permute-start | bytes 2359304 | tf_op jit(solution)/shard_map/ppermute | solution.py:254
  408.1 47.5 %collective-permute-start.50 = (bf16[2,192,2608]{2,1,0:T(8,128)(2,1)}, bf16[2,192,2608]{2,1,0:T(8,128)(2,1)S(1)}, u32[]{:S(2)}, u32[]{:S(2)}) collective-permute-start(bf16[2,192,2608]{2,1,0:T(8,128)(2,1)} %pad_maximum_fusion.1), channel_id=1, source_target_pairs={{0,8},{4,12},{8,0},{12,4},{16,24},{20,28},{24,16},{28,20},{1,9},{5... | collective-permute-start | bytes 6008840 | tf_op jit(solution)/shard_map/ppermute | solution.py:254
  414.4 28.5 %collective-permute-start.45 = (bf16[4,2,48,1536]{3,2,0,1:T(8,128)(2,1)}, bf16[4,2,48,1536]{3,2,0,1:T(8,128)(2,1)}, u32[]{:S(2)}, u32[]{:S(2)}) collective-permute-start(bf16[4,2,48,1536]{3,2,0,1:T(8,128)(2,1)} %bitcast.317), channel_id=1, source_target_pairs={{0,2},{1,3},{2,0},{3,1},{4,6},{5,7},{6,4},{7,5},{8,10},{9,11},{10,... | collective-permute-start | bytes 3538952 | tf_op jit(solution)/shard_map/ppermute | solution.py:254
  415.3 27.6 %collective-permute-start.46 = (f32[2609]{0:T(1024)S(1)}, f32[2609]{0:T(1024)S(1)}, u32[]{:S(2)}, u32[]{:S(2)}) collective-permute-start(f32[2609]{0:T(1024)S(1)} %add.601), channel_id=1, source_target_pairs={{0,2},{1,3},{2,0},{3,1},{4,6},{5,7},{6,4},{7,5},{8,10},{9,11},{10,... | collective-permute-start | bytes 31316 | tf_op jit(solution)/shard_map/ppermute | solution.py:254
  429.1 29.1 %collective-permute-start.48 = (bf16[4,2,48,1536]{3,2,0,1:T(8,128)(2,1)}, bf16[4,2,48,1536]{3,2,0,1:T(8,128)(2,1)}, u32[]{:S(2)}, u32[]{:S(2)}) collective-permute-start(bf16[4,2,48,1536]{3,2,0,1:T(8,128)(2,1)} %bitcast.316), channel_id=1, source_target_pairs={{0,4},{4,0},{8,12},{12,8},{16,20},{20,16},{24,28},{28,24},{1,5},{5... | collective-permute-start | bytes 3538952 | tf_op jit(solution)/shard_map/ppermute | solution.py:254
  443.1 27.6 %collective-permute-start.47 = (bf16[256,1536]{1,0:T(8,128)(2,1)S(1)}, bf16[256,1536]{1,0:T(8,128)(2,1)S(1)}, u32[]{:S(2)}, u32[]{:S(2)}) collective-permute-start(bf16[256,1536]{1,0:T(8,128)(2,1)S(1)} %fusion.50), channel_id=1, source_target_pairs={{0,2},{1,3},{2,0},{3,1},{4,6},{5,7},{6,4},{7,5},{8,10},{9,11},{10,... | collective-permute-start | bytes 2359304 | tf_op jit(solution)/shard_map/ppermute | solution.py:254
  445.8 25.0 %collective-permute-start.49 = (bf16[4,48,1536]{2,1,0:T(8,128)(2,1)S(1)}, bf16[4,48,1536]{2,1,0:T(8,128)(2,1)S(1)}, u32[]{:S(2)}, u32[]{:S(2)}) collective-permute-start(bf16[4,48,1536]{2,1,0:T(8,128)(2,1)S(1)} %dynamic-slice_bitcast_fusion.2), channel_id=1, source_target_pairs={{0,4},{4,0},{8,12},{12,8},{16,20},{20,16},{24,28},{28,24},{1,5},{5... | collective-permute-start | bytes 1769480 | tf_op jit(solution)/shard_map/ppermute | solution.py:254
  450.3 45.3 %collective-permute-start.54 = (bf16[4,96,1536]{2,1,0:T(8,128)(2,1)S(1)}, bf16[4,96,1536]{2,1,0:T(8,128)(2,1)S(1)}, u32[]{:S(2)}, u32[]{:S(2)}) collective-permute-start(bf16[4,96,1536]{2,1,0:T(8,128)(2,1)S(1)} %get-tuple-element.387), channel_id=1, source_target_pairs={{0,4},{4,0},{8,12},{12,8},{16,20},{20,16},{24,28},{28,24},{1,5},{5... | collective-permute-start | bytes 3538952 | tf_op jit(solution)/shard_map/ppermute | solution.py:254
  479.1 76.7 %collective-permute-start.61 = (bf16[2,48,1536]{2,1,0:T(8,128)(2,1)}, bf16[2,48,1536]{2,1,0:T(8,128)(2,1)}, u32[]{:S(2)}, u32[]{:S(2)}) collective-permute-start(bf16[2,48,1536]{2,1,0:T(8,128)(2,1)} %pad_maximum_fusion.16), channel_id=1, source_target_pairs={{0,8},{4,12},{8,0},{12,4},{16,24},{20,28},{24,16},{28,20},{1,9},{5... | collective-permute-start | bytes 884744 | tf_op jit(solution)/shard_map/ppermute | solution.py:254
  483.7 36.6 %collective-permute-start.57 = (bf16[4,48,1536]{2,1,0:T(8,128)(2,1)S(1)}, bf16[4,48,1536]{2,1,0:T(8,128)(2,1)S(1)}, u32[]{:S(2)}, u32[]{:S(2)}) collective-permute-start(bf16[4,48,1536]{2,1,0:T(8,128)(2,1)S(1)} %dynamic-slice_bitcast_fusion.1), channel_id=1, source_target_pairs={{0,2},{1,3},{2,0},{3,1},{4,6},{5,7},{6,4},{7,5},{8,10},{9,11},{10,... | collective-permute-start | bytes 1769480 | tf_op jit(solution)/shard_map/ppermute | solution.py:254
  487.3 69.7 %collective-permute-start.62 = (bf16[192,2608]{1,0:T(8,128)(2,1)}, bf16[192,2608]{1,0:T(8,128)(2,1)}, u32[]{:S(2)}, u32[]{:S(2)}) collective-permute-start(bf16[192,2608]{1,0:T(8,128)(2,1)} %fusion.47), channel_id=1, source_target_pairs={{0,16},{4,20},{8,24},{12,28},{16,0},{20,4},{24,8},{28,12},{1,17},{... | collective-permute-start | bytes 3004424 | tf_op jit(solution)/shard_map/ppermute | solution.py:254
  495.6 27.7 %collective-permute-start.55 = (bf16[4,192,768]{2,1,0:T(8,128)(2,1)S(1)}, bf16[4,192,768]{2,1,0:T(8,128)(2,1)S(1)}, u32[]{:S(2)}, u32[]{:S(2)}) collective-permute-start(bf16[4,192,768]{2,1,0:T(8,128)(2,1)S(1)} %get-tuple-element.403), channel_id=1, source_target_pairs={{0,4},{4,0},{8,12},{12,8},{16,20},{20,16},{24,28},{28,24},{1,5},{5... | collective-permute-start | bytes 3538952 | tf_op jit(solution)/shard_map/ppermute | solution.py:254
  520.3 36.7 %collective-permute-start.60 = (bf16[2,96,1536]{2,1,0:T(8,128)(2,1)}, bf16[2,96,1536]{2,1,0:T(8,128)(2,1)}, u32[]{:S(2)}, u32[]{:S(2)}) collective-permute-start(bf16[2,96,1536]{2,1,0:T(8,128)(2,1)} %pad_maximum_fusion.12), channel_id=1, source_target_pairs={{0,8},{4,12},{8,0},{12,4},{16,24},{20,28},{24,16},{28,20},{1,9},{5... | collective-permute-start | bytes 1769480 | tf_op jit(solution)/shard_map/ppermute | solution.py:254
  553.7 43.7 %collective-permute-start.58 = (bf16[2,256,1536]{2,1,0:T(8,128)(2,1)S(1)}, bf16[2,256,1536]{2,1,0:T(8,128)(2,1)S(1)}, u32[]{:S(2)}, u32[]{:S(2)}) collective-permute-start(bf16[2,256,1536]{2,1,0:T(8,128)(2,1)S(1)} %pad_maximum_fusion.6), channel_id=1, source_target_pairs={{0,1},{1,0},{2,3},{3,2},{4,5},{5,4},{6,7},{7,6},{8,9},{9,8},{10,11... | collective-permute-start | bytes 4718600 | tf_op jit(solution)/shard_map/ppermute | solution.py:254
  555.8 54.5 %collective-permute-start.70 = (bf16[4,2,88,1536]{3,2,0,1:T(8,128)(2,1)S(1)}, bf16[4,2,88,1536]{3,2,0,1:T(8,128)(2,1)S(1)}, u32[]{:S(2)}, u32[]{:S(2)}) collective-permute-start(bf16[4,2,88,1536]{3,2,0,1:T(8,128)(2,1)S(1)} %pad_maximum_fusion), channel_id=1, source_target_pairs={{0,2},{1,3},{2,0},{3,1},{4,6},{5,7},{6,4},{7,5},{8,10},{9,11},{10,... | collective-permute-start | bytes 6488072 | tf_op jit(solution)/shard_map/ppermute | solution.py:254
  567.9 29.5 %collective-permute-start.65 = (bf16[4,224,640]{2,1,0:T(8,128)(2,1)S(1)}, bf16[4,224,640]{2,1,0:T(8,128)(2,1)S(1)}, u32[]{:S(2)}, u32[]{:S(2)}) collective-permute-start(bf16[4,224,640]{2,1,0:T(8,128)(2,1)S(1)} %bitcast.403), channel_id=1, source_target_pairs={{0,4},{4,0},{8,12},{12,8},{16,20},{20,16},{24,28},{28,24},{1,5},{5... | collective-permute-start | bytes 3440648 | tf_op jit(solution)/shard_map/ppermute | solution.py:254
  657.6 27.2 %collective-permute-start.82 = (bf16[48,1536]{1,0:T(8,128)(2,1)S(1)}, bf16[48,1536]{1,0:T(8,128)(2,1)S(1)}, u32[]{:S(2)}, u32[]{:S(2)}) collective-permute-start(bf16[48,1536]{1,0:T(8,128)(2,1)S(1)} %fusion.70), channel_id=1, source_target_pairs={{0,16},{4,20},{8,24},{12,28},{16,0},{20,4},{24,8},{28,12},{1,17},{... | collective-permute-start | bytes 442376 | tf_op jit(solution)/shard_map/ppermute | solution.py:254
  (195 other events, 2325.4 us)
Sparse Core Ops, SparseCore 0:
  11.5 179.7 all-gather.5
  194.2 94.2 all-gather.3
